TPU v7x, 32 devices: a whole 2x2x4 slice. The times are simulated.
32 devices in a mesh: groups: 2 (over y), cells: 4 (over z), sub: 2 (over x), rep: 2 (over core).
Axes of the slice: x: 2, y: 2, z: 4, core: 2. Of those that a mesh axis runs over, the one named last changes fastest.
Arguments:
- queries: bfloat16 [128, 1024], P('groups', 'sub'), parts along dimension 0, may hold values from -6 to 6
- rerank_queries: bfloat16 [128, 1024], P(('groups', 'cells', 'rep'), 'sub'), parts along dimension 0, may hold values from -6 to 6
- coarse_book: bfloat16 [64, 256, 16], P('sub'), may hold values from -0.1875 to 0.1875
- refine_book: bfloat16 [16, 256, 64], P('sub'), may hold values from -0.1875 to 0.1875
- coarse_codes: int32 [64, 65536], P('sub', ('groups', 'cells')), parts along dimension 1, may hold values from 0 to 255
- refine_codes: int32 [16, 65536], P('sub', ('groups', 'cells')), parts along dimension 1, may hold values from 0 to 255
- block_place: int32 [512], P('groups'), parts along dimension 0, may hold values from 0 to 255, as said below
- candidates: int32 [128, 4], P(('groups', 'cells', 'rep')), parts along dimension 0, may hold values from 0 to 255, as said below
Outputs:
- coarse_scores: bfloat16 [128, 4, 8192], P(('groups', 'cells', 'rep'), None, 'sub'), parts along dimension 0
- refined: bfloat16 [128, 4, 128], P(('groups', 'cells', 'rep'), 'sub'), parts along dimension 0
There are 2 independent parts, one for each index of `groups`. A program takes and returns all parts, laid end to end along the dimension named above; an argument that names none is the same for every part. Nothing has to cross between parts.
Inputs may be any that keep to these rules, and one draw needn't show every extreme that they name: `block_place`: A permutation: every block id has one storage position. `candidates`: take the aligned blocks of 8 query rows (one query owner's rows). Of the 32 candidate blocks of such rows, at most 24 have block_place // 64 equal to any one value; in every draw some value is reached by exactly 24 from every such block of rows.
All inputs are finite; a program needn't handle non-finite values.
Results may differ from a plain program's by a relative error of at most 0.0049.
Values may be sent and summed in bfloat16 or wider, within the bound.
No kernel may reach another device: no remote copies, remote signals or barrier semaphores. Data moves between devices by JAX's collectives and lax.ppermute only.
A program may use at most 64 MiB of HBM per device.

v0:
```python
from functools import partial

import jax
import jax.numpy as jnp
from jax import lax
from jax.experimental import pallas as pl
from jax.experimental.pallas import tpu as pltpu
from jax.sharding import PartitionSpec as P


BLOCK = 128
LANES = 128

ALONG_LANES = lax.GatherDimensionNumbers(
    offset_dims=(),
    collapsed_slice_dims=(1,),
    start_index_map=(1,),
    operand_batching_dims=(0,),
    start_indices_batching_dims=(0,),
)


def take_lanes(table, index):
    return lax.gather(
        table,
        index[..., None],
        ALONG_LANES,
        (1, 1),
        mode=lax.GatherScatterMode.PROMISE_IN_BOUNDS,
    )


def lookup(table, codes):
    within = codes & (LANES - 1)
    found = take_lanes(table[:, :LANES], within)
    for start in range(LANES, table.shape[1], LANES):
        found = jnp.where(codes >= start, take_lanes(table[:, start : start + LANES], within), found)
    return found


def on_chip(value):
    return pltpu.with_memory_space_constraint(value, pltpu.VMEM)


def coarse_kernel(halves, q_ref, book_ref, codes_ref, *refs):
    out_refs, tiles_ref = refs[:halves], refs[halves]
    spaces, depth, _ = book_ref.shape
    holders, own, chunk = out_refs[0].shape
    half = lax.axis_index("rep")
    rows = jnp.concatenate(
        [
            q_ref[h * halves + (half ^ r)].astype(jnp.float32)
            for r in range(halves)
            for h in range(holders)
        ],
        axis=0,
    ).astype(jnp.bfloat16)

    def fill(group, _):
        lanes = pl.ds(pl.multiple_of(group * LANES, LANES), LANES)
        for m in range(spaces):
            table = book_ref[m].astype(jnp.float32)
            codes = jnp.broadcast_to(codes_ref[m : m + 1, lanes], (8, LANES))
            found = [lookup(table[d : d + 8], codes) for d in range(0, depth, 8)]
            tiles_ref[m * depth : (m + 1) * depth, lanes] = jnp.concatenate(found, axis=0).astype(
                jnp.bfloat16
            )
        return 0

    lax.fori_loop(0, chunk // LANES, fill, 0, unroll=2)
    scores = jnp.dot(rows, tiles_ref[...], preferred_element_type=jnp.float32)
    for r in range(halves):
        for h in range(holders):
            at = (r * holders + h) * own
            out_refs[r][h] = scores[at : at + own].astype(out_refs[r].dtype)


def coarse_part(shift, subs, halves, holders, own, queries, book, codes):
    spaces, stored = codes.shape
    quarter = stored // subs // halves

    def place(step):
        return 0, (lax.axis_index("sub") ^ shift) * halves + lax.axis_index("rep")

    whole = pl.BlockSpec(memory_space=pltpu.VMEM)
    kinds = [jnp.bfloat16] * halves
    if shift == 0:
        kinds[0] = jnp.float32
    return pl.pallas_call(
        partial(coarse_kernel, halves),
        grid=(1,),
        in_specs=[whole, whole, pl.BlockSpec((spaces, quarter), place)],
        out_specs=[whole] * halves,
        out_shape=[pltpu.VMEM((holders, own, quarter), kind) for kind in kinds],
        scratch_shapes=[pltpu.VMEM((book.shape[0] * book.shape[1], quarter), jnp.bfloat16)],
    )(queries, book, codes)


def refine_kernel(holders, place_ref, cand_ref, rerank_ref, book_ref, *refs):
    codes_refs = refs[:holders]
    out_ref, wide_ref, table_ref = refs[holders:]
    per_query, own = cand_ref.shape
    spaces, stored = codes_refs[0].shape
    width = book_ref.shape[0]
    depth = width // spaces
    cell_blocks = stored // BLOCK
    cell = lax.axis_index("cells")
    slot = -(-spaces // 8) * 8
    mine = lax.broadcasted_iota(jnp.int32, (slot, width), 1) // depth == (
        lax.broadcasted_iota(jnp.int32, (slot, width), 0)
    )
    rerank = rerank_ref[...].astype(jnp.float32)
    for j in range(own):
        wide_ref[j * slot : (j + 1) * slot, :] = jnp.where(mine, rerank[j : j + 1], 0.0)
    table_ref[...] = jnp.dot(
        wide_ref[...].astype(jnp.bfloat16), book_ref[...], preferred_element_type=jnp.float32
    )
    for j in range(own):
        table = table_ref[j * slot : j * slot + spaces, :]
        for c in range(per_query):
            position = place_ref[cand_ref[c, j]]
            source = position // cell_blocks ^ cell
            lanes = pl.ds(pl.multiple_of(position % cell_blocks * BLOCK, BLOCK), BLOCK)
            codes = codes_refs[0][:, lanes].astype(jnp.float32)
            for k in range(1, holders):
                codes = jnp.where(source == k, codes_refs[k][:, lanes].astype(jnp.float32), codes)
            found = lookup(table, codes.astype(jnp.int32))
            out_ref[j : j + 1, c * BLOCK : (c + 1) * BLOCK] = jnp.sum(found, axis=0, keepdims=True)


def refine_partials(place, cands, reranks, book, codes):
    per_query, own = cands.shape
    spaces = codes[0].shape[0]
    rows = own * (-(-spaces // 8) * 8)
    smem = pl.BlockSpec(memory_space=pltpu.SMEM)
    vmem = pl.BlockSpec(memory_space=pltpu.VMEM)
    return pl.pallas_call(
        partial(refine_kernel, len(codes)),
        in_specs=[smem, smem] + [vmem] * (2 + len(codes)),
        out_specs=vmem,
        out_shape=pltpu.VMEM((own, per_query * BLOCK), jnp.float32),
        scratch_shapes=[
            pltpu.VMEM((rows, book.shape[0]), jnp.float32),
            pltpu.VMEM((rows, book.shape[1]), jnp.float32),
        ],
        name="refine",
    )(place, cands, reranks, book, *[on_chip(c) for c in codes])


def combine_kernel(subs, halves, *refs):
    in_refs, out_refs = refs[: subs * halves], refs[subs * halves :]
    cell = lax.axis_index("cells")
    quarter = in_refs[0].shape[2]
    for k, out_ref in enumerate(out_refs):
        for r in range(halves):
            total = in_refs[r][cell ^ k].astype(jnp.float32)
            for shift in range(1, subs):
                total = total + in_refs[shift * halves + r][cell ^ k].astype(jnp.float32)
            at = pl.multiple_of((lax.axis_index("rep") ^ r) * quarter, quarter)
            out_ref[:, pl.ds(at, quarter)] = total.astype(jnp.bfloat16)


def combine(subs, halves, sums):
    holders, own, quarter = sums[0].shape
    vmem = pl.BlockSpec(memory_space=pltpu.VMEM)
    return pl.pallas_call(
        partial(combine_kernel, subs, halves),
        in_specs=[vmem] * len(sums),
        out_specs=[vmem] * holders,
        out_shape=[pltpu.VMEM((own, quarter * halves), jnp.bfloat16)] * holders,
        name="combine",
    )(*[on_chip(s) for s in sums])


def pick_kernel(subs, holders, place_ref, cand_ref, fine_ref, *refs):
    got_refs, out_refs = refs[:holders], refs[holders:]
    per_query, own = cand_ref.shape
    part_blocks = got_refs[0].shape[1] // BLOCK
    cell_blocks = part_blocks * subs
    cell = lax.axis_index("cells")
    sub = lax.axis_index("sub")
    row = lax.broadcasted_iota(jnp.int32, (own, BLOCK), 0)
    sums = []
    for c in range(per_query):
        total = jnp.zeros((own, BLOCK), jnp.float32)
        for j in range(own):
            position = place_ref[cand_ref[c, j]]
            block = position % cell_blocks
            source = position // cell_blocks ^ cell
            lanes = pl.ds(pl.multiple_of(block % part_blocks * BLOCK, BLOCK), BLOCK)
            score = got_refs[0][:, lanes].astype(jnp.float32)
            for k in range(1, holders):
                score = jnp.where(source == k, got_refs[k][:, lanes].astype(jnp.float32), score)
            total = jnp.where((row == j) & (block // part_blocks == sub), score, total)
        sums.append(total + fine_ref[:, c * BLOCK : (c + 1) * BLOCK])
    each = per_query // subs
    for shift, out_ref in enumerate(out_refs):
        for c in range(each):
            value = sums[c]
            for other in range(1, subs):
                value = jnp.where(sub ^ shift == other, sums[other * each + c], value)
            out_ref[:, c * BLOCK : (c + 1) * BLOCK] = value


def pick(subs, place, cands, fine, got):
    per_query, own = cands.shape
    smem = pl.BlockSpec(memory_space=pltpu.SMEM)
    vmem = pl.BlockSpec(memory_space=pltpu.VMEM)
    return pl.pallas_call(
        partial(pick_kernel, subs, len(got)),
        in_specs=[smem, smem] + [vmem] * (1 + len(got)),
        out_specs=[vmem] * subs,
        out_shape=[pltpu.VMEM((own, per_query // subs * BLOCK), jnp.float32)] * subs,
        name="pick",
    )(place, cands, on_chip(fine), *[on_chip(g) for g in got])


def arrange_kernel(*refs):
    in_refs, out_ref, order_ref = refs[:-2], refs[-2], refs[-1]
    cell = lax.axis_index("cells")
    for k, in_ref in enumerate(in_refs):
        order_ref[cell ^ k] = in_ref[...].astype(jnp.float32)
    out_ref[...] = jnp.stack([order_ref[h] for h in range(len(in_refs))], axis=1).astype(
        jnp.bfloat16
    )


def arrange(got):
    holders, (own, part) = len(got), got[0].shape
    return pl.pallas_call(
        arrange_kernel,
        out_shape=jax.ShapeDtypeStruct((own, holders, part), jnp.bfloat16),
        scratch_shapes=[pltpu.VMEM((holders, own, part), jnp.float32)],
        name="arrange",
    )(*[on_chip(g) for g in got])


def swap(value, axis, shift):
    return lax.ppermute(value, axis, [(i, i ^ shift) for i in range(lax.axis_size(axis))])


def shards(
    queries,
    rerank_queries,
    coarse_book,
    refine_book,
    coarse_codes,
    refine_codes,
    block_place,
    candidates,
):
    holders = lax.axis_size("cells")
    subs = lax.axis_size("sub")
    halves = lax.axis_size("rep")
    own, features = rerank_queries.shape
    per_query = candidates.shape[1]
    rows = queries.reshape(queries.shape[0] // own, own, features)
    book = jnp.swapaxes(coarse_book, 1, 2)
    fine_book = jnp.swapaxes(refine_book, 1, 2).reshape(features, refine_book.shape[1])
    sums = []
    for shift in [*range(1, subs), 0]:
        sent = coarse_part(shift, subs, halves, holders, own, rows, book, coarse_codes)
        if shift:
            rows, sent = lax.optimization_barrier((rows, sent))
        here = []
        for r, value in enumerate(sent):
            if shift or r:
                value = swap(value, ("sub", "rep"), shift * halves + r)
            here.append(value)
        sums = sums + here if shift else here + sums
    fine_codes = [refine_codes.astype(jnp.bfloat16)]
    for k in range(1, holders):
        fine_codes.append(swap(fine_codes[0], "cells", k))
    fine = refine_partials(block_place, candidates.T, rerank_queries, fine_book, fine_codes)
    pieces = combine(subs, halves, sums)
    got = [pieces[0]]
    for k in range(1, holders):
        got.append(swap(pieces[k], "cells", k))
    fine_parts = pick(subs, block_place, candidates.T, fine, got)
    refined = fine_parts[0]
    for shift in range(1, subs):
        refined = refined + swap(fine_parts[shift], "sub", shift)
    coarse = arrange(got)
    return coarse, refined.astype(jnp.bfloat16).reshape(own, per_query // subs, BLOCK)


def solution(mesh):
    placed = (
        P("groups", "sub"),
        P(("groups", "cells", "rep"), "sub"),
        P("sub", None, None),
        P("sub", None, None),
        P("sub", ("groups", "cells")),
        P("sub", ("groups", "cells")),
        P("groups"),
        P(("groups", "cells", "rep"), None),
    )
    return jax.shard_map(
        shards,
        mesh=mesh,
        in_specs=placed,
        out_specs=(
            P(("groups", "cells", "rep"), None, "sub"),
            P(("groups", "cells", "rep"), "sub", None),
        ),
        check_vma=False,
    )
```

profile of v0, /device:TPU:0, one launch (start us, length us, event | category | flops | bytes accessed | tf_op | source)
XLA Modules:
  0.0 40.4 jit_solution(16858073946866982342)
XLA Ops:
  0.6 4.6 %shard_map.95 = (bf16[4,8,2048]{2,1,0:T(8,128)(2,1)S(1)}, bf16[4,8,2048]{2,1,0:T(8,128)(2,1)S(1)}) custom-call(bf16[8,8,512]{2,1,0:T(8,128)(2,1)} %bitcast.11, bf16[32,16,256]{2,1,0:T(8,128)(2,1)} %bitcast.8, s32[32,8192]{1,0:T(8,128)} %codes_ref.3), custom_call_target="tpu_custom_call" | custom-call | tf_op jit(solution)/shard_map/pallas_call | solution.py:89
  5.2 0.0 copy-start
  5.3 4.7 %shard_map.96 = (f32[4,8,2048]{2,1,0:T(8,128)S(1)}, bf16[4,8,2048]{2,1,0:T(8,128)(2,1)S(1)}) custom-call(bf16[8,8,512]{2,1,0:T(8,128)(2,1)} %bitcast.12, bf16[32,16,256]{2,1,0:T(8,128)(2,1)} %bitcast.9, s32[32,8192]{1,0:T(8,128)} %codes_ref.3), custom_call_target="tpu_custom_call" | custom-call | tf_op jit(solution)/shard_map/pallas_call | solution.py:89
  9.9 0.6 %collective-permute-start = (bf16[4,8,2048]{2,1,0:T(8,128)(2,1)S(1)}, bf16[4,8,2048]{2,1,0:T(8,128)(2,1)S(1)}, u32[]{:S(2)}, u32[]{:S(2)}) collective-permute-start(bf16[4,8,2048]{2,1,0:T(8,128)(2,1)S(1)} %get-tuple-element.19), channel_id=1, source_target_pairs={{0,1},{1,0},{2,3},{3,2},{4,5},{5,4},{6,7},{7,6},{8,9},{9,8},{10,11... | collective-permute-start | bytes 393224 | tf_op jit(solution)/shard_map/ppermute | solution.py:239
  10.5 2.6 %collective-permute-start.1 = (bf16[4,8,2048]{2,1,0:T(8,128)(2,1)S(1)}, bf16[4,8,2048]{2,1,0:T(8,128)(2,1)S(1)}, u32[]{:S(2)}, u32[]{:S(2)}) collective-permute-start(bf16[4,8,2048]{2,1,0:T(8,128)(2,1)S(1)} %get-tuple-element.20), channel_id=1, source_target_pairs={{0,2},{1,3},{2,0},{3,1},{4,6},{5,7},{6,4},{7,5},{8,10},{9,11},{10,... | collective-permute-start | bytes 393224 | tf_op jit(solution)/shard_map/ppermute | solution.py:239
  13.0 0.0 collective-permute-start.2
  13.1 0.0 copy-done
  13.1 1.9 %collective-permute-start.6 = (bf16[8,8192]{1,0:T(8,128)(2,1)S(1)}, bf16[8,8192]{1,0:T(8,128)(2,1)S(1)}, u32[]{:S(2)}, u32[]{:S(2)}) collective-permute-start(bf16[8,8192]{1,0:T(8,128)(2,1)S(1)} %convert_element_type.6.refs_0_), channel_id=1, source_target_pairs={{0,4},{4,0},{8,12},{12,8},{1,5},{5,1},{9,13},{13,9},{2,6},{6,2},{1... | collective-permute-start | bytes 393224 | tf_op jit(solution)/shard_map/ppermute | solution.py:239
  15.0 2.6 %collective-permute-start.7 = (bf16[8,8192]{1,0:T(8,128)(2,1)S(1)}, bf16[8,8192]{1,0:T(8,128)(2,1)S(1)}, u32[]{:S(2)}, u32[]{:S(2)}) collective-permute-start(bf16[8,8192]{1,0:T(8,128)(2,1)S(1)} %convert_element_type.6.refs_0_), channel_id=1, source_target_pairs={{0,8},{4,12},{8,0},{12,4},{1,9},{5,13},{9,1},{13,5},{2,10},{6,14},... | collective-permute-start | bytes 393224 | tf_op jit(solution)/shard_map/ppermute | solution.py:239
  17.6 0.0 collective-permute-done.refs_1_
  17.6 0.0 collective-permute-start.8
  17.6 0.0 collective-permute-done.1.refs_2_
  17.6 2.1 %collective-permute-done.2.refs_3_ = bf16[4,8,2048]{2,1,0:T(8,128)(2,1)S(1)} collective-permute-done((bf16[4,8,2048]{2,1,0:T(8,128)(2,1)S(1)}, bf16[4,8,2048]{2,1,0:T(8,128)(2,1)S(1)}, u32[]{:S(2)}, u32[]{:S(2)}) %collective-permute-start.2) | collective-permute-done | bytes 131104 | tf_op jit(solution)/shard_map/ppermute | solution.py:239
  19.7 0.1 combine.1
  19.7 1.6 %collective-permute-start.3 = (bf16[8,4096]{1,0:T(8,128)(2,1)S(1)}, bf16[8,4096]{1,0:T(8,128)(2,1)S(1)}, u32[]{:S(2)}, u32[]{:S(2)}) collective-permute-start(bf16[8,4096]{1,0:T(8,128)(2,1)S(1)} %get-tuple-element.23), channel_id=1, source_target_pairs={{0,4},{4,0},{8,12},{12,8},{1,5},{5,1},{9,13},{13,9},{2,6},{6,2},{1... | collective-permute-start | bytes 196616 | tf_op jit(solution)/shard_map/ppermute | solution.py:239
  21.3 2.6 %collective-permute-start.4 = (bf16[8,4096]{1,0:T(8,128)(2,1)S(1)}, bf16[8,4096]{1,0:T(8,128)(2,1)S(1)}, u32[]{:S(2)}, u32[]{:S(2)}) collective-permute-start(bf16[8,4096]{1,0:T(8,128)(2,1)S(1)} %get-tuple-element.24), channel_id=1, source_target_pairs={{0,8},{4,12},{8,0},{12,4},{1,9},{5,13},{9,1},{13,5},{2,10},{6,14},... | collective-permute-start | bytes 196616 | tf_op jit(solution)/shard_map/ppermute | solution.py:239
  23.9 0.0 collective-permute-done.6.refs_1_
  23.9 0.4 %collective-permute-start.5 = (bf16[8,4096]{1,0:T(8,128)(2,1)S(1)}, bf16[8,4096]{1,0:T(8,128)(2,1)S(1)}, u32[]{:S(2)}, u32[]{:S(2)}) collective-permute-start(bf16[8,4096]{1,0:T(8,128)(2,1)S(1)} %get-tuple-element.25), channel_id=1, source_target_pairs={{0,12},{4,8},{8,4},{12,0},{1,13},{5,9},{9,5},{13,1},{2,14},{6,10},... | collective-permute-start | bytes 196616 | tf_op jit(solution)/shard_map/ppermute | solution.py:239
  24.3 3.8 %collective-permute-done.7.refs_2_ = bf16[8,8192]{1,0:T(8,128)(2,1)S(1)} collective-permute-done((bf16[8,8192]{1,0:T(8,128)(2,1)S(1)}, bf16[8,8192]{1,0:T(8,128)(2,1)S(1)}, u32[]{:S(2)}, u32[]{:S(2)}) %collective-permute-start.7) | collective-permute-done | bytes 131104 | tf_op jit(solution)/shard_map/ppermute | solution.py:239
  28.2 0.0 collective-permute-done.8.refs_3_
  28.2 1.4 %refine.1.fine_ref = f32[8,512]{1,0:T(8,128)S(1)} custom-call(s32[256]{0:T(256)} %place_ref.3, s32[4,8]{1,0:T(4,128)} %bitcast.13, bf16[8,512]{1,0:T(8,128)(2,1)} %rerank_ref.1, bf16[512,256]{1,0:T(8,128)(2,1)} %bitcast.10, bf16[8,8192]{1,0:T(8,128)(2,1)S(1)} %convert_element_type.6.refs_0_, bf16[8,8192]{1,0:T(8,128)(2,1)S(1)} %collective-permute-done.6.refs_1_, ...), custom_call_target="tpu_custom_call" | custom-call | tf_op jit(solution)/shard_map/refine/pallas_call | solution.py:137
  29.6 0.0 collective-permute-done.3.refs_1_
  29.6 5.1 %collective-permute-done.4.refs_2_ = bf16[8,4096]{1,0:T(8,128)(2,1)S(1)} collective-permute-done((bf16[8,4096]{1,0:T(8,128)(2,1)S(1)}, bf16[8,4096]{1,0:T(8,128)(2,1)S(1)}, u32[]{:S(2)}, u32[]{:S(2)}) %collective-permute-start.4) | collective-permute-done | bytes 65568 | tf_op jit(solution)/shard_map/ppermute | solution.py:239
  34.8 0.0 collective-permute-done.5.refs_3_
  34.8 1.3 %pick.1 = (f32[8,256]{1,0:T(8,128)S(1)}, f32[8,256]{1,0:T(8,128)S(1)}) custom-call(s32[256]{0:T(256)} %place_ref.3, s32[4,8]{1,0:T(4,128)} %bitcast.14, f32[8,512]{1,0:T(8,128)S(1)} %refine.1.fine_ref, bf16[8,4096]{1,0:T(8,128)(2,1)S(1)} %get-tuple-element.22.refs_0_, bf16[8,4096]{1,0:T(8,128)(2,1)S(1)} %collective-permute-done.3.refs_1_, ...), custom_call_target="tpu_custom_call" | custom-call | tf_op jit(solution)/shard_map/pick/pallas_call | solution.py:209
  36.1 1.6 %collective-permute-start.9 = (f32[8,256]{1,0:T(8,128)S(1)}, f32[8,256]{1,0:T(8,128)S(1)}, u32[]{:S(2)}, u32[]{:S(2)}) collective-permute-start(f32[8,256]{1,0:T(8,128)S(1)} %get-tuple-element.27), channel_id=1, source_target_pairs={{0,2},{2,0},{1,3},{3,1},{4,6},{6,4},{5,7},{7,5},{8,10},{10,8},{9,1... | collective-permute-start | bytes 24584 | tf_op jit(solution)/shard_map/ppermute | solution.py:239
  37.7 1.2 %arrange.1 = bf16[8,4,4096]{2,1,0:T(4,128)(2,1)} custom-call(bf16[8,4096]{1,0:T(8,128)(2,1)S(1)} %get-tuple-element.22.refs_0_, bf16[8,4096]{1,0:T(8,128)(2,1)S(1)} %collective-permute-done.3.refs_1_, bf16[8,4096]{1,0:T(8,128)(2,1)S(1)} %collective-permute-done.4.refs_2_, bf16[8,4096]{1,0:T(8,128)(2,1)S(1)} %collective-permute-done.5.refs_3_), custom_call_target="tpu_custom_call" | custom-call | tf_op jit(solution)/shard_map/arrange/pallas_call | solution.py:230
  38.8 0.9 %collective-permute-done.9 = f32[8,256]{1,0:T(8,128)S(1)} collective-permute-done((f32[8,256]{1,0:T(8,128)S(1)}, f32[8,256]{1,0:T(8,128)S(1)}, u32[]{:S(2)}, u32[]{:S(2)}) %collective-permute-start.9) | collective-permute-done | bytes 8224 | tf_op jit(solution)/shard_map/ppermute | solution.py:239
  39.8 0.6 %copy.10 = bf16[8,2,128]{2,1,0:T(2,128)(2,1)} copy(bf16[8,2,128]{2,0,1:T(8,128)(2,1)S(1)} %fusion) | data formatting | bytes 8192
  (2 shorter events, 0.0 us)
Async XLA Ops:
  5.2 7.8 %copy-start = (s32[8,8192]{1,0:T(8,128)S(1)}, s32[8,8192]{1,0:T(8,128)}, u32[]{:S(2)}) copy-start(s32[8,8192]{1,0:T(8,128)} %param.13) | copy-start | bytes 786436
  9.9 7.7 %collective-permute-start = (bf16[4,8,2048]{2,1,0:T(8,128)(2,1)S(1)}, bf16[4,8,2048]{2,1,0:T(8,128)(2,1)S(1)}, u32[]{:S(2)}, u32[]{:S(2)}) collective-permute-start(bf16[4,8,2048]{2,1,0:T(8,128)(2,1)S(1)} %get-tuple-element.19), channel_id=1, source_target_pairs={{0,1},{1,0},{2,3},{3,2},{4,5},{5,4},{6,7},{7,6},{8,9},{9,8},{10,11... | collective-permute-start | bytes 393224 | tf_op jit(solution)/shard_map/ppermute | solution.py:239
  10.5 7.1 %collective-permute-start.1 = (bf16[4,8,2048]{2,1,0:T(8,128)(2,1)S(1)}, bf16[4,8,2048]{2,1,0:T(8,128)(2,1)S(1)}, u32[]{:S(2)}, u32[]{:S(2)}) collective-permute-start(bf16[4,8,2048]{2,1,0:T(8,128)(2,1)S(1)} %get-tuple-element.20), channel_id=1, source_target_pairs={{0,2},{1,3},{2,0},{3,1},{4,6},{5,7},{6,4},{7,5},{8,10},{9,11},{10,... | collective-permute-start | bytes 393224 | tf_op jit(solution)/shard_map/ppermute | solution.py:239
  13.0 6.6 %collective-permute-start.2 = (bf16[4,8,2048]{2,1,0:T(8,128)(2,1)S(1)}, bf16[4,8,2048]{2,1,0:T(8,128)(2,1)S(1)}, u32[]{:S(2)}, u32[]{:S(2)}) collective-permute-start(bf16[4,8,2048]{2,1,0:T(8,128)(2,1)S(1)} %get-tuple-element.21), channel_id=1, source_target_pairs={{0,3},{1,2},{2,1},{3,0},{4,7},{5,6},{6,5},{7,4},{8,11},{9,10},{10,... | collective-permute-start | bytes 393224 | tf_op jit(solution)/shard_map/ppermute | solution.py:239
  13.1 10.8 %collective-permute-start.6 = (bf16[8,8192]{1,0:T(8,128)(2,1)S(1)}, bf16[8,8192]{1,0:T(8,128)(2,1)S(1)}, u32[]{:S(2)}, u32[]{:S(2)}) collective-permute-start(bf16[8,8192]{1,0:T(8,128)(2,1)S(1)} %convert_element_type.6.refs_0_), channel_id=1, source_target_pairs={{0,4},{4,0},{8,12},{12,8},{1,5},{5,1},{9,13},{13,9},{2,6},{6,2},{1... | collective-permute-start | bytes 393224 | tf_op jit(solution)/shard_map/ppermute | solution.py:239
  15.0 13.2 %collective-permute-start.7 = (bf16[8,8192]{1,0:T(8,128)(2,1)S(1)}, bf16[8,8192]{1,0:T(8,128)(2,1)S(1)}, u32[]{:S(2)}, u32[]{:S(2)}) collective-permute-start(bf16[8,8192]{1,0:T(8,128)(2,1)S(1)} %convert_element_type.6.refs_0_), channel_id=1, source_target_pairs={{0,8},{4,12},{8,0},{12,4},{1,9},{5,13},{9,1},{13,5},{2,10},{6,14},... | collective-permute-start | bytes 393224 | tf_op jit(solution)/shard_map/ppermute | solution.py:239
  17.6 10.6 %collective-permute-start.8 = (bf16[8,8192]{1,0:T(8,128)(2,1)S(1)}, bf16[8,8192]{1,0:T(8,128)(2,1)S(1)}, u32[]{:S(2)}, u32[]{:S(2)}) collective-permute-start(bf16[8,8192]{1,0:T(8,128)(2,1)S(1)} %convert_element_type.6.refs_0_), channel_id=1, source_target_pairs={{0,12},{4,8},{8,4},{12,0},{1,13},{5,9},{9,5},{13,1},{2,14},{6,10},... | collective-permute-start | bytes 393224 | tf_op jit(solution)/shard_map/ppermute | solution.py:239
  19.7 9.9 %collective-permute-start.3 = (bf16[8,4096]{1,0:T(8,128)(2,1)S(1)}, bf16[8,4096]{1,0:T(8,128)(2,1)S(1)}, u32[]{:S(2)}, u32[]{:S(2)}) collective-permute-start(bf16[8,4096]{1,0:T(8,128)(2,1)S(1)} %get-tuple-element.23), channel_id=1, source_target_pairs={{0,4},{4,0},{8,12},{12,8},{1,5},{5,1},{9,13},{13,9},{2,6},{6,2},{1... | collective-permute-start | bytes 196616 | tf_op jit(solution)/shard_map/ppermute | solution.py:239
  21.3 13.4 %collective-permute-start.4 = (bf16[8,4096]{1,0:T(8,128)(2,1)S(1)}, bf16[8,4096]{1,0:T(8,128)(2,1)S(1)}, u32[]{:S(2)}, u32[]{:S(2)}) collective-permute-start(bf16[8,4096]{1,0:T(8,128)(2,1)S(1)} %get-tuple-element.24), channel_id=1, source_target_pairs={{0,8},{4,12},{8,0},{12,4},{1,9},{5,13},{9,1},{13,5},{2,10},{6,14},... | collective-permute-start | bytes 196616 | tf_op jit(solution)/shard_map/ppermute | solution.py:239
  23.9 10.8 %collective-permute-start.5 = (bf16[8,4096]{1,0:T(8,128)(2,1)S(1)}, bf16[8,4096]{1,0:T(8,128)(2,1)S(1)}, u32[]{:S(2)}, u32[]{:S(2)}) collective-permute-start(bf16[8,4096]{1,0:T(8,128)(2,1)S(1)} %get-tuple-element.25), channel_id=1, source_target_pairs={{0,12},{4,8},{8,4},{12,0},{1,13},{5,9},{9,5},{13,1},{2,14},{6,10},... | collective-permute-start | bytes 196616 | tf_op jit(solution)/shard_map/ppermute | solution.py:239
  36.1 3.7 %collective-permute-start.9 = (f32[8,256]{1,0:T(8,128)S(1)}, f32[8,256]{1,0:T(8,128)S(1)}, u32[]{:S(2)}, u32[]{:S(2)}) collective-permute-start(f32[8,256]{1,0:T(8,128)S(1)} %get-tuple-element.27), channel_id=1, source_target_pairs={{0,2},{2,0},{1,3},{3,1},{4,6},{6,4},{5,7},{7,5},{8,10},{10,8},{9,1... | collective-permute-start | bytes 24584 | tf_op jit(solution)/shard_map/ppermute | solution.py:239
where the time goes:
time: 40.6 us; the launch traced here: 40.4 us
  starting transfers between devices  13.8 us (34%)
  Pallas kernels  13.2 us (33%)
  waiting for transfers between devices  12 us (30%)
  between operations  0.69 us (2%)
  local copies, waits for them, and re-layouts  0.61 us (2%)
    ppermute x10, starting transfers between devices, swap(): lax.ppermute(value, axis, [(i, i ^ shift) for i in range(lax.axis_size(ax...  13.8 us
    ppermute x10, waiting for transfers between devices, swap(): lax.ppermute(value, axis, [(i, i ^ shift) for i in range(lax.axis_size(ax...  12 us
    pallas_call x2, Pallas kernels, coarse_part(): pl.pallas_call(partial(coarse_kernel, halves), grid=(1,), in_specs=[whole...  9.26 us
    pallas_call x1, Pallas kernels, refine_partials(): pl.pallas_call(partial(refine_kernel, len(codes)), in_specs=[smem, smem]...  1.44 us
    pallas_call x1, Pallas kernels, pick(): pl.pallas_call(partial(pick_kernel, subs, len(got)), in_specs=[smem, smem...  1.3 us
    pallas_call x1, Pallas kernels, arrange(): pl.pallas_call(arrange_kernel, out_shape=jax.ShapeDtypeStruct((own, holde...  1.18 us
  transfers between devices with their start and end apart: 10, of which 4 were waited for; matrix products, arithmetic and copies ran while one was open for 0% of the time, Pallas kernels for 7%

commit v1 on v0

--- a/solution.py
+++ b/solution.py
@@ -42,10 +42,21 @@
     return pltpu.with_memory_space_constraint(value, pltpu.VMEM)
 
 
-def coarse_kernel(halves, q_ref, book_ref, codes_ref, *refs):
-    out_refs, tiles_ref = refs[:halves], refs[halves]
+def decode(table, codes):
+    codes = jnp.broadcast_to(codes.astype(jnp.int16), (table.shape[0], codes.shape[1]))
+    within = codes & jnp.int16(LANES - 1)
+    found = take_lanes(table[:, :LANES], within)
+    for start in range(LANES, table.shape[1], LANES):
+        found = jnp.where(
+            codes >= jnp.int16(start), take_lanes(table[:, start : start + LANES], within), found
+        )
+    return found
+
+
+def coarse_kernel(halves, q_ref, book_ref, codes_ref, out_ref):
     spaces, depth, _ = book_ref.shape
-    holders, own, chunk = out_refs[0].shape
+    _, own, tiles = out_ref.shape
+    holders = out_ref.shape[0] // halves
     half = lax.axis_index("rep")
     rows = jnp.concatenate(
         [
@@ -55,24 +66,33 @@
         ],
         axis=0,
     ).astype(jnp.bfloat16)
-
-    def fill(group, _):
-        lanes = pl.ds(pl.multiple_of(group * LANES, LANES), LANES)
-        for m in range(spaces):
-            table = book_ref[m].astype(jnp.float32)
-            codes = jnp.broadcast_to(codes_ref[m : m + 1, lanes], (8, LANES))
-            found = [lookup(table[d : d + 8], codes) for d in range(0, depth, 8)]
-            tiles_ref[m * depth : (m + 1) * depth, lanes] = jnp.concatenate(found, axis=0).astype(
-                jnp.bfloat16
+    step = min(spaces, 256 // depth)
+    for first in range(0, tiles, 2 * LANES):
+        scores = None
+        for low in range(0, spaces, step):
+            decoded = jnp.concatenate(
+                [
+                    jnp.concatenate(
+                        [
+                            decode(book_ref[m], codes_ref[m : m + 1, at : at + LANES])
+                            for at in (first, first + LANES)
+                        ],
+                        axis=1,
+                    )
+                    for m in range(low, low + step)
+                ],
+                axis=0,
             )
-        return 0
-
-    lax.fori_loop(0, chunk // LANES, fill, 0, unroll=2)
-    scores = jnp.dot(rows, tiles_ref[...], preferred_element_type=jnp.float32)
-    for r in range(halves):
-        for h in range(holders):
-            at = (r * holders + h) * own
-            out_refs[r][h] = scores[at : at + own].astype(out_refs[r].dtype)
+            part = jnp.dot(
+                rows[:, low * depth : (low + step) * depth],
+                decoded,
+                preferred_element_type=jnp.float32,
+            )
+            scores = part if scores is None else scores + part
+        for h in range(halves * holders):
+            out_ref[h, :, first : first + 2 * LANES] = scores[h * own : (h + 1) * own].astype(
+                out_ref.dtype
+            )
 
 
 def coarse_part(shift, subs, halves, holders, own, queries, book, codes):
@@ -83,16 +103,14 @@
         return 0, (lax.axis_index("sub") ^ shift) * halves + lax.axis_index("rep")
 
     whole = pl.BlockSpec(memory_space=pltpu.VMEM)
-    kinds = [jnp.bfloat16] * halves
-    if shift == 0:
-        kinds[0] = jnp.float32
     return pl.pallas_call(
         partial(coarse_kernel, halves),
         grid=(1,),
         in_specs=[whole, whole, pl.BlockSpec((spaces, quarter), place)],
-        out_specs=[whole] * halves,
-        out_shape=[pltpu.VMEM((holders, own, quarter), kind) for kind in kinds],
-        scratch_shapes=[pltpu.VMEM((book.shape[0] * book.shape[1], quarter), jnp.bfloat16)],
+        out_specs=whole,
+        out_shape=pltpu.VMEM(
+            (halves * holders, own, quarter), jnp.bfloat16 if shift else jnp.float32
+        ),
     )(queries, book, codes)
 
 
@@ -119,8 +137,8 @@
         table = table_ref[j * slot : j * slot + spaces, :]
         for c in range(per_query):
             position = place_ref[cand_ref[c, j]]
-            source = position // cell_blocks ^ cell
-            lanes = pl.ds(pl.multiple_of(position % cell_blocks * BLOCK, BLOCK), BLOCK)
+            source = lax.div(position, cell_blocks) ^ cell
+            lanes = pl.ds(pl.multiple_of(lax.rem(position, cell_blocks) * BLOCK, BLOCK), BLOCK)
             codes = codes_refs[0][:, lanes].astype(jnp.float32)
             for k in range(1, holders):
                 codes = jnp.where(source == k, codes_refs[k][:, lanes].astype(jnp.float32), codes)
@@ -147,29 +165,49 @@
     )(place, cands, reranks, book, *[on_chip(c) for c in codes])
 
 
-def combine_kernel(subs, halves, *refs):
-    in_refs, out_refs = refs[: subs * halves], refs[subs * halves :]
+def reduce_kernel(halves, *refs):
+    in_refs, out_refs = refs[:-halves], refs[-halves:]
+    holders = out_refs[0].shape[0]
+    for r, out_ref in enumerate(out_refs):
+        for h in range(holders):
+            total = in_refs[0][r * holders + h]
+            for in_ref in in_refs[1:]:
+                total = total + in_ref[r * holders + h].astype(jnp.float32)
+            out_ref[h] = total.astype(jnp.bfloat16)
+
+
+def reduce_subs(halves, sums):
+    rows, own, quarter = sums[0].shape
+    vmem = pl.BlockSpec(memory_space=pltpu.VMEM)
+    return pl.pallas_call(
+        partial(reduce_kernel, halves),
+        in_specs=[vmem] * len(sums),
+        out_specs=[vmem] * halves,
+        out_shape=[pltpu.VMEM((rows // halves, own, quarter), jnp.bfloat16)] * halves,
+        name="reduce",
+    )(*[on_chip(s) for s in sums])
+
+
+def combine_kernel(halves, *refs):
+    in_refs, out_refs = refs[:halves], refs[halves:]
     cell = lax.axis_index("cells")
     quarter = in_refs[0].shape[2]
     for k, out_ref in enumerate(out_refs):
-        for r in range(halves):
-            total = in_refs[r][cell ^ k].astype(jnp.float32)
-            for shift in range(1, subs):
-                total = total + in_refs[shift * halves + r][cell ^ k].astype(jnp.float32)
+        for r, in_ref in enumerate(in_refs):
             at = pl.multiple_of((lax.axis_index("rep") ^ r) * quarter, quarter)
-            out_ref[:, pl.ds(at, quarter)] = total.astype(jnp.bfloat16)
-
-
-def combine(subs, halves, sums):
-    holders, own, quarter = sums[0].shape
+            out_ref[:, pl.ds(at, quarter)] = in_ref[cell ^ k]
+
+
+def combine(quarters):
+    holders, own, quarter = quarters[0].shape
     vmem = pl.BlockSpec(memory_space=pltpu.VMEM)
     return pl.pallas_call(
-        partial(combine_kernel, subs, halves),
-        in_specs=[vmem] * len(sums),
+        partial(combine_kernel, len(quarters)),
+        in_specs=[vmem] * len(quarters),
         out_specs=[vmem] * holders,
-        out_shape=[pltpu.VMEM((own, quarter * halves), jnp.bfloat16)] * holders,
+        out_shape=[pltpu.VMEM((own, quarter * len(quarters)), jnp.bfloat16)] * holders,
         name="combine",
-    )(*[on_chip(s) for s in sums])
+    )(*[on_chip(q) for q in quarters])
 
 
 def pick_kernel(subs, holders, place_ref, cand_ref, fine_ref, *refs):
@@ -185,13 +223,13 @@
         total = jnp.zeros((own, BLOCK), jnp.float32)
         for j in range(own):
             position = place_ref[cand_ref[c, j]]
-            block = position % cell_blocks
-            source = position // cell_blocks ^ cell
-            lanes = pl.ds(pl.multiple_of(block % part_blocks * BLOCK, BLOCK), BLOCK)
+            block = lax.rem(position, cell_blocks)
+            source = lax.div(position, cell_blocks) ^ cell
+            lanes = pl.ds(pl.multiple_of(lax.rem(block, part_blocks) * BLOCK, BLOCK), BLOCK)
             score = got_refs[0][:, lanes].astype(jnp.float32)
             for k in range(1, holders):
                 score = jnp.where(source == k, got_refs[k][:, lanes].astype(jnp.float32), score)
-            total = jnp.where((row == j) & (block // part_blocks == sub), score, total)
+            total = jnp.where((row == j) & (lax.div(block, part_blocks) == sub), score, total)
         sums.append(total + fine_ref[:, c * BLOCK : (c + 1) * BLOCK])
     each = per_query // subs
     for shift, out_ref in enumerate(out_refs):
@@ -233,6 +271,25 @@
         scratch_shapes=[pltpu.VMEM((holders, own, part), jnp.float32)],
         name="arrange",
     )(*[on_chip(g) for g in got])
+
+
+def finish_kernel(*refs):
+    in_refs, out_ref = refs[:-1], refs[-1]
+    total = in_refs[0][...]
+    for in_ref in in_refs[1:]:
+        total = total + in_ref[...]
+    out_ref[...] = jnp.stack(
+        [total[:, c * BLOCK : (c + 1) * BLOCK] for c in range(out_ref.shape[1])], axis=1
+    ).astype(jnp.bfloat16)
+
+
+def finish(parts):
+    own, width = parts[0].shape
+    return pl.pallas_call(
+        finish_kernel,
+        out_shape=jax.ShapeDtypeStruct((own, width // BLOCK, BLOCK), jnp.bfloat16),
+        name="finish",
+    )(*[on_chip(p) for p in parts])
 
 
 def swap(value, axis, shift):
@@ -253,35 +310,33 @@
     subs = lax.axis_size("sub")
     halves = lax.axis_size("rep")
     own, features = rerank_queries.shape
-    per_query = candidates.shape[1]
     rows = queries.reshape(queries.shape[0] // own, own, features)
     book = jnp.swapaxes(coarse_book, 1, 2)
     fine_book = jnp.swapaxes(refine_book, 1, 2).reshape(features, refine_book.shape[1])
     sums = []
     for shift in [*range(1, subs), 0]:
-        sent = coarse_part(shift, subs, halves, holders, own, rows, book, coarse_codes)
+        score = coarse_part(shift, subs, halves, holders, own, rows, book, coarse_codes)
         if shift:
-            rows, sent = lax.optimization_barrier((rows, sent))
-        here = []
-        for r, value in enumerate(sent):
-            if shift or r:
-                value = swap(value, ("sub", "rep"), shift * halves + r)
-            here.append(value)
-        sums = sums + here if shift else here + sums
+            rows, score = lax.optimization_barrier((rows, score))
+            score = swap(score, "sub", shift)
+        sums.insert(0 if shift == 0 else len(sums), score)
     fine_codes = [refine_codes.astype(jnp.bfloat16)]
     for k in range(1, holders):
         fine_codes.append(swap(fine_codes[0], "cells", k))
     fine = refine_partials(block_place, candidates.T, rerank_queries, fine_book, fine_codes)
-    pieces = combine(subs, halves, sums)
+    quarters = list(reduce_subs(halves, sums))
+    for r in range(1, halves):
+        quarters[r] = swap(quarters[r], "rep", r)
+    pieces = combine(quarters)
     got = [pieces[0]]
     for k in range(1, holders):
         got.append(swap(pieces[k], "cells", k))
     fine_parts = pick(subs, block_place, candidates.T, fine, got)
-    refined = fine_parts[0]
+    fine_parts = list(fine_parts)
     for shift in range(1, subs):
-        refined = refined + swap(fine_parts[shift], "sub", shift)
+        fine_parts[shift] = swap(fine_parts[shift], "sub", shift)
     coarse = arrange(got)
-    return coarse, refined.astype(jnp.bfloat16).reshape(own, per_query // subs, BLOCK)
+    return coarse, finish(fine_parts)
 
 
 def solution(mesh):

time: 40.6 us -> 41.4 us (1.020)
  starting transfers between devices: 13.8 us -> 16.5 us
  Pallas kernels: 13.2 us -> 12 us
  local copies, waits for them, and re-layouts: 0.61 us -> 0.01 us
    ppermute x10 -> x9, starting transfers between devices: 13.8 us -> 16.5 us  [swap(): lax.ppermute(value, axis, [(i, i ^ shift) for i in range(lax.axis_size(ax...]
    pallas_call x2, Pallas kernels: 9.26 us -> 7.64 us  [coarse_part(): pl.pallas_call(partial(coarse_kernel, halves), grid=(1,), in_specs=[whole...]
    pallas_call x1 -> x3, Pallas kernels: 0.06 us -> 0.67 us  [the longest x1 0.61 us: finish(): pl.pallas_call(finish_kernel, out_shape=jax.ShapeDtypeStruct((own, width...]
    unnamed x3 -> x2, local copies, waits for them, and re-layouts: 0.61 us -> 0.01 us
    ppermute x10 -> x9, waiting for transfers between devices: 12 us -> 12 us  [swap(): lax.ppermute(value, axis, [(i, i ^ shift) for i in range(lax.axis_size(ax...]
  transfers between devices with their start and end apart: 10 -> 9, of which waited for: 4 -> 4; matrix products, arithmetic and copies ran while one was open for 0% -> 0% of each run, Pallas kernels for 7% -> 16%
where the time goes in v1:
time: 41.4 us; the launch traced here: 41.2 us
  starting transfers between devices  16.5 us (40%)
  Pallas kernels  12 us (29%)
  waiting for transfers between devices  12 us (29%)
  between operations  0.72 us (2%)
    ppermute x9, starting transfers between devices, swap(): lax.ppermute(value, axis, [(i, i ^ shift) for i in range(lax.axis_size(ax...  16.5 us
    ppermute x9, waiting for transfers between devices, swap(): lax.ppermute(value, axis, [(i, i ^ shift) for i in range(lax.axis_size(ax...  12 us
    pallas_call x2, Pallas kernels, coarse_part(): pl.pallas_call(partial(coarse_kernel, halves), grid=(1,), in_specs=[whole...  7.64 us
    pallas_call x1, Pallas kernels, refine_partials(): pl.pallas_call(partial(refine_kernel, len(codes)), in_specs=[smem, smem]...  1.38 us
    pallas_call x1, Pallas kernels, arrange(): pl.pallas_call(arrange_kernel, out_shape=jax.ShapeDtypeStruct((own, holde...  1.18 us
    pallas_call x1, Pallas kernels, pick(): pl.pallas_call(partial(pick_kernel, subs, len(got)), in_specs=[smem, smem...  1.13 us
  transfers between devices with their start and end apart: 9, of which 4 were waited for; matrix products, arithmetic and copies ran while one was open for 0% of the time, Pallas kernels for 16%

profile of v1, /device:TPU:0, one launch (start us, length us, event | category | flops | bytes accessed | tf_op | source)
XLA Modules:
  0.0 41.2 jit_solution(2732885828583254742)
XLA Ops:
  0.6 3.8 %shard_map.95 = bf16[8,8,2048]{2,1,0:T(8,128)(2,1)S(1)} custom-call(bf16[8,8,512]{2,1,0:T(8,128)(2,1)} %bitcast.9, bf16[32,16,256]{2,1,0:T(8,128)(2,1)} %bitcast.6, s32[32,8192]{1,0:T(8,128)} %codes_ref.3), custom_call_target="tpu_custom_call" | custom-call | tf_op jit(solution)/shard_map/pallas_call | solution.py:106
  4.5 3.0 %collective-permute-start = (bf16[8,8,2048]{2,1,0:T(8,128)(2,1)S(1)}, bf16[8,8,2048]{2,1,0:T(8,128)(2,1)S(1)}, u32[]{:S(2)}, u32[]{:S(2)}) collective-permute-start(bf16[8,8,2048]{2,1,0:T(8,128)(2,1)S(1)} %shard_map.95), channel_id=1, source_target_pairs={{0,2},{2,0},{1,3},{3,1},{4,6},{6,4},{5,7},{7,5},{8,10},{10,8},{9,1... | collective-permute-start | bytes 786440 | tf_op jit(solution)/shard_map/ppermute | solution.py:296
  7.5 3.8 %shard_map.96.refs_0_ = f32[8,8,2048]{2,1,0:T(8,128)S(1)} custom-call(bf16[8,8,512]{2,1,0:T(8,128)(2,1)} %bitcast.10, bf16[32,16,256]{2,1,0:T(8,128)(2,1)} %bitcast.7, s32[32,8192]{1,0:T(8,128)} %codes_ref.3), custom_call_target="tpu_custom_call" | custom-call | tf_op jit(solution)/shard_map/pallas_call | solution.py:106
  11.3 0.0 copy-start
  11.3 2.5 %collective-permute-done.refs_1_ = bf16[8,8,2048]{2,1,0:T(8,128)(2,1)S(1)} collective-permute-done((bf16[8,8,2048]{2,1,0:T(8,128)(2,1)S(1)}, bf16[8,8,2048]{2,1,0:T(8,128)(2,1)S(1)}, u32[]{:S(2)}, u32[]{:S(2)}) %collective-permute-start) | collective-permute-done | bytes 262176 | tf_op jit(solution)/shard_map/ppermute | solution.py:296
  13.8 0.1 collective-permute-start.1
  13.9 0.0 copy-done
  14.0 1.9 %collective-permute-start.5 = (bf16[8,8192]{1,0:T(8,128)(2,1)S(1)}, bf16[8,8192]{1,0:T(8,128)(2,1)S(1)}, u32[]{:S(2)}, u32[]{:S(2)}) collective-permute-start(bf16[8,8192]{1,0:T(8,128)(2,1)S(1)} %convert_element_type.3.refs_0_), channel_id=1, source_target_pairs={{0,4},{4,0},{8,12},{12,8},{1,5},{5,1},{9,13},{13,9},{2,6},{6,2},{1... | collective-permute-start | bytes 393224 | tf_op jit(solution)/shard_map/ppermute | solution.py:296
  15.9 2.6 %collective-permute-start.6 = (bf16[8,8192]{1,0:T(8,128)(2,1)S(1)}, bf16[8,8192]{1,0:T(8,128)(2,1)S(1)}, u32[]{:S(2)}, u32[]{:S(2)}) collective-permute-start(bf16[8,8192]{1,0:T(8,128)(2,1)S(1)} %convert_element_type.3.refs_0_), channel_id=1, source_target_pairs={{0,8},{4,12},{8,0},{12,4},{1,9},{5,13},{9,1},{13,5},{2,10},{6,14},... | collective-permute-start | bytes 393224 | tf_op jit(solution)/shard_map/ppermute | solution.py:296
  18.4 0.0 collective-permute-start.7
  18.4 0.0 collective-permute-done.1.refs_1_
  18.5 1.0 %collective-permute-start.2 = (bf16[8,4096]{1,0:T(8,128)(2,1)S(1)}, bf16[8,4096]{1,0:T(8,128)(2,1)S(1)}, u32[]{:S(2)}, u32[]{:S(2)}) collective-permute-start(bf16[8,4096]{1,0:T(8,128)(2,1)S(1)} %get-tuple-element.17), channel_id=1, source_target_pairs={{0,4},{4,0},{8,12},{12,8},{1,5},{5,1},{9,13},{13,9},{2,6},{6,2},{1... | collective-permute-start | bytes 196616 | tf_op jit(solution)/shard_map/ppermute | solution.py:296
  19.4 3.5 %collective-permute-start.3 = (bf16[8,4096]{1,0:T(8,128)(2,1)S(1)}, bf16[8,4096]{1,0:T(8,128)(2,1)S(1)}, u32[]{:S(2)}, u32[]{:S(2)}) collective-permute-start(bf16[8,4096]{1,0:T(8,128)(2,1)S(1)} %get-tuple-element.18), channel_id=1, source_target_pairs={{0,8},{4,12},{8,0},{12,4},{1,9},{5,13},{9,1},{13,5},{2,10},{6,14},... | collective-permute-start | bytes 196616 | tf_op jit(solution)/shard_map/ppermute | solution.py:296
  22.9 0.0 collective-permute-done.5.refs_1_
  22.9 2.9 %collective-permute-start.4 = (bf16[8,4096]{1,0:T(8,128)(2,1)S(1)}, bf16[8,4096]{1,0:T(8,128)(2,1)S(1)}, u32[]{:S(2)}, u32[]{:S(2)}) collective-permute-start(bf16[8,4096]{1,0:T(8,128)(2,1)S(1)} %get-tuple-element.19), channel_id=1, source_target_pairs={{0,12},{4,8},{8,4},{12,0},{1,13},{5,9},{9,5},{13,1},{2,14},{6,10},... | collective-permute-start | bytes 196616 | tf_op jit(solution)/shard_map/ppermute | solution.py:296
  25.8 3.0 %collective-permute-done.6.refs_2_ = bf16[8,8192]{1,0:T(8,128)(2,1)S(1)} collective-permute-done((bf16[8,8192]{1,0:T(8,128)(2,1)S(1)}, bf16[8,8192]{1,0:T(8,128)(2,1)S(1)}, u32[]{:S(2)}, u32[]{:S(2)}) %collective-permute-start.6) | collective-permute-done | bytes 131104 | tf_op jit(solution)/shard_map/ppermute | solution.py:296
  28.8 0.0 collective-permute-done.7.refs_3_
  28.8 1.4 %refine.1.fine_ref = f32[8,512]{1,0:T(8,128)S(1)} custom-call(s32[256]{0:T(256)} %place_ref.3, s32[4,8]{1,0:T(4,128)} %bitcast.11, bf16[8,512]{1,0:T(8,128)(2,1)} %rerank_ref.1, bf16[512,256]{1,0:T(8,128)(2,1)} %bitcast.8, bf16[8,8192]{1,0:T(8,128)(2,1)S(1)} %convert_element_type.3.refs_0_, bf16[8,8192]{1,0:T(8,128)(2,1)S(1)} %collective-permute-done.5.refs_1_, ...), custom_call_target="tpu_custom_call" | custom-call | tf_op jit(solution)/shard_map/refine/pallas_call | solution.py:155
  30.2 0.0 collective-permute-done.2.refs_1_
  30.2 5.6 %collective-permute-done.3.refs_2_ = bf16[8,4096]{1,0:T(8,128)(2,1)S(1)} collective-permute-done((bf16[8,4096]{1,0:T(8,128)(2,1)S(1)}, bf16[8,4096]{1,0:T(8,128)(2,1)S(1)}, u32[]{:S(2)}, u32[]{:S(2)}) %collective-permute-start.3) | collective-permute-done | bytes 65568 | tf_op jit(solution)/shard_map/ppermute | solution.py:296
  35.8 0.0 collective-permute-done.4.refs_3_
  35.8 1.1 %pick.1 = (f32[8,256]{1,0:T(8,128)S(1)}, f32[8,256]{1,0:T(8,128)S(1)}) custom-call(s32[256]{0:T(256)} %place_ref.3, s32[4,8]{1,0:T(4,128)} %bitcast.12, f32[8,512]{1,0:T(8,128)S(1)} %refine.1.fine_ref, bf16[8,4096]{1,0:T(8,128)(2,1)S(1)} %get-tuple-element.16.refs_0_, bf16[8,4096]{1,0:T(8,128)(2,1)S(1)} %collective-permute-done.2.refs_1_, ...), custom_call_target="tpu_custom_call" | custom-call | tf_op jit(solution)/shard_map/pick/pallas_call | solution.py:247
  36.9 1.6 %collective-permute-start.8 = (f32[8,256]{1,0:T(8,128)S(1)}, f32[8,256]{1,0:T(8,128)S(1)}, u32[]{:S(2)}, u32[]{:S(2)}) collective-permute-start(f32[8,256]{1,0:T(8,128)S(1)} %get-tuple-element.21), channel_id=1, source_target_pairs={{0,2},{2,0},{1,3},{3,1},{4,6},{6,4},{5,7},{7,5},{8,10},{10,8},{9,1... | collective-permute-start | bytes 24584 | tf_op jit(solution)/shard_map/ppermute | solution.py:296
  38.5 1.2 %arrange.1 = bf16[8,4,4096]{2,1,0:T(4,128)(2,1)} custom-call(bf16[8,4096]{1,0:T(8,128)(2,1)S(1)} %get-tuple-element.16.refs_0_, bf16[8,4096]{1,0:T(8,128)(2,1)S(1)} %collective-permute-done.2.refs_1_, bf16[8,4096]{1,0:T(8,128)(2,1)S(1)} %collective-permute-done.3.refs_2_, bf16[8,4096]{1,0:T(8,128)(2,1)S(1)} %collective-permute-done.4.refs_3_), custom_call_target="tpu_custom_call" | custom-call | tf_op jit(solution)/shard_map/arrange/pallas_call | solution.py:268
  39.6 1.0 %collective-permute-done.8.refs_1_ = f32[8,256]{1,0:T(8,128)S(1)} collective-permute-done((f32[8,256]{1,0:T(8,128)S(1)}, f32[8,256]{1,0:T(8,128)S(1)}, u32[]{:S(2)}, u32[]{:S(2)}) %collective-permute-start.8) | collective-permute-done | bytes 8224 | tf_op jit(solution)/shard_map/ppermute | solution.py:296
  40.6 0.6 %finish.1 = bf16[8,2,128]{2,1,0:T(2,128)(2,1)} custom-call(f32[8,256]{1,0:T(8,128)S(1)} %get-tuple-element.20.refs_0_, f32[8,256]{1,0:T(8,128)S(1)} %collective-permute-done.8.refs_1_), custom_call_target="tpu_custom_call" | custom-call | tf_op jit(solution)/shard_map/finish/pallas_call | solution.py:288
  (3 shorter events, 0.1 us)
Async XLA Ops:
  4.5 9.3 %collective-permute-start = (bf16[8,8,2048]{2,1,0:T(8,128)(2,1)S(1)}, bf16[8,8,2048]{2,1,0:T(8,128)(2,1)S(1)}, u32[]{:S(2)}, u32[]{:S(2)}) collective-permute-start(bf16[8,8,2048]{2,1,0:T(8,128)(2,1)S(1)} %shard_map.95), channel_id=1, source_target_pairs={{0,2},{2,0},{1,3},{3,1},{4,6},{6,4},{5,7},{7,5},{8,10},{10,8},{9,1... | collective-permute-start | bytes 786440 | tf_op jit(solution)/shard_map/ppermute | solution.py:296
  11.3 2.6 %copy-start = (s32[8,8192]{1,0:T(8,128)S(1)}, s32[8,8192]{1,0:T(8,128)}, u32[]{:S(2)}) copy-start(s32[8,8192]{1,0:T(8,128)} %param.13) | copy-start | bytes 786436
  13.8 4.6 %collective-permute-start.1 = (bf16[4,8,2048]{2,1,0:T(8,128)(2,1)S(1)}, bf16[4,8,2048]{2,1,0:T(8,128)(2,1)S(1)}, u32[]{:S(2)}, u32[]{:S(2)}) collective-permute-start(bf16[4,8,2048]{2,1,0:T(8,128)(2,1)S(1)} %get-tuple-element.15), channel_id=1, source_target_pairs={{0,1},{1,0},{2,3},{3,2},{4,5},{5,4},{6,7},{7,6},{8,9},{9,8},{10,11... | collective-permute-start | bytes 393224 | tf_op jit(solution)/shard_map/ppermute | solution.py:296
  14.0 9.0 %collective-permute-start.5 = (bf16[8,8192]{1,0:T(8,128)(2,1)S(1)}, bf16[8,8192]{1,0:T(8,128)(2,1)S(1)}, u32[]{:S(2)}, u32[]{:S(2)}) collective-permute-start(bf16[8,8192]{1,0:T(8,128)(2,1)S(1)} %convert_element_type.3.refs_0_), channel_id=1, source_target_pairs={{0,4},{4,0},{8,12},{12,8},{1,5},{5,1},{9,13},{13,9},{2,6},{6,2},{1... | collective-permute-start | bytes 393224 | tf_op jit(solution)/shard_map/ppermute | solution.py:296
  15.9 12.9 %collective-permute-start.6 = (bf16[8,8192]{1,0:T(8,128)(2,1)S(1)}, bf16[8,8192]{1,0:T(8,128)(2,1)S(1)}, u32[]{:S(2)}, u32[]{:S(2)}) collective-permute-start(bf16[8,8192]{1,0:T(8,128)(2,1)S(1)} %convert_element_type.3.refs_0_), channel_id=1, source_target_pairs={{0,8},{4,12},{8,0},{12,4},{1,9},{5,13},{9,1},{13,5},{2,10},{6,14},... | collective-permute-start | bytes 393224 | tf_op jit(solution)/shard_map/ppermute | solution.py:296
  18.4 10.4 %collective-permute-start.7 = (bf16[8,8192]{1,0:T(8,128)(2,1)S(1)}, bf16[8,8192]{1,0:T(8,128)(2,1)S(1)}, u32[]{:S(2)}, u32[]{:S(2)}) collective-permute-start(bf16[8,8192]{1,0:T(8,128)(2,1)S(1)} %convert_element_type.3.refs_0_), channel_id=1, source_target_pairs={{0,12},{4,8},{8,4},{12,0},{1,13},{5,9},{9,5},{13,1},{2,14},{6,10},... | collective-permute-start | bytes 393224 | tf_op jit(solution)/shard_map/ppermute | solution.py:296
  18.5 11.7 %collective-permute-start.2 = (bf16[8,4096]{1,0:T(8,128)(2,1)S(1)}, bf16[8,4096]{1,0:T(8,128)(2,1)S(1)}, u32[]{:S(2)}, u32[]{:S(2)}) collective-permute-start(bf16[8,4096]{1,0:T(8,128)(2,1)S(1)} %get-tuple-element.17), channel_id=1, source_target_pairs={{0,4},{4,0},{8,12},{12,8},{1,5},{5,1},{9,13},{13,9},{2,6},{6,2},{1... | collective-permute-start | bytes 196616 | tf_op jit(solution)/shard_map/ppermute | solution.py:296
  19.4 16.3 %collective-permute-start.3 = (bf16[8,4096]{1,0:T(8,128)(2,1)S(1)}, bf16[8,4096]{1,0:T(8,128)(2,1)S(1)}, u32[]{:S(2)}, u32[]{:S(2)}) collective-permute-start(bf16[8,4096]{1,0:T(8,128)(2,1)S(1)} %get-tuple-element.18), channel_id=1, source_target_pairs={{0,8},{4,12},{8,0},{12,4},{1,9},{5,13},{9,1},{13,5},{2,10},{6,14},... | collective-permute-start | bytes 196616 | tf_op jit(solution)/shard_map/ppermute | solution.py:296
  22.9 12.8 %collective-permute-start.4 = (bf16[8,4096]{1,0:T(8,128)(2,1)S(1)}, bf16[8,4096]{1,0:T(8,128)(2,1)S(1)}, u32[]{:S(2)}, u32[]{:S(2)}) collective-permute-start(bf16[8,4096]{1,0:T(8,128)(2,1)S(1)} %get-tuple-element.19), channel_id=1, source_target_pairs={{0,12},{4,8},{8,4},{12,0},{1,13},{5,9},{9,5},{13,1},{2,14},{6,10},... | collective-permute-start | bytes 196616 | tf_op jit(solution)/shard_map/ppermute | solution.py:296
  36.9 3.7 %collective-permute-start.8 = (f32[8,256]{1,0:T(8,128)S(1)}, f32[8,256]{1,0:T(8,128)S(1)}, u32[]{:S(2)}, u32[]{:S(2)}) collective-permute-start(f32[8,256]{1,0:T(8,128)S(1)} %get-tuple-element.21), channel_id=1, source_target_pairs={{0,2},{2,0},{1,3},{3,1},{4,6},{6,4},{5,7},{7,5},{8,10},{10,8},{9,1... | collective-permute-start | bytes 24584 | tf_op jit(solution)/shard_map/ppermute | solution.py:296

commit v2 on v1

--- a/solution.py
+++ b/solution.py
@@ -40,6 +40,10 @@
 
 def on_chip(value):
     return pltpu.with_memory_space_constraint(value, pltpu.VMEM)
+
+
+def lane_group(at):
+    return pl.ds(at if isinstance(at, int) else pl.multiple_of(at, LANES), LANES)
 
 
 def decode(table, codes):
@@ -53,7 +57,7 @@
     return found
 
 
-def coarse_kernel(halves, q_ref, book_ref, codes_ref, out_ref):
+def coarse_kernel(halves, place, q_ref, book_ref, codes_ref, out_ref):
     spaces, depth, _ = book_ref.shape
     _, own, tiles = out_ref.shape
     holders = out_ref.shape[0] // halves
@@ -67,6 +71,7 @@
         axis=0,
     ).astype(jnp.bfloat16)
     step = min(spaces, 256 // depth)
+    start = place() * tiles if codes_ref.shape[1] > tiles else 0
     for first in range(0, tiles, 2 * LANES):
         scores = None
         for low in range(0, spaces, step):
@@ -74,7 +79,7 @@
                 [
                     jnp.concatenate(
                         [
-                            decode(book_ref[m], codes_ref[m : m + 1, at : at + LANES])
+                            decode(book_ref[m], codes_ref[m : m + 1, lane_group(start + at)])
                             for at in (first, first + LANES)
                         ],
                         axis=1,
@@ -99,30 +104,36 @@
     spaces, stored = codes.shape
     quarter = stored // subs // halves
 
-    def place(step):
-        return 0, (lax.axis_index("sub") ^ shift) * halves + lax.axis_index("rep")
+    def place():
+        return (lax.axis_index("sub") ^ shift) * halves + lax.axis_index("rep")
 
     whole = pl.BlockSpec(memory_space=pltpu.VMEM)
-    return pl.pallas_call(
-        partial(coarse_kernel, halves),
+    block = pl.BlockSpec((spaces, quarter), lambda step: (0, place()))
+    operands = (queries, book, codes)
+    if shift == 0:
+        block, operands = whole, [on_chip(x) for x in operands]
+    return pl.pallas_call(
+        partial(coarse_kernel, halves, place),
         grid=(1,),
-        in_specs=[whole, whole, pl.BlockSpec((spaces, quarter), place)],
+        in_specs=[whole, whole, block],
         out_specs=whole,
         out_shape=pltpu.VMEM(
             (halves * holders, own, quarter), jnp.bfloat16 if shift else jnp.float32
         ),
-    )(queries, book, codes)
-
-
-def refine_kernel(holders, place_ref, cand_ref, rerank_ref, book_ref, *refs):
+    )(*operands)
+
+
+def refine_kernel(holders, subs, place_ref, cand_ref, rerank_ref, book_ref, *refs):
     codes_refs = refs[:holders]
-    out_ref, wide_ref, table_ref = refs[holders:]
+    out_ref, found_ref, wide_ref, table_ref = refs[holders:]
     per_query, own = cand_ref.shape
     spaces, stored = codes_refs[0].shape
     width = book_ref.shape[0]
     depth = width // spaces
     cell_blocks = stored // BLOCK
+    part_blocks = cell_blocks // subs
     cell = lax.axis_index("cells")
+    sub = lax.axis_index("sub")
     slot = -(-spaces // 8) * 8
     mine = lax.broadcasted_iota(jnp.int32, (slot, width), 1) // depth == (
         lax.broadcasted_iota(jnp.int32, (slot, width), 0)
@@ -138,7 +149,14 @@
         for c in range(per_query):
             position = place_ref[cand_ref[c, j]]
             source = lax.div(position, cell_blocks) ^ cell
-            lanes = pl.ds(pl.multiple_of(lax.rem(position, cell_blocks) * BLOCK, BLOCK), BLOCK)
+            block = lax.rem(position, cell_blocks)
+            arrival = jnp.where(
+                lax.div(block, part_blocks) == sub,
+                source * part_blocks + lax.rem(block, part_blocks),
+                -1,
+            )
+            found_ref[j : j + 1, c * BLOCK : (c + 1) * BLOCK] = jnp.full((1, BLOCK), arrival)
+            lanes = pl.ds(pl.multiple_of(block * BLOCK, BLOCK), BLOCK)
             codes = codes_refs[0][:, lanes].astype(jnp.float32)
             for k in range(1, holders):
                 codes = jnp.where(source == k, codes_refs[k][:, lanes].astype(jnp.float32), codes)
@@ -146,17 +164,20 @@
             out_ref[j : j + 1, c * BLOCK : (c + 1) * BLOCK] = jnp.sum(found, axis=0, keepdims=True)
 
 
-def refine_partials(place, cands, reranks, book, codes):
+def refine_partials(subs, place, cands, reranks, book, codes):
     per_query, own = cands.shape
     spaces = codes[0].shape[0]
     rows = own * (-(-spaces // 8) * 8)
     smem = pl.BlockSpec(memory_space=pltpu.SMEM)
     vmem = pl.BlockSpec(memory_space=pltpu.VMEM)
     return pl.pallas_call(
-        partial(refine_kernel, len(codes)),
+        partial(refine_kernel, len(codes), subs),
         in_specs=[smem, smem] + [vmem] * (2 + len(codes)),
-        out_specs=vmem,
-        out_shape=pltpu.VMEM((own, per_query * BLOCK), jnp.float32),
+        out_specs=[vmem, vmem],
+        out_shape=[
+            pltpu.VMEM((own, per_query * BLOCK), jnp.float32),
+            pltpu.VMEM((own, per_query * BLOCK), jnp.int32),
+        ],
         scratch_shapes=[
             pltpu.VMEM((rows, book.shape[0]), jnp.float32),
             pltpu.VMEM((rows, book.shape[1]), jnp.float32),
@@ -210,28 +231,22 @@
     )(*[on_chip(q) for q in quarters])
 
 
-def pick_kernel(subs, holders, place_ref, cand_ref, fine_ref, *refs):
-    got_refs, out_refs = refs[:holders], refs[holders:]
-    per_query, own = cand_ref.shape
+def pick_kernel(subs, fine_ref, found_ref, *refs):
+    got_refs, out_refs = refs[:-subs], refs[-subs:]
     part_blocks = got_refs[0].shape[1] // BLOCK
-    cell_blocks = part_blocks * subs
-    cell = lax.axis_index("cells")
     sub = lax.axis_index("sub")
-    row = lax.broadcasted_iota(jnp.int32, (own, BLOCK), 0)
-    sums = []
-    for c in range(per_query):
-        total = jnp.zeros((own, BLOCK), jnp.float32)
-        for j in range(own):
-            position = place_ref[cand_ref[c, j]]
-            block = lax.rem(position, cell_blocks)
-            source = lax.div(position, cell_blocks) ^ cell
-            lanes = pl.ds(pl.multiple_of(lax.rem(block, part_blocks) * BLOCK, BLOCK), BLOCK)
-            score = got_refs[0][:, lanes].astype(jnp.float32)
-            for k in range(1, holders):
-                score = jnp.where(source == k, got_refs[k][:, lanes].astype(jnp.float32), score)
-            total = jnp.where((row == j) & (lax.div(block, part_blocks) == sub), score, total)
-        sums.append(total + fine_ref[:, c * BLOCK : (c + 1) * BLOCK])
-    each = per_query // subs
+    starts = range(0, fine_ref.shape[1], BLOCK)
+    arrivals = [found_ref[:, at : at + BLOCK] for at in starts]
+    coarse = [jnp.zeros(arrivals[0].shape, jnp.float32) for _ in starts]
+    for k, got_ref in enumerate(got_refs):
+        for b in range(part_blocks):
+            score = got_ref[:, b * BLOCK : (b + 1) * BLOCK].astype(jnp.float32)
+            coarse = [
+                jnp.where(arrival == k * part_blocks + b, score, value)
+                for arrival, value in zip(arrivals, coarse)
+            ]
+    sums = [fine_ref[:, at : at + BLOCK] + value for at, value in zip(starts, coarse)]
+    each = len(sums) // subs
     for shift, out_ref in enumerate(out_refs):
         for c in range(each):
             value = sums[c]
@@ -240,17 +255,16 @@
             out_ref[:, c * BLOCK : (c + 1) * BLOCK] = value
 
 
-def pick(subs, place, cands, fine, got):
-    per_query, own = cands.shape
-    smem = pl.BlockSpec(memory_space=pltpu.SMEM)
+def pick(subs, fine, found, got):
+    own, width = fine.shape
     vmem = pl.BlockSpec(memory_space=pltpu.VMEM)
     return pl.pallas_call(
-        partial(pick_kernel, subs, len(got)),
-        in_specs=[smem, smem] + [vmem] * (1 + len(got)),
+        partial(pick_kernel, subs),
+        in_specs=[vmem] * (2 + len(got)),
         out_specs=[vmem] * subs,
-        out_shape=[pltpu.VMEM((own, per_query // subs * BLOCK), jnp.float32)] * subs,
+        out_shape=[pltpu.VMEM((own, width // subs), jnp.float32)] * subs,
         name="pick",
-    )(place, cands, on_chip(fine), *[on_chip(g) for g in got])
+    )(on_chip(fine), on_chip(found), *[on_chip(g) for g in got])
 
 
 def arrange_kernel(*refs):
@@ -323,7 +337,9 @@
     fine_codes = [refine_codes.astype(jnp.bfloat16)]
     for k in range(1, holders):
         fine_codes.append(swap(fine_codes[0], "cells", k))
-    fine = refine_partials(block_place, candidates.T, rerank_queries, fine_book, fine_codes)
+    fine, found = refine_partials(
+        subs, block_place, candidates.T, rerank_queries, fine_book, fine_codes
+    )
     quarters = list(reduce_subs(halves, sums))
     for r in range(1, halves):
         quarters[r] = swap(quarters[r], "rep", r)
@@ -331,7 +347,7 @@
     got = [pieces[0]]
     for k in range(1, holders):
         got.append(swap(pieces[k], "cells", k))
-    fine_parts = pick(subs, block_place, candidates.T, fine, got)
+    fine_parts = pick(subs, fine, found, got)
     fine_parts = list(fine_parts)
     for shift in range(1, subs):
         fine_parts[shift] = swap(fine_parts[shift], "sub", shift)

time: 41.4 us -> 40.5 us (0.978)
  Pallas kernels: 12 us -> 10.2 us
  waiting for transfers between devices: 12 us -> 12.9 us
    pallas_call x4, Pallas kernels: 10.2 us -> 8.31 us  [the longest x2 6.7 us: coarse_part(): pl.pallas_call(partial(coarse_kernel, halves, place), grid=(1,), in_specs...]
    ppermute x9, waiting for transfers between devices: 12 us -> 12.9 us  [swap(): lax.ppermute(value, axis, [(i, i ^ shift) for i in range(lax.axis_size(ax...]
  transfers between devices with their start and end apart: 9 -> 9, of which waited for: 4 -> 4; matrix products, arithmetic and copies ran while one was open for 0% -> 0% of each run, Pallas kernels for 16% -> 13%
where the time goes in v2:
time: 40.5 us; the launch traced here: 40.4 us
  starting transfers between devices  16.5 us (41%)
  waiting for transfers between devices  12.9 us (32%)
  Pallas kernels  10.2 us (25%)
  between operations  0.74 us (2%)
    ppermute x9, starting transfers between devices, swap(): lax.ppermute(value, axis, [(i, i ^ shift) for i in range(lax.axis_size(ax...  16.5 us
    ppermute x9, waiting for transfers between devices, swap(): lax.ppermute(value, axis, [(i, i ^ shift) for i in range(lax.axis_size(ax...  12.9 us
    pallas_call x2, Pallas kernels, coarse_part(): pl.pallas_call(partial(coarse_kernel, halves, place), grid=(1,), in_specs...  6.7 us
    pallas_call x1, Pallas kernels, refine_partials(): pl.pallas_call(partial(refine_kernel, len(codes), subs), in_specs=[smem,...  1.46 us
    pallas_call x1, Pallas kernels, arrange(): pl.pallas_call(arrange_kernel, out_shape=jax.ShapeDtypeStruct((own, holde...  1.18 us
  transfers between devices with their start and end apart: 9, of which 4 were waited for; matrix products, arithmetic and copies ran while one was open for 0% of the time, Pallas kernels for 13%

profile of v2, /device:TPU:0, one launch (start us, length us, event | category | flops | bytes accessed | tf_op | source)
XLA Modules:
  0.0 40.4 jit_solution(12932015475768971468)
XLA Ops:
  0.6 0.0 copy-start
  0.6 0.0 copy-start.1
  0.6 0.0 copy-start.2
  0.7 3.9 %shard_map.95 = bf16[8,8,2048]{2,1,0:T(8,128)(2,1)S(1)} custom-call(bf16[8,8,512]{2,1,0:T(8,128)(2,1)} %bitcast.8, bf16[32,16,256]{2,1,0:T(8,128)(2,1)} %bitcast.6, s32[32,8192]{1,0:T(8,128)} %codes_ref.3), custom_call_target="tpu_custom_call" | custom-call | tf_op jit(solution)/shard_map/pallas_call | solution.py:115
  4.6 3.0 %collective-permute-start = (bf16[8,8,2048]{2,1,0:T(8,128)(2,1)S(1)}, bf16[8,8,2048]{2,1,0:T(8,128)(2,1)S(1)}, u32[]{:S(2)}, u32[]{:S(2)}) collective-permute-start(bf16[8,8,2048]{2,1,0:T(8,128)(2,1)S(1)} %shard_map.95), channel_id=1, source_target_pairs={{0,2},{2,0},{1,3},{3,1},{4,6},{6,4},{5,7},{7,5},{8,10},{10,8},{9,1... | collective-permute-start | bytes 786440 | tf_op jit(solution)/shard_map/ppermute | solution.py:310
  7.6 0.0 copy-done
  7.6 0.0 copy-done.1
  7.6 0.0 copy-done.2
  7.6 2.8 %shard_map.96.refs_0_ = f32[8,8,2048]{2,1,0:T(8,128)S(1)} custom-call(bf16[8,8,512]{2,1,0:T(8,128)(2,1)S(1)} %bitcast.9, bf16[32,16,256]{2,1,0:T(8,128)(2,1)S(1)} %bitcast.7, s32[32,8192]{1,0:T(8,128)S(1)} %copy-done), custom_call_target="tpu_custom_call" | custom-call | tf_op jit(solution)/shard_map/pallas_call | solution.py:115
  10.4 0.0 copy-start.3
  10.4 3.5 %collective-permute-done.refs_1_ = bf16[8,8,2048]{2,1,0:T(8,128)(2,1)S(1)} collective-permute-done((bf16[8,8,2048]{2,1,0:T(8,128)(2,1)S(1)}, bf16[8,8,2048]{2,1,0:T(8,128)(2,1)S(1)}, u32[]{:S(2)}, u32[]{:S(2)}) %collective-permute-start) | collective-permute-done | bytes 262176 | tf_op jit(solution)/shard_map/ppermute | solution.py:310
  14.0 0.1 collective-permute-start.1
  14.1 0.0 copy-done.3
  14.1 1.9 %collective-permute-start.5 = (bf16[8,8192]{1,0:T(8,128)(2,1)S(1)}, bf16[8,8192]{1,0:T(8,128)(2,1)S(1)}, u32[]{:S(2)}, u32[]{:S(2)}) collective-permute-start(bf16[8,8192]{1,0:T(8,128)(2,1)S(1)} %convert_element_type.3.refs_0_), channel_id=1, source_target_pairs={{0,4},{4,0},{8,12},{12,8},{1,5},{5,1},{9,13},{13,9},{2,6},{6,2},{1... | collective-permute-start | bytes 393224 | tf_op jit(solution)/shard_map/ppermute | solution.py:310
  16.0 2.6 %collective-permute-start.6 = (bf16[8,8192]{1,0:T(8,128)(2,1)S(1)}, bf16[8,8192]{1,0:T(8,128)(2,1)S(1)}, u32[]{:S(2)}, u32[]{:S(2)}) collective-permute-start(bf16[8,8192]{1,0:T(8,128)(2,1)S(1)} %convert_element_type.3.refs_0_), channel_id=1, source_target_pairs={{0,8},{4,12},{8,0},{12,4},{1,9},{5,13},{9,1},{13,5},{2,10},{6,14},... | collective-permute-start | bytes 393224 | tf_op jit(solution)/shard_map/ppermute | solution.py:310
  18.6 0.0 collective-permute-start.7
  18.6 0.0 collective-permute-done.1.refs_1_
  18.6 1.0 %collective-permute-start.2 = (bf16[8,4096]{1,0:T(8,128)(2,1)S(1)}, bf16[8,4096]{1,0:T(8,128)(2,1)S(1)}, u32[]{:S(2)}, u32[]{:S(2)}) collective-permute-start(bf16[8,4096]{1,0:T(8,128)(2,1)S(1)} %get-tuple-element.19), channel_id=1, source_target_pairs={{0,4},{4,0},{8,12},{12,8},{1,5},{5,1},{9,13},{13,9},{2,6},{6,2},{1... | collective-permute-start | bytes 196616 | tf_op jit(solution)/shard_map/ppermute | solution.py:310
  19.6 3.5 %collective-permute-start.3 = (bf16[8,4096]{1,0:T(8,128)(2,1)S(1)}, bf16[8,4096]{1,0:T(8,128)(2,1)S(1)}, u32[]{:S(2)}, u32[]{:S(2)}) collective-permute-start(bf16[8,4096]{1,0:T(8,128)(2,1)S(1)} %get-tuple-element.20), channel_id=1, source_target_pairs={{0,8},{4,12},{8,0},{12,4},{1,9},{5,13},{9,1},{13,5},{2,10},{6,14},... | collective-permute-start | bytes 196616 | tf_op jit(solution)/shard_map/ppermute | solution.py:310
  23.1 0.0 collective-permute-done.5.refs_1_
  23.1 2.9 %collective-permute-start.4 = (bf16[8,4096]{1,0:T(8,128)(2,1)S(1)}, bf16[8,4096]{1,0:T(8,128)(2,1)S(1)}, u32[]{:S(2)}, u32[]{:S(2)}) collective-permute-start(bf16[8,4096]{1,0:T(8,128)(2,1)S(1)} %get-tuple-element.21), channel_id=1, source_target_pairs={{0,12},{4,8},{8,4},{12,0},{1,13},{5,9},{9,5},{13,1},{2,14},{6,10},... | collective-permute-start | bytes 196616 | tf_op jit(solution)/shard_map/ppermute | solution.py:310
  25.9 3.0 %collective-permute-done.6.refs_2_ = bf16[8,8192]{1,0:T(8,128)(2,1)S(1)} collective-permute-done((bf16[8,8192]{1,0:T(8,128)(2,1)S(1)}, bf16[8,8192]{1,0:T(8,128)(2,1)S(1)}, u32[]{:S(2)}, u32[]{:S(2)}) %collective-permute-start.6) | collective-permute-done | bytes 131104 | tf_op jit(solution)/shard_map/ppermute | solution.py:310
  28.9 0.0 collective-permute-done.7.refs_3_
  28.9 1.5 %refine.1 = (f32[8,512]{1,0:T(8,128)S(1)}, s32[8,512]{1,0:T(8,128)S(1)}) custom-call(s32[256]{0:T(256)} %place_ref.1, s32[4,8]{1,0:T(4,128)} %bitcast.11, bf16[8,512]{1,0:T(8,128)(2,1)} %rerank_ref.1, bf16[512,256]{1,0:T(8,128)(2,1)} %bitcast.10, bf16[8,8192]{1,0:T(8,128)(2,1)S(1)} %convert_element_type.3.refs_0_, ...), custom_call_target="tpu_custom_call" | custom-call | tf_op jit(solution)/shard_map/refine/pallas_call | solution.py:173
  30.4 0.0 collective-permute-done.2.refs_1_
  30.4 5.5 %collective-permute-done.3.refs_2_ = bf16[8,4096]{1,0:T(8,128)(2,1)S(1)} collective-permute-done((bf16[8,4096]{1,0:T(8,128)(2,1)S(1)}, bf16[8,4096]{1,0:T(8,128)(2,1)S(1)}, u32[]{:S(2)}, u32[]{:S(2)}) %collective-permute-start.3) | collective-permute-done | bytes 65568 | tf_op jit(solution)/shard_map/ppermute | solution.py:310
  35.9 0.0 collective-permute-done.4.refs_3_
  35.9 0.2 pick.1
  36.0 1.6 %collective-permute-start.8 = (f32[8,256]{1,0:T(8,128)S(1)}, f32[8,256]{1,0:T(8,128)S(1)}, u32[]{:S(2)}, u32[]{:S(2)}) collective-permute-start(f32[8,256]{1,0:T(8,128)S(1)} %get-tuple-element.25), channel_id=1, source_target_pairs={{0,2},{2,0},{1,3},{3,1},{4,6},{6,4},{5,7},{7,5},{8,10},{10,8},{9,1... | collective-permute-start | bytes 24584 | tf_op jit(solution)/shard_map/ppermute | solution.py:310
  37.6 1.2 %arrange.1 = bf16[8,4,4096]{2,1,0:T(4,128)(2,1)} custom-call(bf16[8,4096]{1,0:T(8,128)(2,1)S(1)} %get-tuple-element.18.refs_0_, bf16[8,4096]{1,0:T(8,128)(2,1)S(1)} %collective-permute-done.2.refs_1_, bf16[8,4096]{1,0:T(8,128)(2,1)S(1)} %collective-permute-done.3.refs_2_, bf16[8,4096]{1,0:T(8,128)(2,1)S(1)} %collective-permute-done.4.refs_3_), custom_call_target="tpu_custom_call" | custom-call | tf_op jit(solution)/shard_map/arrange/pallas_call | solution.py:282
  38.8 1.0 %collective-permute-done.8.refs_1_ = f32[8,256]{1,0:T(8,128)S(1)} collective-permute-done((f32[8,256]{1,0:T(8,128)S(1)}, f32[8,256]{1,0:T(8,128)S(1)}, u32[]{:S(2)}, u32[]{:S(2)}) %collective-permute-start.8) | collective-permute-done | bytes 8224 | tf_op jit(solution)/shard_map/ppermute | solution.py:310
  39.8 0.6 %finish.1 = bf16[8,2,128]{2,1,0:T(2,128)(2,1)} custom-call(f32[8,256]{1,0:T(8,128)S(1)} %get-tuple-element.24.refs_0_, f32[8,256]{1,0:T(8,128)S(1)} %collective-permute-done.8.refs_1_), custom_call_target="tpu_custom_call" | custom-call | tf_op jit(solution)/shard_map/finish/pallas_call | solution.py:302
  (3 shorter events, 0.1 us)
Async XLA Ops:
  0.6 7.0 %copy-start = (s32[32,8192]{1,0:T(8,128)S(1)}, s32[32,8192]{1,0:T(8,128)}, u32[]{:S(2)}) copy-start(s32[32,8192]{1,0:T(8,128)} %codes_ref.3) | copy-start | bytes 3145732
  0.6 7.0 %copy-start.1 = (bf16[32,256,16]{1,2,0:T(8,128)(2,1)S(1)}, bf16[32,256,16]{1,2,0:T(8,128)(2,1)}, u32[]{:S(2)}) copy-start(bf16[32,256,16]{1,2,0:T(8,128)(2,1)} %param.10) | copy-start | bytes 786436
  0.6 7.0 %copy-start.2 = (bf16[64,512]{1,0:T(8,128)(2,1)S(1)}, bf16[64,512]{1,0:T(8,128)(2,1)}, u32[]{:S(2)}) copy-start(bf16[64,512]{1,0:T(8,128)(2,1)} %param.8) | copy-start | bytes 196612
  4.6 9.3 %collective-permute-start = (bf16[8,8,2048]{2,1,0:T(8,128)(2,1)S(1)}, bf16[8,8,2048]{2,1,0:T(8,128)(2,1)S(1)}, u32[]{:S(2)}, u32[]{:S(2)}) collective-permute-start(bf16[8,8,2048]{2,1,0:T(8,128)(2,1)S(1)} %shard_map.95), channel_id=1, source_target_pairs={{0,2},{2,0},{1,3},{3,1},{4,6},{6,4},{5,7},{7,5},{8,10},{10,8},{9,1... | collective-permute-start | bytes 786440 | tf_op jit(solution)/shard_map/ppermute | solution.py:310
  10.4 3.6 %copy-start.3 = (s32[8,8192]{1,0:T(8,128)S(1)}, s32[8,8192]{1,0:T(8,128)}, u32[]{:S(2)}) copy-start(s32[8,8192]{1,0:T(8,128)} %param.13) | copy-start | bytes 786436
  14.0 4.6 %collective-permute-start.1 = (bf16[4,8,2048]{2,1,0:T(8,128)(2,1)S(1)}, bf16[4,8,2048]{2,1,0:T(8,128)(2,1)S(1)}, u32[]{:S(2)}, u32[]{:S(2)}) collective-permute-start(bf16[4,8,2048]{2,1,0:T(8,128)(2,1)S(1)} %get-tuple-element.17), channel_id=1, source_target_pairs={{0,1},{1,0},{2,3},{3,2},{4,5},{5,4},{6,7},{7,6},{8,9},{9,8},{10,11... | collective-permute-start | bytes 393224 | tf_op jit(solution)/shard_map/ppermute | solution.py:310
  14.1 9.0 %collective-permute-start.5 = (bf16[8,8192]{1,0:T(8,128)(2,1)S(1)}, bf16[8,8192]{1,0:T(8,128)(2,1)S(1)}, u32[]{:S(2)}, u32[]{:S(2)}) collective-permute-start(bf16[8,8192]{1,0:T(8,128)(2,1)S(1)} %convert_element_type.3.refs_0_), channel_id=1, source_target_pairs={{0,4},{4,0},{8,12},{12,8},{1,5},{5,1},{9,13},{13,9},{2,6},{6,2},{1... | collective-permute-start | bytes 393224 | tf_op jit(solution)/shard_map/ppermute | solution.py:310
  16.0 12.9 %collective-permute-start.6 = (bf16[8,8192]{1,0:T(8,128)(2,1)S(1)}, bf16[8,8192]{1,0:T(8,128)(2,1)S(1)}, u32[]{:S(2)}, u32[]{:S(2)}) collective-permute-start(bf16[8,8192]{1,0:T(8,128)(2,1)S(1)} %convert_element_type.3.refs_0_), channel_id=1, source_target_pairs={{0,8},{4,12},{8,0},{12,4},{1,9},{5,13},{9,1},{13,5},{2,10},{6,14},... | collective-permute-start | bytes 393224 | tf_op jit(solution)/shard_map/ppermute | solution.py:310
  18.6 10.4 %collective-permute-start.7 = (bf16[8,8192]{1,0:T(8,128)(2,1)S(1)}, bf16[8,8192]{1,0:T(8,128)(2,1)S(1)}, u32[]{:S(2)}, u32[]{:S(2)}) collective-permute-start(bf16[8,8192]{1,0:T(8,128)(2,1)S(1)} %convert_element_type.3.refs_0_), channel_id=1, source_target_pairs={{0,12},{4,8},{8,4},{12,0},{1,13},{5,9},{9,5},{13,1},{2,14},{6,10},... | collective-permute-start | bytes 393224 | tf_op jit(solution)/shard_map/ppermute | solution.py:310
  18.6 11.8 %collective-permute-start.2 = (bf16[8,4096]{1,0:T(8,128)(2,1)S(1)}, bf16[8,4096]{1,0:T(8,128)(2,1)S(1)}, u32[]{:S(2)}, u32[]{:S(2)}) collective-permute-start(bf16[8,4096]{1,0:T(8,128)(2,1)S(1)} %get-tuple-element.19), channel_id=1, source_target_pairs={{0,4},{4,0},{8,12},{12,8},{1,5},{5,1},{9,13},{13,9},{2,6},{6,2},{1... | collective-permute-start | bytes 196616 | tf_op jit(solution)/shard_map/ppermute | solution.py:310
  19.6 16.3 %collective-permute-start.3 = (bf16[8,4096]{1,0:T(8,128)(2,1)S(1)}, bf16[8,4096]{1,0:T(8,128)(2,1)S(1)}, u32[]{:S(2)}, u32[]{:S(2)}) collective-permute-start(bf16[8,4096]{1,0:T(8,128)(2,1)S(1)} %get-tuple-element.20), channel_id=1, source_target_pairs={{0,8},{4,12},{8,0},{12,4},{1,9},{5,13},{9,1},{13,5},{2,10},{6,14},... | collective-permute-start | bytes 196616 | tf_op jit(solution)/shard_map/ppermute | solution.py:310
  23.1 12.8 %collective-permute-start.4 = (bf16[8,4096]{1,0:T(8,128)(2,1)S(1)}, bf16[8,4096]{1,0:T(8,128)(2,1)S(1)}, u32[]{:S(2)}, u32[]{:S(2)}) collective-permute-start(bf16[8,4096]{1,0:T(8,128)(2,1)S(1)} %get-tuple-element.21), channel_id=1, source_target_pairs={{0,12},{4,8},{8,4},{12,0},{1,13},{5,9},{9,5},{13,1},{2,14},{6,10},... | collective-permute-start | bytes 196616 | tf_op jit(solution)/shard_map/ppermute | solution.py:310
  36.0 3.7 %collective-permute-start.8 = (f32[8,256]{1,0:T(8,128)S(1)}, f32[8,256]{1,0:T(8,128)S(1)}, u32[]{:S(2)}, u32[]{:S(2)}) collective-permute-start(f32[8,256]{1,0:T(8,128)S(1)} %get-tuple-element.25), channel_id=1, source_target_pairs={{0,2},{2,0},{1,3},{3,1},{4,6},{6,4},{5,7},{7,5},{8,10},{10,8},{9,1... | collective-permute-start | bytes 24584 | tf_op jit(solution)/shard_map/ppermute | solution.py:310

commit v3 on v2

--- a/solution.py
+++ b/solution.py
@@ -57,9 +57,29 @@
     return found
 
 
-def coarse_kernel(halves, place, q_ref, book_ref, codes_ref, out_ref):
+def coarse_kernel(halves, place, q_ref, book_ref, codes_ref, out_ref, *loads):
+    tiles = out_ref.shape[2]
+    start = place() * tiles
+    chunk = tiles // 4 if tiles % (8 * LANES) == 0 else tiles
+    waits = []
+    if loads:
+        q_load, book_load, codes_load, sems = loads
+        copies = [(book_ref, book_load), (q_ref, q_load)] + [
+            (
+                codes_ref.at[:, pl.ds(pl.multiple_of(start + at, LANES), chunk)],
+                codes_load.at[:, at : at + chunk],
+            )
+            for at in range(0, tiles, chunk)
+        ]
+        waits = [pltpu.make_async_copy(*pair, sems.at[i]) for i, pair in enumerate(copies)]
+        for copy in waits:
+            copy.start()
+        q_ref, book_ref, codes_ref, start = q_load, book_load, codes_load, 0
+        for copy in waits[:2]:
+            copy.wait()
+        waits = waits[2:]
     spaces, depth, _ = book_ref.shape
-    _, own, tiles = out_ref.shape
+    own = out_ref.shape[1]
     holders = out_ref.shape[0] // halves
     half = lax.axis_index("rep")
     rows = jnp.concatenate(
@@ -71,8 +91,9 @@
         axis=0,
     ).astype(jnp.bfloat16)
     step = min(spaces, 256 // depth)
-    start = place() * tiles if codes_ref.shape[1] > tiles else 0
     for first in range(0, tiles, 2 * LANES):
+        if waits and first % chunk == 0:
+            waits.pop(0).wait()
         scores = None
         for low in range(0, spaces, step):
             decoded = jnp.concatenate(
@@ -107,33 +128,36 @@
     def place():
         return (lax.axis_index("sub") ^ shift) * halves + lax.axis_index("rep")
 
-    whole = pl.BlockSpec(memory_space=pltpu.VMEM)
-    block = pl.BlockSpec((spaces, quarter), lambda step: (0, place()))
-    operands = (queries, book, codes)
-    if shift == 0:
-        block, operands = whole, [on_chip(x) for x in operands]
+    operands, loads = (queries, book, codes), []
+    if shift:
+        loads = [pltpu.VMEM(x.shape, x.dtype) for x in (queries, book)]
+        loads += [pltpu.VMEM((spaces, quarter), codes.dtype), pltpu.SemaphoreType.DMA((6,))]
+    else:
+        operands = [on_chip(x) for x in operands]
     return pl.pallas_call(
         partial(coarse_kernel, halves, place),
-        grid=(1,),
-        in_specs=[whole, whole, block],
-        out_specs=whole,
+        in_specs=[pl.BlockSpec(memory_space=pl.ANY if shift else pltpu.VMEM)] * 3,
+        out_specs=pl.BlockSpec(memory_space=pltpu.VMEM),
         out_shape=pltpu.VMEM(
             (halves * holders, own, quarter), jnp.bfloat16 if shift else jnp.float32
         ),
+        scratch_shapes=loads,
     )(*operands)
 
 
 def refine_kernel(holders, subs, place_ref, cand_ref, rerank_ref, book_ref, *refs):
-    codes_refs = refs[:holders]
-    out_ref, found_ref, wide_ref, table_ref = refs[holders:]
+    own_ref, codes_refs = refs[0], refs[1:-4]
+    out_ref, found_ref, wide_ref, table_ref = refs[-4:]
+    halves = len(codes_refs) // (holders - 1)
     per_query, own = cand_ref.shape
-    spaces, stored = codes_refs[0].shape
+    spaces, stored = own_ref.shape
     width = book_ref.shape[0]
     depth = width // spaces
     cell_blocks = stored // BLOCK
     part_blocks = cell_blocks // subs
     cell = lax.axis_index("cells")
     sub = lax.axis_index("sub")
+    half = lax.axis_index("rep")
     slot = -(-spaces // 8) * 8
     mine = lax.broadcasted_iota(jnp.int32, (slot, width), 1) // depth == (
         lax.broadcasted_iota(jnp.int32, (slot, width), 0)
@@ -157,21 +181,25 @@
             )
             found_ref[j : j + 1, c * BLOCK : (c + 1) * BLOCK] = jnp.full((1, BLOCK), arrival)
             lanes = pl.ds(pl.multiple_of(block * BLOCK, BLOCK), BLOCK)
-            codes = codes_refs[0][:, lanes].astype(jnp.float32)
-            for k in range(1, holders):
-                codes = jnp.where(source == k, codes_refs[k][:, lanes].astype(jnp.float32), codes)
-            found = lookup(table, codes.astype(jnp.int32))
+            codes = own_ref[:, lanes]
+            share = cell_blocks // halves
+            lanes = pl.ds(pl.multiple_of(lax.rem(block, share) * BLOCK, BLOCK), BLOCK)
+            where = source * halves + (lax.div(block, share) ^ half)
+            for at, codes_ref in enumerate(codes_refs, halves):
+                got = codes_ref[:, lanes].astype(jnp.float32).astype(jnp.int32)
+                codes = jnp.where(where == at, got, codes)
+            found = lookup(table, codes)
             out_ref[j : j + 1, c * BLOCK : (c + 1) * BLOCK] = jnp.sum(found, axis=0, keepdims=True)
 
 
-def refine_partials(subs, place, cands, reranks, book, codes):
+def refine_partials(holders, subs, place, cands, reranks, book, codes):
     per_query, own = cands.shape
     spaces = codes[0].shape[0]
     rows = own * (-(-spaces // 8) * 8)
     smem = pl.BlockSpec(memory_space=pltpu.SMEM)
     vmem = pl.BlockSpec(memory_space=pltpu.VMEM)
     return pl.pallas_call(
-        partial(refine_kernel, len(codes), subs),
+        partial(refine_kernel, holders, subs),
         in_specs=[smem, smem] + [vmem] * (2 + len(codes)),
         out_specs=[vmem, vmem],
         out_shape=[
@@ -334,11 +362,17 @@
             rows, score = lax.optimization_barrier((rows, score))
             score = swap(score, "sub", shift)
         sums.insert(0 if shift == 0 else len(sums), score)
-    fine_codes = [refine_codes.astype(jnp.bfloat16)]
+    share = refine_codes.shape[1] // halves
+    half_codes = lax.dynamic_slice_in_dim(
+        refine_codes, lax.axis_index("rep") * share, share, 1
+    ).astype(jnp.bfloat16)
+    fine_codes = [refine_codes]
     for k in range(1, holders):
-        fine_codes.append(swap(fine_codes[0], "cells", k))
+        fine_codes.append(swap(half_codes, "cells", k))
+        for r in range(1, halves):
+            fine_codes.append(swap(fine_codes[1 + (k - 1) * halves], "rep", r))
     fine, found = refine_partials(
-        subs, block_place, candidates.T, rerank_queries, fine_book, fine_codes
+        holders, subs, block_place, candidates.T, rerank_queries, fine_book, fine_codes
     )
     quarters = list(reduce_subs(halves, sums))
     for r in range(1, halves):

time: 40.5 us -> 39.6 us (0.978)
  starting transfers between devices: 16.5 us -> 13.6 us
  waiting for transfers between devices: 12.9 us -> 14.2 us
  Pallas kernels: 10.2 us -> 10.8 us
    ppermute x9 -> x12, starting transfers between devices: 16.5 us -> 13.6 us  [swap(): lax.ppermute(value, axis, [(i, i ^ shift) for i in range(lax.axis_size(ax...]
    ppermute x9 -> x12, waiting for transfers between devices: 12.9 us -> 14.2 us  [swap(): lax.ppermute(value, axis, [(i, i ^ shift) for i in range(lax.axis_size(ax...]
    pallas_call x3, Pallas kernels: 8.16 us -> 8.82 us  [the longest x2 7.23 us: coarse_part(): pl.pallas_call(partial(coarse_kernel, halves, place), in_specs=[pl.BlockS...]
  transfers between devices with their start and end apart: 9 -> 12, of which waited for: 4 -> 6; matrix products, arithmetic and copies ran while one was open for 0% -> 0% of each run, Pallas kernels for 13% -> 14%
where the time goes in v3:
time: 39.6 us; the launch traced here: 39.4 us
  waiting for transfers between devices  14.2 us (36%)
  starting transfers between devices  13.6 us (34%)
  Pallas kernels  10.8 us (27%)
  between operations  0.75 us (2%)
    ppermute x12, waiting for transfers between devices, swap(): lax.ppermute(value, axis, [(i, i ^ shift) for i in range(lax.axis_size(ax...  14.2 us
    ppermute x12, starting transfers between devices, swap(): lax.ppermute(value, axis, [(i, i ^ shift) for i in range(lax.axis_size(ax...  13.6 us
    pallas_call x2, Pallas kernels, coarse_part(): pl.pallas_call(partial(coarse_kernel, halves, place), in_specs=[pl.BlockS...  7.23 us
    pallas_call x1, Pallas kernels, refine_partials(): pl.pallas_call(partial(refine_kernel, holders, subs), in_specs=[smem, sme...  1.59 us
    pallas_call x1, Pallas kernels, arrange(): pl.pallas_call(arrange_kernel, out_shape=jax.ShapeDtypeStruct((own, holde...  1.18 us
  transfers between devices with their start and end apart: 12, of which 6 were waited for; matrix products, arithmetic and copies ran while one was open for 0% of the time, Pallas kernels for 14%

profile of v3, /device:TPU:0, one launch (start us, length us, event | category | flops | bytes accessed | tf_op | source)
XLA Modules:
  0.0 39.4 jit_solution(17257419741833884134)
XLA Ops:
  0.6 0.0 copy-start
  0.6 0.0 copy-start.1
  0.6 0.0 copy-start.3
  0.7 4.5 %shard_map.95 = bf16[8,8,2048]{2,1,0:T(8,128)(2,1)S(1)} custom-call(bf16[8,8,512]{2,1,0:T(8,128)(2,1)} %bitcast.8, bf16[32,16,256]{2,1,0:T(8,128)(2,1)} %bitcast.6, s32[32,8192]{1,0:T(8,128)} %codes_ref.3), custom_call_target="tpu_custom_call" | custom-call | tf_op jit(solution)/shard_map/pallas_call | solution.py:137
  5.1 3.0 %collective-permute-start = (bf16[8,8,2048]{2,1,0:T(8,128)(2,1)S(1)}, bf16[8,8,2048]{2,1,0:T(8,128)(2,1)S(1)}, u32[]{:S(2)}, u32[]{:S(2)}) collective-permute-start(bf16[8,8,2048]{2,1,0:T(8,128)(2,1)S(1)} %shard_map.95), channel_id=1, source_target_pairs={{0,2},{2,0},{1,3},{3,1},{4,6},{6,4},{5,7},{7,5},{8,10},{10,8},{9,1... | collective-permute-start | bytes 786440 | tf_op jit(solution)/shard_map/ppermute | solution.py:338
  8.2 0.0 copy-done
  8.2 0.0 copy-done.1
  8.2 0.0 copy-done.3
  8.2 2.8 %shard_map.96.refs_0_ = f32[8,8,2048]{2,1,0:T(8,128)S(1)} custom-call(bf16[8,8,512]{2,1,0:T(8,128)(2,1)S(1)} %bitcast.9, bf16[32,16,256]{2,1,0:T(8,128)(2,1)S(1)} %bitcast.7, s32[32,8192]{1,0:T(8,128)S(1)} %copy-done), custom_call_target="tpu_custom_call" | custom-call | tf_op jit(solution)/shard_map/pallas_call | solution.py:137
  11.0 0.0 copy-start.2
  11.0 3.5 %collective-permute-done.refs_1_ = bf16[8,8,2048]{2,1,0:T(8,128)(2,1)S(1)} collective-permute-done((bf16[8,8,2048]{2,1,0:T(8,128)(2,1)S(1)}, bf16[8,8,2048]{2,1,0:T(8,128)(2,1)S(1)}, u32[]{:S(2)}, u32[]{:S(2)}) %collective-permute-start) | collective-permute-done | bytes 262176 | tf_op jit(solution)/shard_map/ppermute | solution.py:338
  14.5 0.1 collective-permute-start.1
  14.6 0.0 copy-done.2
  14.6 1.9 %collective-permute-start.5 = (bf16[8,4096]{1,0:T(8,128)(2,1)S(1)}, bf16[8,4096]{1,0:T(8,128)(2,1)S(1)}, u32[]{:S(2)}, u32[]{:S(2)}) collective-permute-start(bf16[8,4096]{1,0:T(8,128)(2,1)S(1)} %dynamic-slice_convert_fusion), channel_id=1, source_target_pairs={{0,4},{4,0},{8,12},{12,8},{1,5},{5,1},{9,13},{13,9},{2,6},{6,2},{1... | collective-permute-start | bytes 196616 | tf_op jit(solution)/shard_map/ppermute | solution.py:338
  16.5 2.6 %collective-permute-start.7 = (bf16[8,4096]{1,0:T(8,128)(2,1)S(1)}, bf16[8,4096]{1,0:T(8,128)(2,1)S(1)}, u32[]{:S(2)}, u32[]{:S(2)}) collective-permute-start(bf16[8,4096]{1,0:T(8,128)(2,1)S(1)} %dynamic-slice_convert_fusion), channel_id=1, source_target_pairs={{0,8},{4,12},{8,0},{12,4},{1,9},{5,13},{9,1},{13,5},{2,10},{6,14},... | collective-permute-start | bytes 196616 | tf_op jit(solution)/shard_map/ppermute | solution.py:338
  19.1 0.0 collective-permute-start.9
  19.1 0.1 collective-permute-done.5.refs_1_
  19.3 0.0 collective-permute-start.6
  19.3 4.3 %collective-permute-done.7.refs_3_ = bf16[8,4096]{1,0:T(8,128)(2,1)S(1)} collective-permute-done((bf16[8,4096]{1,0:T(8,128)(2,1)S(1)}, bf16[8,4096]{1,0:T(8,128)(2,1)S(1)}, u32[]{:S(2)}, u32[]{:S(2)}) %collective-permute-start.7) | collective-permute-done | bytes 65568 | tf_op jit(solution)/shard_map/ppermute | solution.py:338
  23.5 0.0 collective-permute-start.8
  23.5 1.6 %collective-permute-done.9.refs_5_ = bf16[8,4096]{1,0:T(8,128)(2,1)S(1)} collective-permute-done((bf16[8,4096]{1,0:T(8,128)(2,1)S(1)}, bf16[8,4096]{1,0:T(8,128)(2,1)S(1)}, u32[]{:S(2)}, u32[]{:S(2)}) %collective-permute-start.9) | collective-permute-done | bytes 65568 | tf_op jit(solution)/shard_map/ppermute | solution.py:338
  25.2 0.0 collective-permute-start.10
  25.2 0.0 collective-permute-done.1.refs_1_
  25.2 1.3 %collective-permute-start.2 = (bf16[8,4096]{1,0:T(8,128)(2,1)S(1)}, bf16[8,4096]{1,0:T(8,128)(2,1)S(1)}, u32[]{:S(2)}, u32[]{:S(2)}) collective-permute-start(bf16[8,4096]{1,0:T(8,128)(2,1)S(1)} %get-tuple-element.19), channel_id=1, source_target_pairs={{0,4},{4,0},{8,12},{12,8},{1,5},{5,1},{9,13},{13,9},{2,6},{6,2},{1... | collective-permute-start | bytes 196616 | tf_op jit(solution)/shard_map/ppermute | solution.py:338
  26.5 2.2 %collective-permute-start.3 = (bf16[8,4096]{1,0:T(8,128)(2,1)S(1)}, bf16[8,4096]{1,0:T(8,128)(2,1)S(1)}, u32[]{:S(2)}, u32[]{:S(2)}) collective-permute-start(bf16[8,4096]{1,0:T(8,128)(2,1)S(1)} %get-tuple-element.20), channel_id=1, source_target_pairs={{0,8},{4,12},{8,0},{12,4},{1,9},{5,13},{9,1},{13,5},{2,10},{6,14},... | collective-permute-start | bytes 196616 | tf_op jit(solution)/shard_map/ppermute | solution.py:338
  28.8 0.0 collective-permute-done.6.refs_2_
  28.8 0.9 %collective-permute-start.4 = (bf16[8,4096]{1,0:T(8,128)(2,1)S(1)}, bf16[8,4096]{1,0:T(8,128)(2,1)S(1)}, u32[]{:S(2)}, u32[]{:S(2)}) collective-permute-start(bf16[8,4096]{1,0:T(8,128)(2,1)S(1)} %get-tuple-element.21), channel_id=1, source_target_pairs={{0,12},{4,8},{8,4},{12,0},{1,13},{5,9},{9,5},{13,1},{2,14},{6,10},... | collective-permute-start | bytes 196616 | tf_op jit(solution)/shard_map/ppermute | solution.py:338
  29.7 0.0 collective-permute-done.8.refs_4_
  29.7 0.0 collective-permute-done.10.refs_6_
  29.7 1.6 %refine.1 = (f32[8,512]{1,0:T(8,128)S(1)}, s32[8,512]{1,0:T(8,128)S(1)}) custom-call(s32[256]{0:T(256)} %place_ref.1, s32[4,8]{1,0:T(4,128)} %bitcast.11, bf16[8,512]{1,0:T(8,128)(2,1)} %rerank_ref.1, bf16[512,256]{1,0:T(8,128)(2,1)} %bitcast.10, s32[8,8192]{1,0:T(8,128)S(1)} %copy-done.2, bf16[8,4096]{1,0:T(8,128)(2,1)S(1)} %collective-permute-done.5.refs_1_, ...), custom_call_target="tpu_custom_call" | custom-call | tf_op jit(solution)/shard_map/refine/pallas_call | solution.py:201
  31.3 0.0 collective-permute-done.2.refs_1_
  31.3 3.7 %collective-permute-done.3.refs_2_ = bf16[8,4096]{1,0:T(8,128)(2,1)S(1)} collective-permute-done((bf16[8,4096]{1,0:T(8,128)(2,1)S(1)}, bf16[8,4096]{1,0:T(8,128)(2,1)S(1)}, u32[]{:S(2)}, u32[]{:S(2)}) %collective-permute-start.3) | collective-permute-done | bytes 65568 | tf_op jit(solution)/shard_map/ppermute | solution.py:338
  35.0 0.0 collective-permute-done.4.refs_3_
  35.0 0.2 pick.1
  35.1 1.6 %collective-permute-start.11 = (f32[8,256]{1,0:T(8,128)S(1)}, f32[8,256]{1,0:T(8,128)S(1)}, u32[]{:S(2)}, u32[]{:S(2)}) collective-permute-start(f32[8,256]{1,0:T(8,128)S(1)} %get-tuple-element.25), channel_id=1, source_target_pairs={{0,2},{2,0},{1,3},{3,1},{4,6},{6,4},{5,7},{7,5},{8,10},{10,8},{9,1... | collective-permute-start | bytes 24584 | tf_op jit(solution)/shard_map/ppermute | solution.py:338
  36.7 1.2 %arrange.1 = bf16[8,4,4096]{2,1,0:T(4,128)(2,1)} custom-call(bf16[8,4096]{1,0:T(8,128)(2,1)S(1)} %get-tuple-element.18.refs_0_, bf16[8,4096]{1,0:T(8,128)(2,1)S(1)} %collective-permute-done.2.refs_1_, bf16[8,4096]{1,0:T(8,128)(2,1)S(1)} %collective-permute-done.3.refs_2_, bf16[8,4096]{1,0:T(8,128)(2,1)S(1)} %collective-permute-done.4.refs_3_), custom_call_target="tpu_custom_call" | custom-call | tf_op jit(solution)/shard_map/arrange/pallas_call | solution.py:310
  37.9 1.0 %collective-permute-done.11.refs_1_ = f32[8,256]{1,0:T(8,128)S(1)} collective-permute-done((f32[8,256]{1,0:T(8,128)S(1)}, f32[8,256]{1,0:T(8,128)S(1)}, u32[]{:S(2)}, u32[]{:S(2)}) %collective-permute-start.11) | collective-permute-done | bytes 8224 | tf_op jit(solution)/shard_map/ppermute | solution.py:338
  38.8 0.6 %finish.1 = bf16[8,2,128]{2,1,0:T(2,128)(2,1)} custom-call(f32[8,256]{1,0:T(8,128)S(1)} %get-tuple-element.24.refs_0_, f32[8,256]{1,0:T(8,128)S(1)} %collective-permute-done.11.refs_1_), custom_call_target="tpu_custom_call" | custom-call | tf_op jit(solution)/shard_map/finish/pallas_call | solution.py:330
  (3 shorter events, 0.1 us)
Async XLA Ops:
  0.6 7.5 %copy-start = (s32[32,8192]{1,0:T(8,128)S(1)}, s32[32,8192]{1,0:T(8,128)}, u32[]{:S(2)}) copy-start(s32[32,8192]{1,0:T(8,128)} %codes_ref.3) | copy-start | bytes 3145732
  0.6 7.5 %copy-start.1 = (bf16[32,256,16]{1,2,0:T(8,128)(2,1)S(1)}, bf16[32,256,16]{1,2,0:T(8,128)(2,1)}, u32[]{:S(2)}) copy-start(bf16[32,256,16]{1,2,0:T(8,128)(2,1)} %param.10) | copy-start | bytes 786436
  0.6 7.5 %copy-start.3 = (bf16[64,512]{1,0:T(8,128)(2,1)S(1)}, bf16[64,512]{1,0:T(8,128)(2,1)}, u32[]{:S(2)}) copy-start(bf16[64,512]{1,0:T(8,128)(2,1)} %param.8) | copy-start | bytes 196612
  5.1 9.3 %collective-permute-start = (bf16[8,8,2048]{2,1,0:T(8,128)(2,1)S(1)}, bf16[8,8,2048]{2,1,0:T(8,128)(2,1)S(1)}, u32[]{:S(2)}, u32[]{:S(2)}) collective-permute-start(bf16[8,8,2048]{2,1,0:T(8,128)(2,1)S(1)} %shard_map.95), channel_id=1, source_target_pairs={{0,2},{2,0},{1,3},{3,1},{4,6},{6,4},{5,7},{7,5},{8,10},{10,8},{9,1... | collective-permute-start | bytes 786440 | tf_op jit(solution)/shard_map/ppermute | solution.py:338
  11.0 3.6 %copy-start.2 = (s32[8,8192]{1,0:T(8,128)S(1)}, s32[8,8192]{1,0:T(8,128)}, u32[]{:S(2)}) copy-start(s32[8,8192]{1,0:T(8,128)} %refs_0_.1) | copy-start | bytes 786436
  14.5 10.7 %collective-permute-start.1 = (bf16[4,8,2048]{2,1,0:T(8,128)(2,1)S(1)}, bf16[4,8,2048]{2,1,0:T(8,128)(2,1)S(1)}, u32[]{:S(2)}, u32[]{:S(2)}) collective-permute-start(bf16[4,8,2048]{2,1,0:T(8,128)(2,1)S(1)} %get-tuple-element.17), channel_id=1, source_target_pairs={{0,1},{1,0},{2,3},{3,2},{4,5},{5,4},{6,7},{7,6},{8,9},{9,8},{10,11... | collective-permute-start | bytes 393224 | tf_op jit(solution)/shard_map/ppermute | solution.py:338
  14.6 4.6 %collective-permute-start.5 = (bf16[8,4096]{1,0:T(8,128)(2,1)S(1)}, bf16[8,4096]{1,0:T(8,128)(2,1)S(1)}, u32[]{:S(2)}, u32[]{:S(2)}) collective-permute-start(bf16[8,4096]{1,0:T(8,128)(2,1)S(1)} %dynamic-slice_convert_fusion), channel_id=1, source_target_pairs={{0,4},{4,0},{8,12},{12,8},{1,5},{5,1},{9,13},{13,9},{2,6},{6,2},{1... | collective-permute-start | bytes 196616 | tf_op jit(solution)/shard_map/ppermute | solution.py:338
  16.5 7.0 %collective-permute-start.7 = (bf16[8,4096]{1,0:T(8,128)(2,1)S(1)}, bf16[8,4096]{1,0:T(8,128)(2,1)S(1)}, u32[]{:S(2)}, u32[]{:S(2)}) collective-permute-start(bf16[8,4096]{1,0:T(8,128)(2,1)S(1)} %dynamic-slice_convert_fusion), channel_id=1, source_target_pairs={{0,8},{4,12},{8,0},{12,4},{1,9},{5,13},{9,1},{13,5},{2,10},{6,14},... | collective-permute-start | bytes 196616 | tf_op jit(solution)/shard_map/ppermute | solution.py:338
  19.1 6.1 %collective-permute-start.9 = (bf16[8,4096]{1,0:T(8,128)(2,1)S(1)}, bf16[8,4096]{1,0:T(8,128)(2,1)S(1)}, u32[]{:S(2)}, u32[]{:S(2)}) collective-permute-start(bf16[8,4096]{1,0:T(8,128)(2,1)S(1)} %dynamic-slice_convert_fusion), channel_id=1, source_target_pairs={{0,12},{4,8},{8,4},{12,0},{1,13},{5,9},{9,5},{13,1},{2,14},{6,10},... | collective-permute-start | bytes 196616 | tf_op jit(solution)/shard_map/ppermute | solution.py:338
  19.3 9.5 %collective-permute-start.6 = (bf16[8,4096]{1,0:T(8,128)(2,1)S(1)}, bf16[8,4096]{1,0:T(8,128)(2,1)S(1)}, u32[]{:S(2)}, u32[]{:S(2)}) collective-permute-start(bf16[8,4096]{1,0:T(8,128)(2,1)S(1)} %collective-permute-done.5.refs_1_), channel_id=1, source_target_pairs={{0,1},{1,0},{2,3},{3,2},{4,5},{5,4},{6,7},{7,6},{8,9},{9,8},{10,11... | collective-permute-start | bytes 196616 | tf_op jit(solution)/shard_map/ppermute | solution.py:338
  23.5 6.1 %collective-permute-start.8 = (bf16[8,4096]{1,0:T(8,128)(2,1)S(1)}, bf16[8,4096]{1,0:T(8,128)(2,1)S(1)}, u32[]{:S(2)}, u32[]{:S(2)}) collective-permute-start(bf16[8,4096]{1,0:T(8,128)(2,1)S(1)} %collective-permute-done.7.refs_3_), channel_id=1, source_target_pairs={{0,1},{1,0},{2,3},{3,2},{4,5},{5,4},{6,7},{7,6},{8,9},{9,8},{10,11... | collective-permute-start | bytes 196616 | tf_op jit(solution)/shard_map/ppermute | solution.py:338
  25.2 4.5 %collective-permute-start.10 = (bf16[8,4096]{1,0:T(8,128)(2,1)S(1)}, bf16[8,4096]{1,0:T(8,128)(2,1)S(1)}, u32[]{:S(2)}, u32[]{:S(2)}) collective-permute-start(bf16[8,4096]{1,0:T(8,128)(2,1)S(1)} %collective-permute-done.9.refs_5_), channel_id=1, source_target_pairs={{0,1},{1,0},{2,3},{3,2},{4,5},{5,4},{6,7},{7,6},{8,9},{9,8},{10,11... | collective-permute-start | bytes 196616 | tf_op jit(solution)/shard_map/ppermute | solution.py:338
  25.2 6.1 %collective-permute-start.2 = (bf16[8,4096]{1,0:T(8,128)(2,1)S(1)}, bf16[8,4096]{1,0:T(8,128)(2,1)S(1)}, u32[]{:S(2)}, u32[]{:S(2)}) collective-permute-start(bf16[8,4096]{1,0:T(8,128)(2,1)S(1)} %get-tuple-element.19), channel_id=1, source_target_pairs={{0,4},{4,0},{8,12},{12,8},{1,5},{5,1},{9,13},{13,9},{2,6},{6,2},{1... | collective-permute-start | bytes 196616 | tf_op jit(solution)/shard_map/ppermute | solution.py:338
  26.5 8.4 %collective-permute-start.3 = (bf16[8,4096]{1,0:T(8,128)(2,1)S(1)}, bf16[8,4096]{1,0:T(8,128)(2,1)S(1)}, u32[]{:S(2)}, u32[]{:S(2)}) collective-permute-start(bf16[8,4096]{1,0:T(8,128)(2,1)S(1)} %get-tuple-element.20), channel_id=1, source_target_pairs={{0,8},{4,12},{8,0},{12,4},{1,9},{5,13},{9,1},{13,5},{2,10},{6,14},... | collective-permute-start | bytes 196616 | tf_op jit(solution)/shard_map/ppermute | solution.py:338
  28.8 6.2 %collective-permute-start.4 = (bf16[8,4096]{1,0:T(8,128)(2,1)S(1)}, bf16[8,4096]{1,0:T(8,128)(2,1)S(1)}, u32[]{:S(2)}, u32[]{:S(2)}) collective-permute-start(bf16[8,4096]{1,0:T(8,128)(2,1)S(1)} %get-tuple-element.21), channel_id=1, source_target_pairs={{0,12},{4,8},{8,4},{12,0},{1,13},{5,9},{9,5},{13,1},{2,14},{6,10},... | collective-permute-start | bytes 196616 | tf_op jit(solution)/shard_map/ppermute | solution.py:338
  35.1 3.7 %collective-permute-start.11 = (f32[8,256]{1,0:T(8,128)S(1)}, f32[8,256]{1,0:T(8,128)S(1)}, u32[]{:S(2)}, u32[]{:S(2)}) collective-permute-start(f32[8,256]{1,0:T(8,128)S(1)} %get-tuple-element.25), channel_id=1, source_target_pairs={{0,2},{2,0},{1,3},{3,1},{4,6},{6,4},{5,7},{7,5},{8,10},{10,8},{9,1... | collective-permute-start | bytes 24584 | tf_op jit(solution)/shard_map/ppermute | solution.py:338

commit v4 on v3

--- a/solution.py
+++ b/solution.py
@@ -40,10 +40,6 @@
 
 def on_chip(value):
     return pltpu.with_memory_space_constraint(value, pltpu.VMEM)
-
-
-def lane_group(at):
-    return pl.ds(at if isinstance(at, int) else pl.multiple_of(at, LANES), LANES)
 
 
 def decode(table, codes):
@@ -57,27 +53,29 @@
     return found
 
 
-def coarse_kernel(halves, place, q_ref, book_ref, codes_ref, out_ref, *loads):
+def coarse_kernel(halves, shifts, q_ref, book_ref, codes_ref, out_ref, *loads):
     tiles = out_ref.shape[2]
-    start = place() * tiles
     chunk = tiles // 4 if tiles % (8 * LANES) == 0 else tiles
-    waits = []
+    waits, later = [], []
     if loads:
-        q_load, book_load, codes_load, sems = loads
-        copies = [(book_ref, book_load), (q_ref, q_load)] + [
-            (
-                codes_ref.at[:, pl.ds(pl.multiple_of(start + at, LANES), chunk)],
-                codes_load.at[:, at : at + chunk],
-            )
-            for at in range(0, tiles, chunk)
-        ]
-        waits = [pltpu.make_async_copy(*pair, sems.at[i]) for i, pair in enumerate(copies)]
-        for copy in waits:
+        q_load, book_load, *later_loads, codes_load, sems = loads
+
+        def quarter(shift, at, size):
+            place = (lax.axis_index("sub") ^ shift) * halves + lax.axis_index("rep")
+            return codes_ref.at[:, pl.ds(pl.multiple_of(place * tiles + at, LANES), size)]
+
+        pairs = [(book_ref, book_load), (q_ref, q_load)]
+        for at in range(0, tiles, chunk):
+            pairs.append((quarter(shifts[0], at, chunk), codes_load.at[:, at : at + chunk]))
+        for shift, load in zip(shifts[1:], later_loads):
+            pairs.append((quarter(shift, 0, tiles), load))
+        copies = [pltpu.make_async_copy(*pair, sems.at[i]) for i, pair in enumerate(pairs)]
+        for copy in copies:
             copy.start()
-        q_ref, book_ref, codes_ref, start = q_load, book_load, codes_load, 0
-        for copy in waits[:2]:
+        q_ref, book_ref, codes_ref = q_load, book_load, codes_load
+        for copy in copies[:2]:
             copy.wait()
-        waits = waits[2:]
+        waits, later = copies[2 : 2 + tiles // chunk], copies[2 + tiles // chunk :]
     spaces, depth, _ = book_ref.shape
     own = out_ref.shape[1]
     holders = out_ref.shape[0] // halves
@@ -100,7 +98,7 @@
                 [
                     jnp.concatenate(
                         [
-                            decode(book_ref[m], codes_ref[m : m + 1, lane_group(start + at)])
+                            decode(book_ref[m], codes_ref[m : m + 1, at : at + LANES])
                             for at in (first, first + LANES)
                         ],
                         axis=1,
@@ -121,28 +119,40 @@
             )
 
 
-def coarse_part(shift, subs, halves, holders, own, queries, book, codes):
+    for copy in later:
+        copy.wait()
+
+
+def coarse_first(shifts, subs, halves, holders, own, queries, book, codes):
     spaces, stored = codes.shape
     quarter = stored // subs // halves
-
-    def place():
-        return (lax.axis_index("sub") ^ shift) * halves + lax.axis_index("rep")
-
-    operands, loads = (queries, book, codes), []
-    if shift:
-        loads = [pltpu.VMEM(x.shape, x.dtype) for x in (queries, book)]
-        loads += [pltpu.VMEM((spaces, quarter), codes.dtype), pltpu.SemaphoreType.DMA((6,))]
-    else:
-        operands = [on_chip(x) for x in operands]
-    return pl.pallas_call(
-        partial(coarse_kernel, halves, place),
-        in_specs=[pl.BlockSpec(memory_space=pl.ANY if shift else pltpu.VMEM)] * 3,
-        out_specs=pl.BlockSpec(memory_space=pltpu.VMEM),
-        out_shape=pltpu.VMEM(
-            (halves * holders, own, quarter), jnp.bfloat16 if shift else jnp.float32
-        ),
-        scratch_shapes=loads,
-    )(*operands)
+    kind = jnp.bfloat16 if shifts[0] else jnp.float32
+    load = pltpu.VMEM((spaces, quarter), codes.dtype)
+    score, queries, book, *rest = pl.pallas_call(
+        partial(coarse_kernel, halves, shifts),
+        in_specs=[pl.BlockSpec(memory_space=pl.ANY)] * 3,
+        out_specs=[pl.BlockSpec(memory_space=pltpu.VMEM)] * (2 + len(shifts)),
+        out_shape=[
+            pltpu.VMEM((halves * holders, own, quarter), kind),
+            pltpu.VMEM(queries.shape, queries.dtype),
+            pltpu.VMEM(book.shape, book.dtype),
+        ]
+        + [load] * (len(shifts) - 1),
+        scratch_shapes=[load, pltpu.SemaphoreType.DMA((5 + len(shifts),))],
+        name="coarse_first",
+    )(queries, book, codes)
+    return score, queries, book, rest
+
+
+def coarse_next(shift, halves, holders, own, queries, book, codes):
+    kind = jnp.bfloat16 if shift else jnp.float32
+    vmem = pl.BlockSpec(memory_space=pltpu.VMEM)
+    return pl.pallas_call(
+        partial(coarse_kernel, halves, (shift,)),
+        in_specs=[vmem] * 3,
+        out_specs=vmem,
+        out_shape=pltpu.VMEM((halves * holders, own, codes.shape[1]), kind),
+    )(*[on_chip(x) for x in (queries, book, codes)])
 
 
 def refine_kernel(holders, subs, place_ref, cand_ref, rerank_ref, book_ref, *refs):
@@ -211,7 +221,7 @@
             pltpu.VMEM((rows, book.shape[1]), jnp.float32),
         ],
         name="refine",
-    )(place, cands, reranks, book, *[on_chip(c) for c in codes])
+    )(place, cands, *[on_chip(x) for x in (reranks, book, *codes)])
 
 
 def reduce_kernel(halves, *refs):
@@ -355,11 +365,15 @@
     rows = queries.reshape(queries.shape[0] // own, own, features)
     book = jnp.swapaxes(coarse_book, 1, 2)
     fine_book = jnp.swapaxes(refine_book, 1, 2).reshape(features, refine_book.shape[1])
+    shifts = [*range(1, subs), 0]
+    score, rows, book, rest = coarse_first(
+        shifts, subs, halves, holders, own, rows, book, coarse_codes
+    )
     sums = []
-    for shift in [*range(1, subs), 0]:
-        score = coarse_part(shift, subs, halves, holders, own, rows, book, coarse_codes)
+    for at, shift in enumerate(shifts):
+        if at:
+            score = coarse_next(shift, halves, holders, own, rows, book, rest[at - 1])
         if shift:
-            rows, score = lax.optimization_barrier((rows, score))
             score = swap(score, "sub", shift)
         sums.insert(0 if shift == 0 else len(sums), score)
     share = refine_codes.shape[1] // halves

time: 39.6 us -> 39.5 us (level)
  Pallas kernels: 10.8 us -> 10.4 us
  transfers between devices with their start and end apart: 12 -> 12, of which waited for: 6 -> 6; matrix products, arithmetic and copies ran while one was open for 0% -> 0% of each run, Pallas kernels for 14% -> 13%
where the time goes in v4:
time: 39.5 us; the launch traced here: 39.3 us
  waiting for transfers between devices  14.5 us (37%)
  starting transfers between devices  13.6 us (34%)
  Pallas kernels  10.4 us (26%)
  between operations  0.75 us (2%)
    ppermute x12, waiting for transfers between devices, swap(): lax.ppermute(value, axis, [(i, i ^ shift) for i in range(lax.axis_size(ax...  14.5 us
    ppermute x12, starting transfers between devices, swap(): lax.ppermute(value, axis, [(i, i ^ shift) for i in range(lax.axis_size(ax...  13.6 us
    pallas_call x1, Pallas kernels, coarse_first(): pl.pallas_call(partial(coarse_kernel, halves, shifts), in_specs=[pl.Block...  4.37 us
    pallas_call x1, Pallas kernels, coarse_next(): pl.pallas_call(partial(coarse_kernel, halves, (shift,)), in_specs=[vmem]...  2.76 us
    pallas_call x1, Pallas kernels, refine_partials(): pl.pallas_call(partial(refine_kernel, holders, subs), in_specs=[smem, sme...  1.32 us
    pallas_call x1, Pallas kernels, arrange(): pl.pallas_call(arrange_kernel, out_shape=jax.ShapeDtypeStruct((own, holde...  1.18 us
  transfers between devices with their start and end apart: 12, of which 6 were waited for; matrix products, arithmetic and copies ran while one was open for 0% of the time, Pallas kernels for 13%

profile of v4, /device:TPU:0, one launch (start us, length us, event | category | flops | bytes accessed | tf_op | source)
XLA Modules:
  0.0 39.3 jit_solution(12447878593872643516)
XLA Ops:
  0.6 4.4 %coarse_first.1 = (bf16[8,8,2048]{2,1,0:T(8,128)(2,1)S(1)}, bf16[8,8,512]{2,1,0:T(8,128)(2,1)S(1)}, bf16[32,16,256]{2,1,0:T(8,128)(2,1)S(1)}, s32[32,2048]{1,0:T(8,128)S(1)}) custom-call(bf16[8,8,512]{2,1,0:T(8,128)(2,1)} %bitcast.8, bf16[32,16,256]{2,1,0:T(8,128)(2,1)} %bitcast.7, s32[32,8192]{1,0:T(8,128)} %codes_ref.1), custom_call_target="tpu_custom_call" | custom-call | tf_op jit(solution)/shard_map/coarse_first/pallas_call | solution.py:131
  5.0 3.0 %collective-permute-start = (bf16[8,8,2048]{2,1,0:T(8,128)(2,1)S(1)}, bf16[8,8,2048]{2,1,0:T(8,128)(2,1)S(1)}, u32[]{:S(2)}, u32[]{:S(2)}) collective-permute-start(bf16[8,8,2048]{2,1,0:T(8,128)(2,1)S(1)} %get-tuple-element.19), channel_id=1, source_target_pairs={{0,2},{2,0},{1,3},{3,1},{4,6},{6,4},{5,7},{7,5},{8,10},{10,8},{9,1... | collective-permute-start | bytes 786440 | tf_op jit(solution)/shard_map/ppermute | solution.py:348
  8.0 2.8 %shard_map.95.refs_0_ = f32[8,8,2048]{2,1,0:T(8,128)S(1)} custom-call(bf16[8,8,512]{2,1,0:T(8,128)(2,1)S(1)} %get-tuple-element.16.q_ref, bf16[32,16,256]{2,1,0:T(8,128)(2,1)S(1)} %get-tuple-element.17.book_ref, s32[32,2048]{1,0:T(8,128)S(1)} %get-tuple-element.18.codes_ref), custom_call_target="tpu_custom_call" | custom-call | tf_op jit(solution)/shard_map/pallas_call | solution.py:150
  10.8 0.0 copy-start
  10.8 3.5 %collective-permute-done.refs_1_ = bf16[8,8,2048]{2,1,0:T(8,128)(2,1)S(1)} collective-permute-done((bf16[8,8,2048]{2,1,0:T(8,128)(2,1)S(1)}, bf16[8,8,2048]{2,1,0:T(8,128)(2,1)S(1)}, u32[]{:S(2)}, u32[]{:S(2)}) %collective-permute-start) | collective-permute-done | bytes 262176 | tf_op jit(solution)/shard_map/ppermute | solution.py:348
  14.4 0.0 copy-start.1
  14.4 0.1 collective-permute-start.1
  14.5 0.0 copy-done
  14.5 1.9 %collective-permute-start.5 = (bf16[8,4096]{1,0:T(8,128)(2,1)S(1)}, bf16[8,4096]{1,0:T(8,128)(2,1)S(1)}, u32[]{:S(2)}, u32[]{:S(2)}) collective-permute-start(bf16[8,4096]{1,0:T(8,128)(2,1)S(1)} %dynamic-slice_convert_fusion), channel_id=1, source_target_pairs={{0,4},{4,0},{8,12},{12,8},{1,5},{5,1},{9,13},{13,9},{2,6},{6,2},{1... | collective-permute-start | bytes 196616 | tf_op jit(solution)/shard_map/ppermute | solution.py:348
  16.4 2.6 %collective-permute-start.7 = (bf16[8,4096]{1,0:T(8,128)(2,1)S(1)}, bf16[8,4096]{1,0:T(8,128)(2,1)S(1)}, u32[]{:S(2)}, u32[]{:S(2)}) collective-permute-start(bf16[8,4096]{1,0:T(8,128)(2,1)S(1)} %dynamic-slice_convert_fusion), channel_id=1, source_target_pairs={{0,8},{4,12},{8,0},{12,4},{1,9},{5,13},{9,1},{13,5},{2,10},{6,14},... | collective-permute-start | bytes 196616 | tf_op jit(solution)/shard_map/ppermute | solution.py:348
  19.0 0.0 collective-permute-start.9
  19.0 0.1 collective-permute-done.5.refs_1_
  19.1 0.0 collective-permute-start.6
  19.1 4.3 %collective-permute-done.7.refs_3_ = bf16[8,4096]{1,0:T(8,128)(2,1)S(1)} collective-permute-done((bf16[8,4096]{1,0:T(8,128)(2,1)S(1)}, bf16[8,4096]{1,0:T(8,128)(2,1)S(1)}, u32[]{:S(2)}, u32[]{:S(2)}) %collective-permute-start.7) | collective-permute-done | bytes 65568 | tf_op jit(solution)/shard_map/ppermute | solution.py:348
  23.4 0.0 collective-permute-start.8
  23.4 1.7 %collective-permute-done.9.refs_5_ = bf16[8,4096]{1,0:T(8,128)(2,1)S(1)} collective-permute-done((bf16[8,4096]{1,0:T(8,128)(2,1)S(1)}, bf16[8,4096]{1,0:T(8,128)(2,1)S(1)}, u32[]{:S(2)}, u32[]{:S(2)}) %collective-permute-start.9) | collective-permute-done | bytes 65568 | tf_op jit(solution)/shard_map/ppermute | solution.py:348
  25.1 0.0 collective-permute-start.10
  25.1 0.0 collective-permute-done.1.refs_1_
  25.1 0.0 copy-start.2
  25.1 1.3 %collective-permute-start.2 = (bf16[8,4096]{1,0:T(8,128)(2,1)S(1)}, bf16[8,4096]{1,0:T(8,128)(2,1)S(1)}, u32[]{:S(2)}, u32[]{:S(2)}) collective-permute-start(bf16[8,4096]{1,0:T(8,128)(2,1)S(1)} %get-tuple-element.23), channel_id=1, source_target_pairs={{0,4},{4,0},{8,12},{12,8},{1,5},{5,1},{9,13},{13,9},{2,6},{6,2},{1... | collective-permute-start | bytes 196616 | tf_op jit(solution)/shard_map/ppermute | solution.py:348
  26.4 2.2 %collective-permute-start.3 = (bf16[8,4096]{1,0:T(8,128)(2,1)S(1)}, bf16[8,4096]{1,0:T(8,128)(2,1)S(1)}, u32[]{:S(2)}, u32[]{:S(2)}) collective-permute-start(bf16[8,4096]{1,0:T(8,128)(2,1)S(1)} %get-tuple-element.24), channel_id=1, source_target_pairs={{0,8},{4,12},{8,0},{12,4},{1,9},{5,13},{9,1},{13,5},{2,10},{6,14},... | collective-permute-start | bytes 196616 | tf_op jit(solution)/shard_map/ppermute | solution.py:348
  28.7 0.0 collective-permute-done.6.refs_2_
  28.7 0.9 %collective-permute-start.4 = (bf16[8,4096]{1,0:T(8,128)(2,1)S(1)}, bf16[8,4096]{1,0:T(8,128)(2,1)S(1)}, u32[]{:S(2)}, u32[]{:S(2)}) collective-permute-start(bf16[8,4096]{1,0:T(8,128)(2,1)S(1)} %get-tuple-element.25), channel_id=1, source_target_pairs={{0,12},{4,8},{8,4},{12,0},{1,13},{5,9},{9,5},{13,1},{2,14},{6,10},... | collective-permute-start | bytes 196616 | tf_op jit(solution)/shard_map/ppermute | solution.py:348
  29.6 0.0 collective-permute-done.8.refs_4_
  29.6 0.0 collective-permute-done.10.refs_6_
  29.6 0.0 copy-done.1
  29.6 0.0 copy-done.2
  29.6 1.3 %refine.1 = (f32[8,512]{1,0:T(8,128)S(1)}, s32[8,512]{1,0:T(8,128)S(1)}) custom-call(s32[256]{0:T(256)} %place_ref.1, s32[4,8]{1,0:T(4,128)} %bitcast.9, bf16[8,512]{1,0:T(8,128)(2,1)S(1)} %copy-done.2, bf16[512,256]{1,0:T(8,128)(2,1)S(1)} %bitcast.6, s32[8,8192]{1,0:T(8,128)S(1)} %copy-done, bf16[8,4096]{1,0:T(8,128)(2,1)S(1)} %collective-permute-done.5.refs_1_, ...), custom_call_target="tpu_custom_call" | custom-call | tf_op jit(solution)/shard_map/refine/pallas_call | solution.py:211
  30.9 0.0 collective-permute-done.2.refs_1_
  30.9 3.9 %collective-permute-done.3.refs_2_ = bf16[8,4096]{1,0:T(8,128)(2,1)S(1)} collective-permute-done((bf16[8,4096]{1,0:T(8,128)(2,1)S(1)}, bf16[8,4096]{1,0:T(8,128)(2,1)S(1)}, u32[]{:S(2)}, u32[]{:S(2)}) %collective-permute-start.3) | collective-permute-done | bytes 65568 | tf_op jit(solution)/shard_map/ppermute | solution.py:348
  34.9 0.0 collective-permute-done.4.refs_3_
  34.9 0.2 pick.1
  35.0 1.6 %collective-permute-start.11 = (f32[8,256]{1,0:T(8,128)S(1)}, f32[8,256]{1,0:T(8,128)S(1)}, u32[]{:S(2)}, u32[]{:S(2)}) collective-permute-start(f32[8,256]{1,0:T(8,128)S(1)} %get-tuple-element.29), channel_id=1, source_target_pairs={{0,2},{2,0},{1,3},{3,1},{4,6},{6,4},{5,7},{7,5},{8,10},{10,8},{9,1... | collective-permute-start | bytes 24584 | tf_op jit(solution)/shard_map/ppermute | solution.py:348
  36.6 1.2 %arrange.1 = bf16[8,4,4096]{2,1,0:T(4,128)(2,1)} custom-call(bf16[8,4096]{1,0:T(8,128)(2,1)S(1)} %get-tuple-element.22.refs_0_, bf16[8,4096]{1,0:T(8,128)(2,1)S(1)} %collective-permute-done.2.refs_1_, bf16[8,4096]{1,0:T(8,128)(2,1)S(1)} %collective-permute-done.3.refs_2_, bf16[8,4096]{1,0:T(8,128)(2,1)S(1)} %collective-permute-done.4.refs_3_), custom_call_target="tpu_custom_call" | custom-call | tf_op jit(solution)/shard_map/arrange/pallas_call | solution.py:320
  37.7 1.0 %collective-permute-done.11.refs_1_ = f32[8,256]{1,0:T(8,128)S(1)} collective-permute-done((f32[8,256]{1,0:T(8,128)S(1)}, f32[8,256]{1,0:T(8,128)S(1)}, u32[]{:S(2)}, u32[]{:S(2)}) %collective-permute-start.11) | collective-permute-done | bytes 8224 | tf_op jit(solution)/shard_map/ppermute | solution.py:348
  38.7 0.6 %finish.1 = bf16[8,2,128]{2,1,0:T(2,128)(2,1)} custom-call(f32[8,256]{1,0:T(8,128)S(1)} %get-tuple-element.28.refs_0_, f32[8,256]{1,0:T(8,128)S(1)} %collective-permute-done.11.refs_1_), custom_call_target="tpu_custom_call" | custom-call | tf_op jit(solution)/shard_map/finish/pallas_call | solution.py:340
  (3 shorter events, 0.1 us)
Async XLA Ops:
  5.0 9.3 %collective-permute-start = (bf16[8,8,2048]{2,1,0:T(8,128)(2,1)S(1)}, bf16[8,8,2048]{2,1,0:T(8,128)(2,1)S(1)}, u32[]{:S(2)}, u32[]{:S(2)}) collective-permute-start(bf16[8,8,2048]{2,1,0:T(8,128)(2,1)S(1)} %get-tuple-element.19), channel_id=1, source_target_pairs={{0,2},{2,0},{1,3},{3,1},{4,6},{6,4},{5,7},{7,5},{8,10},{10,8},{9,1... | collective-permute-start | bytes 786440 | tf_op jit(solution)/shard_map/ppermute | solution.py:348
  10.8 3.7 %copy-start = (s32[8,8192]{1,0:T(8,128)S(1)}, s32[8,8192]{1,0:T(8,128)}, u32[]{:S(2)}) copy-start(s32[8,8192]{1,0:T(8,128)} %refs_0_.1) | copy-start | bytes 786436
  14.4 15.2 %copy-start.1 = (bf16[8,256,64]{1,2,0:T(8,128)(2,1)S(1)}, bf16[8,256,64]{1,2,0:T(8,128)(2,1)}, u32[]{:S(2)}) copy-start(bf16[8,256,64]{1,2,0:T(8,128)(2,1)} %param.11) | copy-start | bytes 786436
  14.4 10.7 %collective-permute-start.1 = (bf16[4,8,2048]{2,1,0:T(8,128)(2,1)S(1)}, bf16[4,8,2048]{2,1,0:T(8,128)(2,1)S(1)}, u32[]{:S(2)}, u32[]{:S(2)}) collective-permute-start(bf16[4,8,2048]{2,1,0:T(8,128)(2,1)S(1)} %get-tuple-element.21), channel_id=1, source_target_pairs={{0,1},{1,0},{2,3},{3,2},{4,5},{5,4},{6,7},{7,6},{8,9},{9,8},{10,11... | collective-permute-start | bytes 393224 | tf_op jit(solution)/shard_map/ppermute | solution.py:348
  14.5 4.6 %collective-permute-start.5 = (bf16[8,4096]{1,0:T(8,128)(2,1)S(1)}, bf16[8,4096]{1,0:T(8,128)(2,1)S(1)}, u32[]{:S(2)}, u32[]{:S(2)}) collective-permute-start(bf16[8,4096]{1,0:T(8,128)(2,1)S(1)} %dynamic-slice_convert_fusion), channel_id=1, source_target_pairs={{0,4},{4,0},{8,12},{12,8},{1,5},{5,1},{9,13},{13,9},{2,6},{6,2},{1... | collective-permute-start | bytes 196616 | tf_op jit(solution)/shard_map/ppermute | solution.py:348
  16.4 7.0 %collective-permute-start.7 = (bf16[8,4096]{1,0:T(8,128)(2,1)S(1)}, bf16[8,4096]{1,0:T(8,128)(2,1)S(1)}, u32[]{:S(2)}, u32[]{:S(2)}) collective-permute-start(bf16[8,4096]{1,0:T(8,128)(2,1)S(1)} %dynamic-slice_convert_fusion), channel_id=1, source_target_pairs={{0,8},{4,12},{8,0},{12,4},{1,9},{5,13},{9,1},{13,5},{2,10},{6,14},... | collective-permute-start | bytes 196616 | tf_op jit(solution)/shard_map/ppermute | solution.py:348
  19.0 6.1 %collective-permute-start.9 = (bf16[8,4096]{1,0:T(8,128)(2,1)S(1)}, bf16[8,4096]{1,0:T(8,128)(2,1)S(1)}, u32[]{:S(2)}, u32[]{:S(2)}) collective-permute-start(bf16[8,4096]{1,0:T(8,128)(2,1)S(1)} %dynamic-slice_convert_fusion), channel_id=1, source_target_pairs={{0,12},{4,8},{8,4},{12,0},{1,13},{5,9},{9,5},{13,1},{2,14},{6,10},... | collective-permute-start | bytes 196616 | tf_op jit(solution)/shard_map/ppermute | solution.py:348
  19.1 9.5 %collective-permute-start.6 = (bf16[8,4096]{1,0:T(8,128)(2,1)S(1)}, bf16[8,4096]{1,0:T(8,128)(2,1)S(1)}, u32[]{:S(2)}, u32[]{:S(2)}) collective-permute-start(bf16[8,4096]{1,0:T(8,128)(2,1)S(1)} %collective-permute-done.5.refs_1_), channel_id=1, source_target_pairs={{0,1},{1,0},{2,3},{3,2},{4,5},{5,4},{6,7},{7,6},{8,9},{9,8},{10,11... | collective-permute-start | bytes 196616 | tf_op jit(solution)/shard_map/ppermute | solution.py:348
  23.4 6.2 %collective-permute-start.8 = (bf16[8,4096]{1,0:T(8,128)(2,1)S(1)}, bf16[8,4096]{1,0:T(8,128)(2,1)S(1)}, u32[]{:S(2)}, u32[]{:S(2)}) collective-permute-start(bf16[8,4096]{1,0:T(8,128)(2,1)S(1)} %collective-permute-done.7.refs_3_), channel_id=1, source_target_pairs={{0,1},{1,0},{2,3},{3,2},{4,5},{5,4},{6,7},{7,6},{8,9},{9,8},{10,11... | collective-permute-start | bytes 196616 | tf_op jit(solution)/shard_map/ppermute | solution.py:348
  25.1 4.5 %collective-permute-start.10 = (bf16[8,4096]{1,0:T(8,128)(2,1)S(1)}, bf16[8,4096]{1,0:T(8,128)(2,1)S(1)}, u32[]{:S(2)}, u32[]{:S(2)}) collective-permute-start(bf16[8,4096]{1,0:T(8,128)(2,1)S(1)} %collective-permute-done.9.refs_5_), channel_id=1, source_target_pairs={{0,1},{1,0},{2,3},{3,2},{4,5},{5,4},{6,7},{7,6},{8,9},{9,8},{10,11... | collective-permute-start | bytes 196616 | tf_op jit(solution)/shard_map/ppermute | solution.py:348
  25.1 4.5 %copy-start.2 = (bf16[8,512]{1,0:T(8,128)(2,1)S(1)}, bf16[8,512]{1,0:T(8,128)(2,1)}, u32[]{:S(2)}) copy-start(bf16[8,512]{1,0:T(8,128)(2,1)} %rerank_ref.1) | copy-start | bytes 24580
  25.1 5.8 %collective-permute-start.2 = (bf16[8,4096]{1,0:T(8,128)(2,1)S(1)}, bf16[8,4096]{1,0:T(8,128)(2,1)S(1)}, u32[]{:S(2)}, u32[]{:S(2)}) collective-permute-start(bf16[8,4096]{1,0:T(8,128)(2,1)S(1)} %get-tuple-element.23), channel_id=1, source_target_pairs={{0,4},{4,0},{8,12},{12,8},{1,5},{5,1},{9,13},{13,9},{2,6},{6,2},{1... | collective-permute-start | bytes 196616 | tf_op jit(solution)/shard_map/ppermute | solution.py:348
  26.4 8.4 %collective-permute-start.3 = (bf16[8,4096]{1,0:T(8,128)(2,1)S(1)}, bf16[8,4096]{1,0:T(8,128)(2,1)S(1)}, u32[]{:S(2)}, u32[]{:S(2)}) collective-permute-start(bf16[8,4096]{1,0:T(8,128)(2,1)S(1)} %get-tuple-element.24), channel_id=1, source_target_pairs={{0,8},{4,12},{8,0},{12,4},{1,9},{5,13},{9,1},{13,5},{2,10},{6,14},... | collective-permute-start | bytes 196616 | tf_op jit(solution)/shard_map/ppermute | solution.py:348
  28.7 6.2 %collective-permute-start.4 = (bf16[8,4096]{1,0:T(8,128)(2,1)S(1)}, bf16[8,4096]{1,0:T(8,128)(2,1)S(1)}, u32[]{:S(2)}, u32[]{:S(2)}) collective-permute-start(bf16[8,4096]{1,0:T(8,128)(2,1)S(1)} %get-tuple-element.25), channel_id=1, source_target_pairs={{0,12},{4,8},{8,4},{12,0},{1,13},{5,9},{9,5},{13,1},{2,14},{6,10},... | collective-permute-start | bytes 196616 | tf_op jit(solution)/shard_map/ppermute | solution.py:348
  35.0 3.7 %collective-permute-start.11 = (f32[8,256]{1,0:T(8,128)S(1)}, f32[8,256]{1,0:T(8,128)S(1)}, u32[]{:S(2)}, u32[]{:S(2)}) collective-permute-start(f32[8,256]{1,0:T(8,128)S(1)} %get-tuple-element.29), channel_id=1, source_target_pairs={{0,2},{2,0},{1,3},{3,1},{4,6},{6,4},{5,7},{7,5},{8,10},{10,8},{9,1... | collective-permute-start | bytes 24584 | tf_op jit(solution)/shard_map/ppermute | solution.py:348

commit v5 on v4

--- a/solution.py
+++ b/solution.py
@@ -55,27 +55,22 @@
 
 def coarse_kernel(halves, shifts, q_ref, book_ref, codes_ref, out_ref, *loads):
     tiles = out_ref.shape[2]
-    chunk = tiles // 4 if tiles % (8 * LANES) == 0 else tiles
-    waits, later = [], []
+    later = []
     if loads:
         q_load, book_load, *later_loads, codes_load, sems = loads
 
-        def quarter(shift, at, size):
+        pairs = [(book_ref, book_load), (q_ref, q_load)]
+        for shift, load in zip(shifts, (codes_load, *later_loads)):
             place = (lax.axis_index("sub") ^ shift) * halves + lax.axis_index("rep")
-            return codes_ref.at[:, pl.ds(pl.multiple_of(place * tiles + at, LANES), size)]
-
-        pairs = [(book_ref, book_load), (q_ref, q_load)]
-        for at in range(0, tiles, chunk):
-            pairs.append((quarter(shifts[0], at, chunk), codes_load.at[:, at : at + chunk]))
-        for shift, load in zip(shifts[1:], later_loads):
-            pairs.append((quarter(shift, 0, tiles), load))
+            start = pl.multiple_of(place * tiles, LANES)
+            pairs.append((codes_ref.at[:, pl.ds(start, tiles)], load))
         copies = [pltpu.make_async_copy(*pair, sems.at[i]) for i, pair in enumerate(pairs)]
         for copy in copies:
             copy.start()
         q_ref, book_ref, codes_ref = q_load, book_load, codes_load
-        for copy in copies[:2]:
+        for copy in copies[:3]:
             copy.wait()
-        waits, later = copies[2 : 2 + tiles // chunk], copies[2 + tiles // chunk :]
+        later = copies[3:]
     spaces, depth, _ = book_ref.shape
     own = out_ref.shape[1]
     holders = out_ref.shape[0] // halves
@@ -90,8 +85,6 @@
     ).astype(jnp.bfloat16)
     step = min(spaces, 256 // depth)
     for first in range(0, tiles, 2 * LANES):
-        if waits and first % chunk == 0:
-            waits.pop(0).wait()
         scores = None
         for low in range(0, spaces, step):
             decoded = jnp.concatenate(
@@ -138,7 +131,7 @@
             pltpu.VMEM(book.shape, book.dtype),
         ]
         + [load] * (len(shifts) - 1),
-        scratch_shapes=[load, pltpu.SemaphoreType.DMA((5 + len(shifts),))],
+        scratch_shapes=[load, pltpu.SemaphoreType.DMA((2 + len(shifts),))],
         name="coarse_first",
     )(queries, book, codes)
     return score, queries, book, rest

time: 39.5 us -> 39 us (0.987)
  Pallas kernels: 10.4 us -> 9.94 us
    pallas_call x1, Pallas kernels: 4.37 us -> 3.86 us  [coarse_first(): pl.pallas_call(partial(coarse_kernel, halves, shifts), in_specs=[pl.Block...]
  transfers between devices with their start and end apart: 12 -> 12, of which waited for: 6 -> 6; matrix products, arithmetic and copies ran while one was open for 0% -> 0% of each run, Pallas kernels for 13% -> 14%
where the time goes in v5:
time: 39 us; the launch traced here: 38.8 us
  waiting for transfers between devices  14.5 us (37%)
  starting transfers between devices  13.6 us (35%)
  Pallas kernels  9.94 us (25%)
  between operations  0.75 us (2%)
    ppermute x12, waiting for transfers between devices, swap(): lax.ppermute(value, axis, [(i, i ^ shift) for i in range(lax.axis_size(ax...  14.5 us
    ppermute x12, starting transfers between devices, swap(): lax.ppermute(value, axis, [(i, i ^ shift) for i in range(lax.axis_size(ax...  13.6 us
    pallas_call x1, Pallas kernels, coarse_first(): pl.pallas_call(partial(coarse_kernel, halves, shifts), in_specs=[pl.Block...  3.86 us
    pallas_call x1, Pallas kernels, coarse_next(): pl.pallas_call(partial(coarse_kernel, halves, (shift,)), in_specs=[vmem]...  2.76 us
    pallas_call x1, Pallas kernels, refine_partials(): pl.pallas_call(partial(refine_kernel, holders, subs), in_specs=[smem, sme...  1.32 us
    pallas_call x1, Pallas kernels, arrange(): pl.pallas_call(arrange_kernel, out_shape=jax.ShapeDtypeStruct((own, holde...  1.18 us
  transfers between devices with their start and end apart: 12, of which 6 were waited for; matrix products, arithmetic and copies ran while one was open for 0% of the time, Pallas kernels for 14%

profile of v5, /device:TPU:0, one launch (start us, length us, event | category | flops | bytes accessed | tf_op | source)
XLA Modules:
  0.0 38.8 jit_solution(520253575483961573)
XLA Ops:
  0.6 3.9 %coarse_first.1 = (bf16[8,8,2048]{2,1,0:T(8,128)(2,1)S(1)}, bf16[8,8,512]{2,1,0:T(8,128)(2,1)S(1)}, bf16[32,16,256]{2,1,0:T(8,128)(2,1)S(1)}, s32[32,2048]{1,0:T(8,128)S(1)}) custom-call(bf16[8,8,512]{2,1,0:T(8,128)(2,1)} %bitcast.8, bf16[32,16,256]{2,1,0:T(8,128)(2,1)} %bitcast.7, s32[32,8192]{1,0:T(8,128)} %codes_ref.1), custom_call_target="tpu_custom_call" | custom-call | tf_op jit(solution)/shard_map/coarse_first/pallas_call | solution.py:124
  4.5 3.0 %collective-permute-start = (bf16[8,8,2048]{2,1,0:T(8,128)(2,1)S(1)}, bf16[8,8,2048]{2,1,0:T(8,128)(2,1)S(1)}, u32[]{:S(2)}, u32[]{:S(2)}) collective-permute-start(bf16[8,8,2048]{2,1,0:T(8,128)(2,1)S(1)} %get-tuple-element.19), channel_id=1, source_target_pairs={{0,2},{2,0},{1,3},{3,1},{4,6},{6,4},{5,7},{7,5},{8,10},{10,8},{9,1... | collective-permute-start | bytes 786440 | tf_op jit(solution)/shard_map/ppermute | solution.py:341
  7.5 2.8 %shard_map.95.refs_0_ = f32[8,8,2048]{2,1,0:T(8,128)S(1)} custom-call(bf16[8,8,512]{2,1,0:T(8,128)(2,1)S(1)} %get-tuple-element.16.q_ref, bf16[32,16,256]{2,1,0:T(8,128)(2,1)S(1)} %get-tuple-element.17.book_ref, s32[32,2048]{1,0:T(8,128)S(1)} %get-tuple-element.18.codes_ref), custom_call_target="tpu_custom_call" | custom-call | tf_op jit(solution)/shard_map/pallas_call | solution.py:143
  10.3 0.0 copy-start
  10.3 3.5 %collective-permute-done.refs_1_ = bf16[8,8,2048]{2,1,0:T(8,128)(2,1)S(1)} collective-permute-done((bf16[8,8,2048]{2,1,0:T(8,128)(2,1)S(1)}, bf16[8,8,2048]{2,1,0:T(8,128)(2,1)S(1)}, u32[]{:S(2)}, u32[]{:S(2)}) %collective-permute-start) | collective-permute-done | bytes 262176 | tf_op jit(solution)/shard_map/ppermute | solution.py:341
  13.9 0.0 copy-start.1
  13.9 0.1 collective-permute-start.1
  14.0 0.0 copy-done
  14.0 1.9 %collective-permute-start.5 = (bf16[8,4096]{1,0:T(8,128)(2,1)S(1)}, bf16[8,4096]{1,0:T(8,128)(2,1)S(1)}, u32[]{:S(2)}, u32[]{:S(2)}) collective-permute-start(bf16[8,4096]{1,0:T(8,128)(2,1)S(1)} %dynamic-slice_convert_fusion), channel_id=1, source_target_pairs={{0,4},{4,0},{8,12},{12,8},{1,5},{5,1},{9,13},{13,9},{2,6},{6,2},{1... | collective-permute-start | bytes 196616 | tf_op jit(solution)/shard_map/ppermute | solution.py:341
  15.9 2.6 %collective-permute-start.7 = (bf16[8,4096]{1,0:T(8,128)(2,1)S(1)}, bf16[8,4096]{1,0:T(8,128)(2,1)S(1)}, u32[]{:S(2)}, u32[]{:S(2)}) collective-permute-start(bf16[8,4096]{1,0:T(8,128)(2,1)S(1)} %dynamic-slice_convert_fusion), channel_id=1, source_target_pairs={{0,8},{4,12},{8,0},{12,4},{1,9},{5,13},{9,1},{13,5},{2,10},{6,14},... | collective-permute-start | bytes 196616 | tf_op jit(solution)/shard_map/ppermute | solution.py:341
  18.5 0.0 collective-permute-start.9
  18.5 0.1 collective-permute-done.5.refs_1_
  18.6 0.0 collective-permute-start.6
  18.6 4.3 %collective-permute-done.7.refs_3_ = bf16[8,4096]{1,0:T(8,128)(2,1)S(1)} collective-permute-done((bf16[8,4096]{1,0:T(8,128)(2,1)S(1)}, bf16[8,4096]{1,0:T(8,128)(2,1)S(1)}, u32[]{:S(2)}, u32[]{:S(2)}) %collective-permute-start.7) | collective-permute-done | bytes 65568 | tf_op jit(solution)/shard_map/ppermute | solution.py:341
  22.9 0.0 collective-permute-start.8
  22.9 1.7 %collective-permute-done.9.refs_5_ = bf16[8,4096]{1,0:T(8,128)(2,1)S(1)} collective-permute-done((bf16[8,4096]{1,0:T(8,128)(2,1)S(1)}, bf16[8,4096]{1,0:T(8,128)(2,1)S(1)}, u32[]{:S(2)}, u32[]{:S(2)}) %collective-permute-start.9) | collective-permute-done | bytes 65568 | tf_op jit(solution)/shard_map/ppermute | solution.py:341
  24.6 0.0 collective-permute-start.10
  24.6 0.0 collective-permute-done.1.refs_1_
  24.6 0.0 copy-start.2
  24.6 1.3 %collective-permute-start.2 = (bf16[8,4096]{1,0:T(8,128)(2,1)S(1)}, bf16[8,4096]{1,0:T(8,128)(2,1)S(1)}, u32[]{:S(2)}, u32[]{:S(2)}) collective-permute-start(bf16[8,4096]{1,0:T(8,128)(2,1)S(1)} %get-tuple-element.23), channel_id=1, source_target_pairs={{0,4},{4,0},{8,12},{12,8},{1,5},{5,1},{9,13},{13,9},{2,6},{6,2},{1... | collective-permute-start | bytes 196616 | tf_op jit(solution)/shard_map/ppermute | solution.py:341
  25.9 2.2 %collective-permute-start.3 = (bf16[8,4096]{1,0:T(8,128)(2,1)S(1)}, bf16[8,4096]{1,0:T(8,128)(2,1)S(1)}, u32[]{:S(2)}, u32[]{:S(2)}) collective-permute-start(bf16[8,4096]{1,0:T(8,128)(2,1)S(1)} %get-tuple-element.24), channel_id=1, source_target_pairs={{0,8},{4,12},{8,0},{12,4},{1,9},{5,13},{9,1},{13,5},{2,10},{6,14},... | collective-permute-start | bytes 196616 | tf_op jit(solution)/shard_map/ppermute | solution.py:341
  28.2 0.0 collective-permute-done.6.refs_2_
  28.2 0.9 %collective-permute-start.4 = (bf16[8,4096]{1,0:T(8,128)(2,1)S(1)}, bf16[8,4096]{1,0:T(8,128)(2,1)S(1)}, u32[]{:S(2)}, u32[]{:S(2)}) collective-permute-start(bf16[8,4096]{1,0:T(8,128)(2,1)S(1)} %get-tuple-element.25), channel_id=1, source_target_pairs={{0,12},{4,8},{8,4},{12,0},{1,13},{5,9},{9,5},{13,1},{2,14},{6,10},... | collective-permute-start | bytes 196616 | tf_op jit(solution)/shard_map/ppermute | solution.py:341
  29.1 0.0 collective-permute-done.8.refs_4_
  29.1 0.0 collective-permute-done.10.refs_6_
  29.1 0.0 copy-done.1
  29.1 0.0 copy-done.2
  29.1 1.3 %refine.1 = (f32[8,512]{1,0:T(8,128)S(1)}, s32[8,512]{1,0:T(8,128)S(1)}) custom-call(s32[256]{0:T(256)} %place_ref.1, s32[4,8]{1,0:T(4,128)} %bitcast.9, bf16[8,512]{1,0:T(8,128)(2,1)S(1)} %copy-done.2, bf16[512,256]{1,0:T(8,128)(2,1)S(1)} %bitcast.6, s32[8,8192]{1,0:T(8,128)S(1)} %copy-done, bf16[8,4096]{1,0:T(8,128)(2,1)S(1)} %collective-permute-done.5.refs_1_, ...), custom_call_target="tpu_custom_call" | custom-call | tf_op jit(solution)/shard_map/refine/pallas_call | solution.py:204
  30.4 0.0 collective-permute-done.2.refs_1_
  30.4 3.9 %collective-permute-done.3.refs_2_ = bf16[8,4096]{1,0:T(8,128)(2,1)S(1)} collective-permute-done((bf16[8,4096]{1,0:T(8,128)(2,1)S(1)}, bf16[8,4096]{1,0:T(8,128)(2,1)S(1)}, u32[]{:S(2)}, u32[]{:S(2)}) %collective-permute-start.3) | collective-permute-done | bytes 65568 | tf_op jit(solution)/shard_map/ppermute | solution.py:341
  34.4 0.0 collective-permute-done.4.refs_3_
  34.4 0.2 pick.1
  34.5 1.6 %collective-permute-start.11 = (f32[8,256]{1,0:T(8,128)S(1)}, f32[8,256]{1,0:T(8,128)S(1)}, u32[]{:S(2)}, u32[]{:S(2)}) collective-permute-start(f32[8,256]{1,0:T(8,128)S(1)} %get-tuple-element.29), channel_id=1, source_target_pairs={{0,2},{2,0},{1,3},{3,1},{4,6},{6,4},{5,7},{7,5},{8,10},{10,8},{9,1... | collective-permute-start | bytes 24584 | tf_op jit(solution)/shard_map/ppermute | solution.py:341
  36.1 1.2 %arrange.1 = bf16[8,4,4096]{2,1,0:T(4,128)(2,1)} custom-call(bf16[8,4096]{1,0:T(8,128)(2,1)S(1)} %get-tuple-element.22.refs_0_, bf16[8,4096]{1,0:T(8,128)(2,1)S(1)} %collective-permute-done.2.refs_1_, bf16[8,4096]{1,0:T(8,128)(2,1)S(1)} %collective-permute-done.3.refs_2_, bf16[8,4096]{1,0:T(8,128)(2,1)S(1)} %collective-permute-done.4.refs_3_), custom_call_target="tpu_custom_call" | custom-call | tf_op jit(solution)/shard_map/arrange/pallas_call | solution.py:313
  37.2 1.0 %collective-permute-done.11.refs_1_ = f32[8,256]{1,0:T(8,128)S(1)} collective-permute-done((f32[8,256]{1,0:T(8,128)S(1)}, f32[8,256]{1,0:T(8,128)S(1)}, u32[]{:S(2)}, u32[]{:S(2)}) %collective-permute-start.11) | collective-permute-done | bytes 8224 | tf_op jit(solution)/shard_map/ppermute | solution.py:341
  38.2 0.6 %finish.1 = bf16[8,2,128]{2,1,0:T(2,128)(2,1)} custom-call(f32[8,256]{1,0:T(8,128)S(1)} %get-tuple-element.28.refs_0_, f32[8,256]{1,0:T(8,128)S(1)} %collective-permute-done.11.refs_1_), custom_call_target="tpu_custom_call" | custom-call | tf_op jit(solution)/shard_map/finish/pallas_call | solution.py:333
  (3 shorter events, 0.1 us)
Async XLA Ops:
  4.5 9.3 %collective-permute-start = (bf16[8,8,2048]{2,1,0:T(8,128)(2,1)S(1)}, bf16[8,8,2048]{2,1,0:T(8,128)(2,1)S(1)}, u32[]{:S(2)}, u32[]{:S(2)}) collective-permute-start(bf16[8,8,2048]{2,1,0:T(8,128)(2,1)S(1)} %get-tuple-element.19), channel_id=1, source_target_pairs={{0,2},{2,0},{1,3},{3,1},{4,6},{6,4},{5,7},{7,5},{8,10},{10,8},{9,1... | collective-permute-start | bytes 786440 | tf_op jit(solution)/shard_map/ppermute | solution.py:341
  10.3 3.7 %copy-start = (s32[8,8192]{1,0:T(8,128)S(1)}, s32[8,8192]{1,0:T(8,128)}, u32[]{:S(2)}) copy-start(s32[8,8192]{1,0:T(8,128)} %refs_0_.1) | copy-start | bytes 786436
  13.9 15.2 %copy-start.1 = (bf16[8,256,64]{1,2,0:T(8,128)(2,1)S(1)}, bf16[8,256,64]{1,2,0:T(8,128)(2,1)}, u32[]{:S(2)}) copy-start(bf16[8,256,64]{1,2,0:T(8,128)(2,1)} %param.11) | copy-start | bytes 786436
  13.9 10.7 %collective-permute-start.1 = (bf16[4,8,2048]{2,1,0:T(8,128)(2,1)S(1)}, bf16[4,8,2048]{2,1,0:T(8,128)(2,1)S(1)}, u32[]{:S(2)}, u32[]{:S(2)}) collective-permute-start(bf16[4,8,2048]{2,1,0:T(8,128)(2,1)S(1)} %get-tuple-element.21), channel_id=1, source_target_pairs={{0,1},{1,0},{2,3},{3,2},{4,5},{5,4},{6,7},{7,6},{8,9},{9,8},{10,11... | collective-permute-start | bytes 393224 | tf_op jit(solution)/shard_map/ppermute | solution.py:341
  14.0 4.6 %collective-permute-start.5 = (bf16[8,4096]{1,0:T(8,128)(2,1)S(1)}, bf16[8,4096]{1,0:T(8,128)(2,1)S(1)}, u32[]{:S(2)}, u32[]{:S(2)}) collective-permute-start(bf16[8,4096]{1,0:T(8,128)(2,1)S(1)} %dynamic-slice_convert_fusion), channel_id=1, source_target_pairs={{0,4},{4,0},{8,12},{12,8},{1,5},{5,1},{9,13},{13,9},{2,6},{6,2},{1... | collective-permute-start | bytes 196616 | tf_op jit(solution)/shard_map/ppermute | solution.py:341
  15.9 7.0 %collective-permute-start.7 = (bf16[8,4096]{1,0:T(8,128)(2,1)S(1)}, bf16[8,4096]{1,0:T(8,128)(2,1)S(1)}, u32[]{:S(2)}, u32[]{:S(2)}) collective-permute-start(bf16[8,4096]{1,0:T(8,128)(2,1)S(1)} %dynamic-slice_convert_fusion), channel_id=1, source_target_pairs={{0,8},{4,12},{8,0},{12,4},{1,9},{5,13},{9,1},{13,5},{2,10},{6,14},... | collective-permute-start | bytes 196616 | tf_op jit(solution)/shard_map/ppermute | solution.py:341
  18.5 6.1 %collective-permute-start.9 = (bf16[8,4096]{1,0:T(8,128)(2,1)S(1)}, bf16[8,4096]{1,0:T(8,128)(2,1)S(1)}, u32[]{:S(2)}, u32[]{:S(2)}) collective-permute-start(bf16[8,4096]{1,0:T(8,128)(2,1)S(1)} %dynamic-slice_convert_fusion), channel_id=1, source_target_pairs={{0,12},{4,8},{8,4},{12,0},{1,13},{5,9},{9,5},{13,1},{2,14},{6,10},... | collective-permute-start | bytes 196616 | tf_op jit(solution)/shard_map/ppermute | solution.py:341
  18.6 9.5 %collective-permute-start.6 = (bf16[8,4096]{1,0:T(8,128)(2,1)S(1)}, bf16[8,4096]{1,0:T(8,128)(2,1)S(1)}, u32[]{:S(2)}, u32[]{:S(2)}) collective-permute-start(bf16[8,4096]{1,0:T(8,128)(2,1)S(1)} %collective-permute-done.5.refs_1_), channel_id=1, source_target_pairs={{0,1},{1,0},{2,3},{3,2},{4,5},{5,4},{6,7},{7,6},{8,9},{9,8},{10,11... | collective-permute-start | bytes 196616 | tf_op jit(solution)/shard_map/ppermute | solution.py:341
  22.9 6.2 %collective-permute-start.8 = (bf16[8,4096]{1,0:T(8,128)(2,1)S(1)}, bf16[8,4096]{1,0:T(8,128)(2,1)S(1)}, u32[]{:S(2)}, u32[]{:S(2)}) collective-permute-start(bf16[8,4096]{1,0:T(8,128)(2,1)S(1)} %collective-permute-done.7.refs_3_), channel_id=1, source_target_pairs={{0,1},{1,0},{2,3},{3,2},{4,5},{5,4},{6,7},{7,6},{8,9},{9,8},{10,11... | collective-permute-start | bytes 196616 | tf_op jit(solution)/shard_map/ppermute | solution.py:341
  24.6 4.5 %collective-permute-start.10 = (bf16[8,4096]{1,0:T(8,128)(2,1)S(1)}, bf16[8,4096]{1,0:T(8,128)(2,1)S(1)}, u32[]{:S(2)}, u32[]{:S(2)}) collective-permute-start(bf16[8,4096]{1,0:T(8,128)(2,1)S(1)} %collective-permute-done.9.refs_5_), channel_id=1, source_target_pairs={{0,1},{1,0},{2,3},{3,2},{4,5},{5,4},{6,7},{7,6},{8,9},{9,8},{10,11... | collective-permute-start | bytes 196616 | tf_op jit(solution)/shard_map/ppermute | solution.py:341
  24.6 4.5 %copy-start.2 = (bf16[8,512]{1,0:T(8,128)(2,1)S(1)}, bf16[8,512]{1,0:T(8,128)(2,1)}, u32[]{:S(2)}) copy-start(bf16[8,512]{1,0:T(8,128)(2,1)} %rerank_ref.1) | copy-start | bytes 24580
  24.6 5.8 %collective-permute-start.2 = (bf16[8,4096]{1,0:T(8,128)(2,1)S(1)}, bf16[8,4096]{1,0:T(8,128)(2,1)S(1)}, u32[]{:S(2)}, u32[]{:S(2)}) collective-permute-start(bf16[8,4096]{1,0:T(8,128)(2,1)S(1)} %get-tuple-element.23), channel_id=1, source_target_pairs={{0,4},{4,0},{8,12},{12,8},{1,5},{5,1},{9,13},{13,9},{2,6},{6,2},{1... | collective-permute-start | bytes 196616 | tf_op jit(solution)/shard_map/ppermute | solution.py:341
  25.9 8.4 %collective-permute-start.3 = (bf16[8,4096]{1,0:T(8,128)(2,1)S(1)}, bf16[8,4096]{1,0:T(8,128)(2,1)S(1)}, u32[]{:S(2)}, u32[]{:S(2)}) collective-permute-start(bf16[8,4096]{1,0:T(8,128)(2,1)S(1)} %get-tuple-element.24), channel_id=1, source_target_pairs={{0,8},{4,12},{8,0},{12,4},{1,9},{5,13},{9,1},{13,5},{2,10},{6,14},... | collective-permute-start | bytes 196616 | tf_op jit(solution)/shard_map/ppermute | solution.py:341
  28.2 6.2 %collective-permute-start.4 = (bf16[8,4096]{1,0:T(8,128)(2,1)S(1)}, bf16[8,4096]{1,0:T(8,128)(2,1)S(1)}, u32[]{:S(2)}, u32[]{:S(2)}) collective-permute-start(bf16[8,4096]{1,0:T(8,128)(2,1)S(1)} %get-tuple-element.25), channel_id=1, source_target_pairs={{0,12},{4,8},{8,4},{12,0},{1,13},{5,9},{9,5},{13,1},{2,14},{6,10},... | collective-permute-start | bytes 196616 | tf_op jit(solution)/shard_map/ppermute | solution.py:341
  34.5 3.7 %collective-permute-start.11 = (f32[8,256]{1,0:T(8,128)S(1)}, f32[8,256]{1,0:T(8,128)S(1)}, u32[]{:S(2)}, u32[]{:S(2)}) collective-permute-start(f32[8,256]{1,0:T(8,128)S(1)} %get-tuple-element.29), channel_id=1, source_target_pairs={{0,2},{2,0},{1,3},{3,1},{4,6},{6,4},{5,7},{7,5},{8,10},{10,8},{9,1... | collective-permute-start | bytes 24584 | tf_op jit(solution)/shard_map/ppermute | solution.py:341

commit v6 on v5

--- a/solution.py
+++ b/solution.py
@@ -53,24 +53,28 @@
     return found
 
 
-def coarse_kernel(halves, shifts, q_ref, book_ref, codes_ref, out_ref, *loads):
+def coarse_kernel(halves, shifts, q_ref, book_ref, codes_ref, *refs):
+    first = len(refs) > 1
+    out_ref, *loads = refs[1:] if first else refs
     tiles = out_ref.shape[2]
     later = []
-    if loads:
-        q_load, book_load, *later_loads, codes_load, sems = loads
-
+    if first:
+        q_load, book_load, fine_load, *later_loads, codes_load, sems = loads
         pairs = [(book_ref, book_load), (q_ref, q_load)]
         for shift, load in zip(shifts, (codes_load, *later_loads)):
             place = (lax.axis_index("sub") ^ shift) * halves + lax.axis_index("rep")
             start = pl.multiple_of(place * tiles, LANES)
             pairs.append((codes_ref.at[:, pl.ds(start, tiles)], load))
+        pairs.append((refs[0], fine_load))
         copies = [pltpu.make_async_copy(*pair, sems.at[i]) for i, pair in enumerate(pairs)]
-        for copy in copies:
+        now, later = copies[:3], copies[3:]
+        for copy in now:
             copy.start()
         q_ref, book_ref, codes_ref = q_load, book_load, codes_load
-        for copy in copies[:3]:
+        for copy in now:
             copy.wait()
-        later = copies[3:]
+        for copy in later:
+            copy.start()
     spaces, depth, _ = book_ref.shape
     own = out_ref.shape[1]
     holders = out_ref.shape[0] // halves
@@ -110,31 +114,30 @@
             out_ref[h, :, first : first + 2 * LANES] = scores[h * own : (h + 1) * own].astype(
                 out_ref.dtype
             )
-
-
     for copy in later:
         copy.wait()
 
 
-def coarse_first(shifts, subs, halves, holders, own, queries, book, codes):
+def coarse_first(shifts, subs, halves, holders, own, queries, book, codes, fine_codes):
     spaces, stored = codes.shape
     quarter = stored // subs // halves
     kind = jnp.bfloat16 if shifts[0] else jnp.float32
     load = pltpu.VMEM((spaces, quarter), codes.dtype)
-    score, queries, book, *rest = pl.pallas_call(
+    score, queries, book, fine_codes, *rest = pl.pallas_call(
         partial(coarse_kernel, halves, shifts),
-        in_specs=[pl.BlockSpec(memory_space=pl.ANY)] * 3,
-        out_specs=[pl.BlockSpec(memory_space=pltpu.VMEM)] * (2 + len(shifts)),
+        in_specs=[pl.BlockSpec(memory_space=pl.ANY)] * 4,
+        out_specs=[pl.BlockSpec(memory_space=pltpu.VMEM)] * (3 + len(shifts)),
         out_shape=[
             pltpu.VMEM((halves * holders, own, quarter), kind),
             pltpu.VMEM(queries.shape, queries.dtype),
             pltpu.VMEM(book.shape, book.dtype),
+            pltpu.VMEM(fine_codes.shape, fine_codes.dtype),
         ]
         + [load] * (len(shifts) - 1),
-        scratch_shapes=[load, pltpu.SemaphoreType.DMA((2 + len(shifts),))],
+        scratch_shapes=[load, pltpu.SemaphoreType.DMA((3 + len(shifts),))],
         name="coarse_first",
-    )(queries, book, codes)
-    return score, queries, book, rest
+    )(queries, book, codes, fine_codes)
+    return score, queries, book, fine_codes, rest
 
 
 def coarse_next(shift, halves, holders, own, queries, book, codes):
@@ -359,8 +362,8 @@
     book = jnp.swapaxes(coarse_book, 1, 2)
     fine_book = jnp.swapaxes(refine_book, 1, 2).reshape(features, refine_book.shape[1])
     shifts = [*range(1, subs), 0]
-    score, rows, book, rest = coarse_first(
-        shifts, subs, halves, holders, own, rows, book, coarse_codes
+    score, rows, book, refine_codes, rest = coarse_first(
+        shifts, subs, halves, holders, own, rows, book, coarse_codes, refine_codes
     )
     sums = []
     for at, shift in enumerate(shifts):

time: 39 us -> 38.3 us (0.982)
  waiting for transfers between devices: 14.5 us -> 13.6 us
    ppermute x12, waiting for transfers between devices: 14.5 us -> 13.6 us  [swap(): lax.ppermute(value, axis, [(i, i ^ shift) for i in range(lax.axis_size(ax...]
where the time goes in v6:
time: 38.3 us; the launch traced here: 38.1 us
  starting transfers between devices  13.8 us (36%)
  waiting for transfers between devices  13.6 us (36%)
  Pallas kernels  9.95 us (26%)
  between operations  0.73 us (2%)
    ppermute x12, starting transfers between devices, swap(): lax.ppermute(value, axis, [(i, i ^ shift) for i in range(lax.axis_size(ax...  13.8 us
    ppermute x12, waiting for transfers between devices, swap(): lax.ppermute(value, axis, [(i, i ^ shift) for i in range(lax.axis_size(ax...  13.6 us
    pallas_call x1, Pallas kernels, coarse_first(): pl.pallas_call(partial(coarse_kernel, halves, shifts), in_specs=[pl.Block...  3.87 us
    pallas_call x1, Pallas kernels, coarse_next(): pl.pallas_call(partial(coarse_kernel, halves, (shift,)), in_specs=[vmem]...  2.76 us
    pallas_call x1, Pallas kernels, refine_partials(): pl.pallas_call(partial(refine_kernel, holders, subs), in_specs=[smem, sme...  1.32 us
    pallas_call x1, Pallas kernels, arrange(): pl.pallas_call(arrange_kernel, out_shape=jax.ShapeDtypeStruct((own, holde...  1.18 us
  transfers between devices with their start and end apart: 12, of which 6 were waited for; matrix products, arithmetic and copies ran while one was open for 0% of the time, Pallas kernels for 14%

profile of v6, /device:TPU:0, one launch (start us, length us, event | category | flops | bytes accessed | tf_op | source)
XLA Modules:
  0.0 38.1 jit_solution(17543753818042809786)
XLA Ops:
  0.6 3.9 %coarse_first.1 = (bf16[8,8,2048]{2,1,0:T(8,128)(2,1)S(1)}, bf16[8,8,512]{2,1,0:T(8,128)(2,1)S(1)}, bf16[32,16,256]{2,1,0:T(8,128)(2,1)S(1)}, s32[8,8192]{1,0:T(8,128)S(1)}, s32[32,2048]{1,0:T(8,128)S(1)}) custom-call(bf16[8,8,512]{2,1,0:T(8,128)(2,1)} %bitcast.8, bf16[32,16,256]{2,1,0:T(8,128)(2,1)} %bitcast.7, s32[32,8192]{1,0:T(8,128)} %codes_ref.1, ...), custom_call_target="tpu_custom_call" | custom-call | tf_op jit(solution)/shard_map/coarse_first/pallas_call | solution.py:126
  4.5 3.0 %collective-permute-start = (bf16[8,8,2048]{2,1,0:T(8,128)(2,1)S(1)}, bf16[8,8,2048]{2,1,0:T(8,128)(2,1)S(1)}, u32[]{:S(2)}, u32[]{:S(2)}) collective-permute-start(bf16[8,8,2048]{2,1,0:T(8,128)(2,1)S(1)} %get-tuple-element.20), channel_id=1, source_target_pairs={{0,2},{2,0},{1,3},{3,1},{4,6},{6,4},{5,7},{7,5},{8,10},{10,8},{9,1... | collective-permute-start | bytes 786440 | tf_op jit(solution)/shard_map/ppermute | solution.py:344
  7.5 2.8 %shard_map.95.refs_0_ = f32[8,8,2048]{2,1,0:T(8,128)S(1)} custom-call(bf16[8,8,512]{2,1,0:T(8,128)(2,1)S(1)} %get-tuple-element.17.q_ref, bf16[32,16,256]{2,1,0:T(8,128)(2,1)S(1)} %get-tuple-element.18.book_ref, s32[32,2048]{1,0:T(8,128)S(1)} %get-tuple-element.19.codes_ref), custom_call_target="tpu_custom_call" | custom-call | tf_op jit(solution)/shard_map/pallas_call | solution.py:146
  10.3 3.5 %collective-permute-done.refs_1_ = bf16[8,8,2048]{2,1,0:T(8,128)(2,1)S(1)} collective-permute-done((bf16[8,8,2048]{2,1,0:T(8,128)(2,1)S(1)}, bf16[8,8,2048]{2,1,0:T(8,128)(2,1)S(1)}, u32[]{:S(2)}, u32[]{:S(2)}) %collective-permute-start) | collective-permute-done | bytes 262176 | tf_op jit(solution)/shard_map/ppermute | solution.py:344
  13.9 0.0 copy-start
  13.9 0.1 collective-permute-start.1
  14.0 3.9 %collective-permute-start.9 = (bf16[8,4096]{1,0:T(8,128)(2,1)S(1)}, bf16[8,4096]{1,0:T(8,128)(2,1)S(1)}, u32[]{:S(2)}, u32[]{:S(2)}) collective-permute-start(bf16[8,4096]{1,0:T(8,128)(2,1)S(1)} %dynamic-slice_convert_fusion), channel_id=1, source_target_pairs={{0,12},{4,8},{8,4},{12,0},{1,13},{5,9},{9,5},{13,1},{2,14},{6,10},... | collective-permute-start | bytes 196616 | tf_op jit(solution)/shard_map/ppermute | solution.py:344
  17.9 0.0 collective-permute-start.5
  17.9 0.6 %collective-permute-start.7 = (bf16[8,4096]{1,0:T(8,128)(2,1)S(1)}, bf16[8,4096]{1,0:T(8,128)(2,1)S(1)}, u32[]{:S(2)}, u32[]{:S(2)}) collective-permute-start(bf16[8,4096]{1,0:T(8,128)(2,1)S(1)} %dynamic-slice_convert_fusion), channel_id=1, source_target_pairs={{0,8},{4,12},{8,0},{12,4},{1,9},{5,13},{9,1},{13,5},{2,10},{6,14},... | collective-permute-start | bytes 196616 | tf_op jit(solution)/shard_map/ppermute | solution.py:344
  18.6 2.4 %collective-permute-done.9.refs_5_ = bf16[8,4096]{1,0:T(8,128)(2,1)S(1)} collective-permute-done((bf16[8,4096]{1,0:T(8,128)(2,1)S(1)}, bf16[8,4096]{1,0:T(8,128)(2,1)S(1)}, u32[]{:S(2)}, u32[]{:S(2)}) %collective-permute-start.9) | collective-permute-done | bytes 65568 | tf_op jit(solution)/shard_map/ppermute | solution.py:344
  20.9 0.0 collective-permute-start.10
  20.9 2.5 %collective-permute-done.5.refs_1_ = bf16[8,4096]{1,0:T(8,128)(2,1)S(1)} collective-permute-done((bf16[8,4096]{1,0:T(8,128)(2,1)S(1)}, bf16[8,4096]{1,0:T(8,128)(2,1)S(1)}, u32[]{:S(2)}, u32[]{:S(2)}) %collective-permute-start.5) | collective-permute-done | bytes 65568 | tf_op jit(solution)/shard_map/ppermute | solution.py:344
  23.5 0.0 collective-permute-start.6
  23.5 0.3 collective-permute-done.7.refs_3_
  23.8 0.2 collective-permute-start.8
  24.0 0.0 collective-permute-done.1.refs_1_
  24.0 0.0 copy-start.1
  24.0 1.2 %collective-permute-start.2 = (bf16[8,4096]{1,0:T(8,128)(2,1)S(1)}, bf16[8,4096]{1,0:T(8,128)(2,1)S(1)}, u32[]{:S(2)}, u32[]{:S(2)}) collective-permute-start(bf16[8,4096]{1,0:T(8,128)(2,1)S(1)} %get-tuple-element.24), channel_id=1, source_target_pairs={{0,4},{4,0},{8,12},{12,8},{1,5},{5,1},{9,13},{13,9},{2,6},{6,2},{1... | collective-permute-start | bytes 196616 | tf_op jit(solution)/shard_map/ppermute | solution.py:344
  25.2 1.5 %collective-permute-start.3 = (bf16[8,4096]{1,0:T(8,128)(2,1)S(1)}, bf16[8,4096]{1,0:T(8,128)(2,1)S(1)}, u32[]{:S(2)}, u32[]{:S(2)}) collective-permute-start(bf16[8,4096]{1,0:T(8,128)(2,1)S(1)} %get-tuple-element.25), channel_id=1, source_target_pairs={{0,8},{4,12},{8,0},{12,4},{1,9},{5,13},{9,1},{13,5},{2,10},{6,14},... | collective-permute-start | bytes 196616 | tf_op jit(solution)/shard_map/ppermute | solution.py:344
  26.8 0.0 collective-permute-done.10.refs_6_
  26.8 1.7 %collective-permute-start.4 = (bf16[8,4096]{1,0:T(8,128)(2,1)S(1)}, bf16[8,4096]{1,0:T(8,128)(2,1)S(1)}, u32[]{:S(2)}, u32[]{:S(2)}) collective-permute-start(bf16[8,4096]{1,0:T(8,128)(2,1)S(1)} %get-tuple-element.26), channel_id=1, source_target_pairs={{0,12},{4,8},{8,4},{12,0},{1,13},{5,9},{9,5},{13,1},{2,14},{6,10},... | collective-permute-start | bytes 196616 | tf_op jit(solution)/shard_map/ppermute | solution.py:344
  28.5 0.0 collective-permute-done.6.refs_2_
  28.5 0.0 collective-permute-done.8.refs_4_
  28.5 0.0 copy-done
  28.5 0.0 copy-done.1
  28.5 1.3 %refine.1 = (f32[8,512]{1,0:T(8,128)S(1)}, s32[8,512]{1,0:T(8,128)S(1)}) custom-call(s32[256]{0:T(256)} %place_ref.1, s32[4,8]{1,0:T(4,128)} %bitcast.9, bf16[8,512]{1,0:T(8,128)(2,1)S(1)} %copy-done.1, bf16[512,256]{1,0:T(8,128)(2,1)S(1)} %bitcast.6, s32[8,8192]{1,0:T(8,128)S(1)} %get-tuple-element.27.refs_0_, ...), custom_call_target="tpu_custom_call" | custom-call | tf_op jit(solution)/shard_map/refine/pallas_call | solution.py:207
  29.8 0.0 collective-permute-done.2.refs_1_
  29.8 3.8 %collective-permute-done.3.refs_2_ = bf16[8,4096]{1,0:T(8,128)(2,1)S(1)} collective-permute-done((bf16[8,4096]{1,0:T(8,128)(2,1)S(1)}, bf16[8,4096]{1,0:T(8,128)(2,1)S(1)}, u32[]{:S(2)}, u32[]{:S(2)}) %collective-permute-start.3) | collective-permute-done | bytes 65568 | tf_op jit(solution)/shard_map/ppermute | solution.py:344
  33.6 0.0 collective-permute-done.4.refs_3_
  33.6 0.2 pick.1
  33.8 1.6 %collective-permute-start.11 = (f32[8,256]{1,0:T(8,128)S(1)}, f32[8,256]{1,0:T(8,128)S(1)}, u32[]{:S(2)}, u32[]{:S(2)}) collective-permute-start(f32[8,256]{1,0:T(8,128)S(1)} %get-tuple-element.31), channel_id=1, source_target_pairs={{0,2},{2,0},{1,3},{3,1},{4,6},{6,4},{5,7},{7,5},{8,10},{10,8},{9,1... | collective-permute-start | bytes 24584 | tf_op jit(solution)/shard_map/ppermute | solution.py:344
  35.4 1.2 %arrange.1 = bf16[8,4,4096]{2,1,0:T(4,128)(2,1)} custom-call(bf16[8,4096]{1,0:T(8,128)(2,1)S(1)} %get-tuple-element.23.refs_0_, bf16[8,4096]{1,0:T(8,128)(2,1)S(1)} %collective-permute-done.2.refs_1_, bf16[8,4096]{1,0:T(8,128)(2,1)S(1)} %collective-permute-done.3.refs_2_, bf16[8,4096]{1,0:T(8,128)(2,1)S(1)} %collective-permute-done.4.refs_3_), custom_call_target="tpu_custom_call" | custom-call | tf_op jit(solution)/shard_map/arrange/pallas_call | solution.py:316
  36.5 1.0 %collective-permute-done.11.refs_1_ = f32[8,256]{1,0:T(8,128)S(1)} collective-permute-done((f32[8,256]{1,0:T(8,128)S(1)}, f32[8,256]{1,0:T(8,128)S(1)}, u32[]{:S(2)}, u32[]{:S(2)}) %collective-permute-start.11) | collective-permute-done | bytes 8224 | tf_op jit(solution)/shard_map/ppermute | solution.py:344
  37.5 0.6 %finish.1 = bf16[8,2,128]{2,1,0:T(2,128)(2,1)} custom-call(f32[8,256]{1,0:T(8,128)S(1)} %get-tuple-element.30.refs_0_, f32[8,256]{1,0:T(8,128)S(1)} %collective-permute-done.11.refs_1_), custom_call_target="tpu_custom_call" | custom-call | tf_op jit(solution)/shard_map/finish/pallas_call | solution.py:336
  (3 shorter events, 0.1 us)
Async XLA Ops:
  4.5 9.3 %collective-permute-start = (bf16[8,8,2048]{2,1,0:T(8,128)(2,1)S(1)}, bf16[8,8,2048]{2,1,0:T(8,128)(2,1)S(1)}, u32[]{:S(2)}, u32[]{:S(2)}) collective-permute-start(bf16[8,8,2048]{2,1,0:T(8,128)(2,1)S(1)} %get-tuple-element.20), channel_id=1, source_target_pairs={{0,2},{2,0},{1,3},{3,1},{4,6},{6,4},{5,7},{7,5},{8,10},{10,8},{9,1... | collective-permute-start | bytes 786440 | tf_op jit(solution)/shard_map/ppermute | solution.py:344
  13.9 14.6 %copy-start = (bf16[8,256,64]{1,2,0:T(8,128)(2,1)S(1)}, bf16[8,256,64]{1,2,0:T(8,128)(2,1)}, u32[]{:S(2)}) copy-start(bf16[8,256,64]{1,2,0:T(8,128)(2,1)} %param.11) | copy-start | bytes 786436
  13.9 10.1 %collective-permute-start.1 = (bf16[4,8,2048]{2,1,0:T(8,128)(2,1)S(1)}, bf16[4,8,2048]{2,1,0:T(8,128)(2,1)S(1)}, u32[]{:S(2)}, u32[]{:S(2)}) collective-permute-start(bf16[4,8,2048]{2,1,0:T(8,128)(2,1)S(1)} %get-tuple-element.22), channel_id=1, source_target_pairs={{0,1},{1,0},{2,3},{3,2},{4,5},{5,4},{6,7},{7,6},{8,9},{9,8},{10,11... | collective-permute-start | bytes 393224 | tf_op jit(solution)/shard_map/ppermute | solution.py:344
  14.0 6.9 %collective-permute-start.9 = (bf16[8,4096]{1,0:T(8,128)(2,1)S(1)}, bf16[8,4096]{1,0:T(8,128)(2,1)S(1)}, u32[]{:S(2)}, u32[]{:S(2)}) collective-permute-start(bf16[8,4096]{1,0:T(8,128)(2,1)S(1)} %dynamic-slice_convert_fusion), channel_id=1, source_target_pairs={{0,12},{4,8},{8,4},{12,0},{1,13},{5,9},{9,5},{13,1},{2,14},{6,10},... | collective-permute-start | bytes 196616 | tf_op jit(solution)/shard_map/ppermute | solution.py:344
  17.9 5.5 %collective-permute-start.5 = (bf16[8,4096]{1,0:T(8,128)(2,1)S(1)}, bf16[8,4096]{1,0:T(8,128)(2,1)S(1)}, u32[]{:S(2)}, u32[]{:S(2)}) collective-permute-start(bf16[8,4096]{1,0:T(8,128)(2,1)S(1)} %dynamic-slice_convert_fusion), channel_id=1, source_target_pairs={{0,4},{4,0},{8,12},{12,8},{1,5},{5,1},{9,13},{13,9},{2,6},{6,2},{1... | collective-permute-start | bytes 196616 | tf_op jit(solution)/shard_map/ppermute | solution.py:344
  17.9 5.9 %collective-permute-start.7 = (bf16[8,4096]{1,0:T(8,128)(2,1)S(1)}, bf16[8,4096]{1,0:T(8,128)(2,1)S(1)}, u32[]{:S(2)}, u32[]{:S(2)}) collective-permute-start(bf16[8,4096]{1,0:T(8,128)(2,1)S(1)} %dynamic-slice_convert_fusion), channel_id=1, source_target_pairs={{0,8},{4,12},{8,0},{12,4},{1,9},{5,13},{9,1},{13,5},{2,10},{6,14},... | collective-permute-start | bytes 196616 | tf_op jit(solution)/shard_map/ppermute | solution.py:344
  20.9 5.8 %collective-permute-start.10 = (bf16[8,4096]{1,0:T(8,128)(2,1)S(1)}, bf16[8,4096]{1,0:T(8,128)(2,1)S(1)}, u32[]{:S(2)}, u32[]{:S(2)}) collective-permute-start(bf16[8,4096]{1,0:T(8,128)(2,1)S(1)} %collective-permute-done.9.refs_5_), channel_id=1, source_target_pairs={{0,1},{1,0},{2,3},{3,2},{4,5},{5,4},{6,7},{7,6},{8,9},{9,8},{10,11... | collective-permute-start | bytes 196616 | tf_op jit(solution)/shard_map/ppermute | solution.py:344
  23.5 5.0 %collective-permute-start.6 = (bf16[8,4096]{1,0:T(8,128)(2,1)S(1)}, bf16[8,4096]{1,0:T(8,128)(2,1)S(1)}, u32[]{:S(2)}, u32[]{:S(2)}) collective-permute-start(bf16[8,4096]{1,0:T(8,128)(2,1)S(1)} %collective-permute-done.5.refs_1_), channel_id=1, source_target_pairs={{0,1},{1,0},{2,3},{3,2},{4,5},{5,4},{6,7},{7,6},{8,9},{9,8},{10,11... | collective-permute-start | bytes 196616 | tf_op jit(solution)/shard_map/ppermute | solution.py:344
  23.8 4.7 %collective-permute-start.8 = (bf16[8,4096]{1,0:T(8,128)(2,1)S(1)}, bf16[8,4096]{1,0:T(8,128)(2,1)S(1)}, u32[]{:S(2)}, u32[]{:S(2)}) collective-permute-start(bf16[8,4096]{1,0:T(8,128)(2,1)S(1)} %collective-permute-done.7.refs_3_), channel_id=1, source_target_pairs={{0,1},{1,0},{2,3},{3,2},{4,5},{5,4},{6,7},{7,6},{8,9},{9,8},{10,11... | collective-permute-start | bytes 196616 | tf_op jit(solution)/shard_map/ppermute | solution.py:344
  24.0 4.5 %copy-start.1 = (bf16[8,512]{1,0:T(8,128)(2,1)S(1)}, bf16[8,512]{1,0:T(8,128)(2,1)}, u32[]{:S(2)}) copy-start(bf16[8,512]{1,0:T(8,128)(2,1)} %rerank_ref.1) | copy-start | bytes 24580
  24.0 5.8 %collective-permute-start.2 = (bf16[8,4096]{1,0:T(8,128)(2,1)S(1)}, bf16[8,4096]{1,0:T(8,128)(2,1)S(1)}, u32[]{:S(2)}, u32[]{:S(2)}) collective-permute-start(bf16[8,4096]{1,0:T(8,128)(2,1)S(1)} %get-tuple-element.24), channel_id=1, source_target_pairs={{0,4},{4,0},{8,12},{12,8},{1,5},{5,1},{9,13},{13,9},{2,6},{6,2},{1... | collective-permute-start | bytes 196616 | tf_op jit(solution)/shard_map/ppermute | solution.py:344
  25.2 8.4 %collective-permute-start.3 = (bf16[8,4096]{1,0:T(8,128)(2,1)S(1)}, bf16[8,4096]{1,0:T(8,128)(2,1)S(1)}, u32[]{:S(2)}, u32[]{:S(2)}) collective-permute-start(bf16[8,4096]{1,0:T(8,128)(2,1)S(1)} %get-tuple-element.25), channel_id=1, source_target_pairs={{0,8},{4,12},{8,0},{12,4},{1,9},{5,13},{9,1},{13,5},{2,10},{6,14},... | collective-permute-start | bytes 196616 | tf_op jit(solution)/shard_map/ppermute | solution.py:344
  26.8 6.9 %collective-permute-start.4 = (bf16[8,4096]{1,0:T(8,128)(2,1)S(1)}, bf16[8,4096]{1,0:T(8,128)(2,1)S(1)}, u32[]{:S(2)}, u32[]{:S(2)}) collective-permute-start(bf16[8,4096]{1,0:T(8,128)(2,1)S(1)} %get-tuple-element.26), channel_id=1, source_target_pairs={{0,12},{4,8},{8,4},{12,0},{1,13},{5,9},{9,5},{13,1},{2,14},{6,10},... | collective-permute-start | bytes 196616 | tf_op jit(solution)/shard_map/ppermute | solution.py:344
  33.8 3.7 %collective-permute-start.11 = (f32[8,256]{1,0:T(8,128)S(1)}, f32[8,256]{1,0:T(8,128)S(1)}, u32[]{:S(2)}, u32[]{:S(2)}) collective-permute-start(f32[8,256]{1,0:T(8,128)S(1)} %get-tuple-element.31), channel_id=1, source_target_pairs={{0,2},{2,0},{1,3},{3,1},{4,6},{6,4},{5,7},{7,5},{8,10},{10,8},{9,1... | collective-permute-start | bytes 24584 | tf_op jit(solution)/shard_map/ppermute | solution.py:344
